TPU v7x, 128 devices: a whole 4x4x4 slice. The times are simulated.
128 devices in a mesh: planes: 16 (over x, z), rows: 8 (over y, core).
Axes of the slice: x: 4, y: 4, z: 4, core: 2. Of those that a mesh axis runs over, the one named last changes fastest.
Arguments:
- movie: bfloat16 [262144, 2048], P(('planes', 'rows')), may hold values from -6 to 6
- entry_tile: int32 [262144], P(('planes', 'rows')), may hold values from 0 to 2047
- entry_neuron: int32 [262144], P(('planes', 'rows')), may hold values from 0 to 98303, as said below
- entry_weights: bfloat16 [262144, 128], P(('planes', 'rows')), may hold values from 0 to 0.1796875
- intersection_self: float32 [98304, 768], P(('planes', 'rows'))
- intersection_prev: float32 [98304, 768], P(('planes', 'rows')), may hold values from -0.0625 to 0.0625
- intersection_next: float32 [98304, 768], P(('planes', 'rows')), may hold values from -0.0625 to 0.0625
- prev_traces: float32 [16, 98304], P(None, ('planes', 'rows')), may hold values from 0 to 2
Outputs:
- traces: float32 [16, 98304], P(None, ('planes', 'rows'))
Inputs may be any that keep to these rules, and one draw needn't show every extreme that they name: `entry_neuron`: the footprint tiles of one device come in groups of 32 consecutive entries; all entries of one group name neurons of one neuron block (neuron // 768); the first group of each device names the device's own block, and the groups of one device name distinct blocks.
All inputs are finite; a program needn't handle non-finite values.
Results may differ from a plain program's by a relative error of at most 0.0003.
Values sent between devices are 32-bit elements; how exact they have to be, the bound alone decides.
No kernel may reach another device: no remote copies, remote signals or barrier semaphores. Data moves between devices by JAX's collectives and lax.ppermute only.
A program may use at most 192 MiB of HBM per device.

v0:
```python
import jax
import jax.numpy as jnp
from jax import lax
from jax.sharding import PartitionSpec as P

SWEEPS = 3


def from_behind(block, axis, distance):
    devices = range(lax.axis_size(axis))
    route = [(i - distance, i) for i in devices if i - distance in devices]
    return lax.ppermute(block, axis, route)


def local(
    movie,
    entry_tile,
    entry_neuron,
    entry_weights,
    intersection_self,
    intersection_prev,
    intersection_next,
    prev_traces,
):
    devices = lax.axis_size(("planes", "rows"))
    neur_dev = prev_traces.shape[1]
    frames = prev_traces.shape[0]
    entries = entry_tile.shape[0]
    voxels = entry_weights.shape[1]
    picked = movie[entry_tile].reshape(entries, frames, voxels)
    contrib = jnp.einsum("efv,ev->ef", picked, entry_weights, preferred_element_type=jnp.float32)
    partial_value = (
        jnp.zeros((frames, neur_dev * devices), jnp.float32).at[:, entry_neuron].add(contrib.T)
    )
    projected = lax.psum_scatter(partial_value, ("planes", "rows"), scatter_dimension=1, tiled=True)
    diagonal = jnp.diagonal(intersection_self)
    highest = lax.Precision.HIGHEST
    current = prev_traces
    for sweep in range(SWEEPS):
        before = from_behind(current, ("planes", "rows"), 1)
        after = from_behind(current, ("planes", "rows"), -1)
        coupled = jnp.dot(current, intersection_self, precision=highest)
        coupled = coupled + jnp.dot(before, intersection_prev, precision=highest)
        coupled = coupled + jnp.dot(after, intersection_next, precision=highest)
        current = jnp.maximum(current + (projected - coupled) / diagonal, 0.0)
    return current


def solution(mesh):
    return jax.shard_map(
        local,
        mesh=mesh,
        in_specs=(
            P(("planes", "rows"), None),
            P(("planes", "rows")),
            P(("planes", "rows")),
            P(("planes", "rows"), None),
            P(("planes", "rows"), None),
            P(("planes", "rows"), None),
            P(("planes", "rows"), None),
            P(None, ("planes", "rows")),
        ),
        out_specs=P(None, ("planes", "rows")),
        check_vma=False,
    )
```

profile of v0, /device:TPU:2, one launch (start us, length us, event | category | flops | bytes accessed | tf_op | source)
XLA Modules:
  0.0 357.6 jit_solution(10171270098648136051)
XLA Ops:
  6.5 0.0 copy-start
  6.5 0.0 reduce-scatter.2.cloned.1.call-start
  6.5 0.9 fusion.16
  7.4 20.8 %gather_fusion = bf16[2048,2048]{1,0:T(8,128)(2,1)} fusion(bf16[2048,2048]{1,0:T(8,128)(2,1)} %param.8, s32[2048]{0:T(1024)S(1)} %fusion.16), kind=kCustom, calls=%fused_computation | custom fusion | bytes 16785408 | tf_op jit(solution)/shard_map/gather | solution.py:30
  28.2 0.0 copy-start.5
  28.2 0.0 copy-start.6
  28.2 9.8 %copy.13 = bf16[256,8,16,128]{3,2,1,0:T(8,128)(2,1)} copy(bf16[256,8,16,128]{3,1,2,0:T(8,128)(2,1)} %bitcast.24) | data formatting | bytes 16777216
  38.0 0.0 copy-done.5
  38.0 0.0 copy-done.6
  38.0 7.8 %fusion.14 = f32[2048,1,16]{2,1,0:T(1,128)S(1)} fusion(bf16[2048,16,128]{2,1,0:T(8,128)(2,1)} %bitcast.25, bf16[2048,128,1]{1,0,2:T(8,128)(2,1)S(1)} %bitcast.27), kind=kOutput, calls=%fused_computation.23 | convolution fusion | flops 8388608 | bytes 9043968 | tf_op jit(solution)/shard_map/efv,ev->ef/dot_general | solution.py:31
  45.8 31.4 %scatter_custom_fusion = f32[16,98304]{0,1:T(8,128)} fusion(s32[2048]{0:T(1024)S(1)} %compare_select_fusion.1, f32[2048,16]{1,0:T(8,128)S(1)} %bitcast.26, f32[]{:T(128)} %constant.4.clone.1), kind=kCustom, calls=%fused_computation.3 | custom fusion | flops 32768 | bytes 6291460 | tf_op jit(solution)/shard_map/scatter-add | solution.py:33
  77.3 27.7 %copy.10 = f32[16,98304]{1,0:T(8,128)} copy(f32[16,98304]{0,1:T(8,128)} %scatter_custom_fusion) | data formatting | bytes 12582912 | tf_op jit(solution)/shard_map/scatter-add | solution.py:33
  105.0 0.0 copy-start.4
  105.0 0.0 reduce-scatter.2.cloned.1.call-update
  105.0 0.8 copy-done.4
  105.8 1.9 collective-permute-start
  107.7 7.9 %collective-permute-start.1 = (f32[16,768]{1,0:T(8,128)S(1)}, f32[16,768]{1,0:T(8,128)S(1)}, u32[]{:S(2)}, u32[]{:S(2)}) collective-permute-start(f32[16,768]{1,0:T(8,128)S(1)} %copy-done.4), channel_id=1, source_target_pairs={{1,0},{2,1},{3,2},{4,3},{5,4},{6,5},{7,6},{8,7},{9,8},{10,9},{11,1... | collective-permute-start | bytes 147464 | tf_op jit(solution)/shard_map/ppermute | solution.py:12
  115.6 0.0 copy-done
  115.6 1.2 fusion.17
  116.8 6.3 %gather_fusion.1 = f32[768]{0:T(1024)S(1)} fusion(f32[768,768]{1,0:T(8,128)S(1)} %copy-done, s32[768]{0:T(1024)S(1)} %or_reduce_fusion), kind=kCustom, calls=%fused_computation.1 | custom fusion | bytes 12288 | tf_op jit(solution)/shard_map/jit(diagonal)/cond/branch_0_fun/gather | solution.py:36
  123.1 0.0 collective-permute-done
  123.1 2.9 convolution_add_fusion.5
  126.1 0.0 collective-permute-done.1
  126.1 192.9 %reduce-scatter.2.cloned.1.call-done = f32[16,768]{1,0:T(8,128)} async-done(((f32[16,98304]{1,0:T(8,128)}), f32[16,768]{1,0:T(8,128)}) %reduce-scatter.2.cloned.1.call-update) | async-done | bytes 49168 | tf_op jit(solution)/shard_map/reduce_scatter | solution.py:35
  318.9 0.0 copy-start.2
  318.9 3.0 fusion.13
  322.0 0.0 copy-start.1
  322.0 0.0 copy-start.3
  322.0 2.1 collective-permute-start.2
  324.1 1.2 fusion.18
  325.3 8.1 %collective-permute-start.3 = (f32[16,768]{1,0:T(8,128)S(1)}, f32[16,768]{1,0:T(8,128)S(1)}, u32[]{:S(2)}, u32[]{:S(2)}) collective-permute-start(f32[16,768]{1,0:T(8,128)S(1)} %fusion.13), channel_id=1, source_target_pairs={{1,0},{2,1},{3,2},{4,3},{5,4},{6,5},{7,6},{8,7},{9,8},{10,9},{11,1... | collective-permute-start | bytes 147464 | tf_op jit(solution)/shard_map/ppermute | solution.py:12
  333.4 0.0 collective-permute-done.2
  333.4 0.0 copy-done.2
  333.4 1.2 convolution_add_fusion.3
  334.6 0.3 collective-permute-done.3
  334.9 0.0 copy-done.1
  334.9 0.0 copy-done.3
  334.9 1.2 fusion.9
  336.1 1.9 collective-permute-start.4
  338.1 1.2 fusion.19
  339.3 7.9 %collective-permute-start.5 = (f32[16,768]{1,0:T(8,128)S(1)}, f32[16,768]{1,0:T(8,128)S(1)}, u32[]{:S(2)}, u32[]{:S(2)}) collective-permute-start(f32[16,768]{1,0:T(8,128)S(1)} %fusion.9), channel_id=1, source_target_pairs={{1,0},{2,1},{3,2},{4,3},{5,4},{6,5},{7,6},{8,7},{9,8},{10,9},{11,1... | collective-permute-start | bytes 147464 | tf_op jit(solution)/shard_map/ppermute | solution.py:12
  347.2 0.0 collective-permute-done.4
  347.2 1.2 convolution_add_fusion.1
  348.4 0.5 collective-permute-done.5
  348.9 1.8 fusion.5
  (2 shorter events, 0.0 us)
Async XLA Ops:
  6.5 109.0 %copy-start = (f32[768,768]{1,0:T(8,128)S(1)}, f32[768,768]{1,0:T(8,128)}, u32[]{:S(2)}) copy-start(f32[768,768]{1,0:T(8,128)} %param.12) | copy-start | bytes 7077892
  6.5 312.4 %reduce-scatter.2.cloned.1.call-start = ((), (), s32[]{:S(2)}) async-start(), calls=%async_computation.1 | async-start | bytes 6340608 | tf_op jit(solution)/shard_map/reduce_scatter | solution.py:35
  28.2 9.8 %copy-start.5 = (s32[2048]{0:T(1024)S(1)}, s32[2048]{0:T(1024)}, u32[]{:S(2)}) copy-start(s32[2048]{0:T(1024)} %param.10) | copy-start | bytes 24580
  28.2 9.8 %copy-start.6 = (bf16[2048,128]{1,0:T(8,128)(2,1)S(1)}, bf16[2048,128]{1,0:T(8,128)(2,1)}, u32[]{:S(2)}) copy-start(bf16[2048,128]{1,0:T(8,128)(2,1)} %param.11) | copy-start | bytes 1572868
  105.0 0.8 copy-start.4
  105.8 17.4 %collective-permute-start = (f32[16,768]{1,0:T(8,128)S(1)}, f32[16,768]{1,0:T(8,128)S(1)}, u32[]{:S(2)}, u32[]{:S(2)}) collective-permute-start(f32[16,768]{1,0:T(8,128)S(1)} %copy-done.4), channel_id=1, source_target_pairs={{0,1},{1,2},{2,3},{3,4},{4,5},{5,6},{6,7},{7,8},{8,9},{9,10},{10,1... | collective-permute-start | bytes 147464 | tf_op jit(solution)/shard_map/ppermute | solution.py:12
  107.7 18.4 %collective-permute-start.1 = (f32[16,768]{1,0:T(8,128)S(1)}, f32[16,768]{1,0:T(8,128)S(1)}, u32[]{:S(2)}, u32[]{:S(2)}) collective-permute-start(f32[16,768]{1,0:T(8,128)S(1)} %copy-done.4), channel_id=1, source_target_pairs={{1,0},{2,1},{3,2},{4,3},{5,4},{6,5},{7,6},{8,7},{9,8},{10,9},{11,1... | collective-permute-start | bytes 147464 | tf_op jit(solution)/shard_map/ppermute | solution.py:12
  318.9 14.4 %copy-start.2 = (f32[768,768]{1,0:T(8,128)S(1)}, f32[768,768]{1,0:T(8,128)}, u32[]{:S(2)}) copy-start(f32[768,768]{1,0:T(8,128)} %param.13) | copy-start | bytes 7077892
  322.0 12.9 %copy-start.1 = (f32[768,768]{1,0:T(8,128)S(1)}, f32[768,768]{1,0:T(8,128)}, u32[]{:S(2)}) copy-start(f32[768,768]{1,0:T(8,128)} %param.14) | copy-start | bytes 7077892
  322.0 12.9 %copy-start.3 = (f32[16,768]{1,0:T(8,128)S(1)}, f32[16,768]{1,0:T(8,128)}, u32[]{:S(2)}) copy-start(f32[16,768]{1,0:T(8,128)} %reduce-scatter.2.cloned.1.call-done) | copy-start | bytes 147460
  322.0 11.4 %collective-permute-start.2 = (f32[16,768]{1,0:T(8,128)S(1)}, f32[16,768]{1,0:T(8,128)S(1)}, u32[]{:S(2)}, u32[]{:S(2)}) collective-permute-start(f32[16,768]{1,0:T(8,128)S(1)} %fusion.13), channel_id=1, source_target_pairs={{0,1},{1,2},{2,3},{3,4},{4,5},{5,6},{6,7},{7,8},{8,9},{9,10},{10,1... | collective-permute-start | bytes 147464 | tf_op jit(solution)/shard_map/ppermute | solution.py:12
  325.3 9.6 %collective-permute-start.3 = (f32[16,768]{1,0:T(8,128)S(1)}, f32[16,768]{1,0:T(8,128)S(1)}, u32[]{:S(2)}, u32[]{:S(2)}) collective-permute-start(f32[16,768]{1,0:T(8,128)S(1)} %fusion.13), channel_id=1, source_target_pairs={{1,0},{2,1},{3,2},{4,3},{5,4},{6,5},{7,6},{8,7},{9,8},{10,9},{11,1... | collective-permute-start | bytes 147464 | tf_op jit(solution)/shard_map/ppermute | solution.py:12
  336.1 11.0 %collective-permute-start.4 = (f32[16,768]{1,0:T(8,128)S(1)}, f32[16,768]{1,0:T(8,128)S(1)}, u32[]{:S(2)}, u32[]{:S(2)}) collective-permute-start(f32[16,768]{1,0:T(8,128)S(1)} %fusion.9), channel_id=1, source_target_pairs={{0,1},{1,2},{2,3},{3,4},{4,5},{5,6},{6,7},{7,8},{8,9},{9,10},{10,1... | collective-permute-start | bytes 147464 | tf_op jit(solution)/shard_map/ppermute | solution.py:12
  339.3 9.6 %collective-permute-start.5 = (f32[16,768]{1,0:T(8,128)S(1)}, f32[16,768]{1,0:T(8,128)S(1)}, u32[]{:S(2)}, u32[]{:S(2)}) collective-permute-start(f32[16,768]{1,0:T(8,128)S(1)} %fusion.9), channel_id=1, source_target_pairs={{1,0},{2,1},{3,2},{4,3},{5,4},{6,5},{7,6},{8,7},{9,8},{10,9},{11,1... | collective-permute-start | bytes 147464 | tf_op jit(solution)/shard_map/ppermute | solution.py:12
Sparse Core Ops, SparseCore 0:
  105.1 213.7 reduce-scatter.1
where the time goes:
time: 358 us
  waiting for transfers between devices  194 us (54%)
  local copies, waits for them, and re-layouts  65.5 us (18%)
  other arithmetic  32.3 us (9%)
  starting transfers between devices  29.7 us (8%)
  matrix products  22.9 us (6%)
  between operations  13.5 us (4%)
    reduce_scatter x1, waiting for transfers between devices, local(): lax.psum_scatter(partial_value, ('planes', 'rows'), scatter_dimension=1,...  193 us
    scatter-add x1, other arithmetic, local(): jnp.zeros((frames, neur_dev * devices), jnp.float32).at[:, entry_neuron]  31.4 us
    ppermute x6, starting transfers between devices, from_behind(): return lax.ppermute(block, axis, route)  29.7 us
    scatter-add x1, local copies, waits for them, and re-layouts, local(): jnp.zeros((frames, neur_dev * devices), jnp.float32).at[:, entry_neuron]  27.7 us
    gather x1, local copies, waits for them, and re-layouts, local(): picked = movie[entry_tile].reshape(entries, frames, voxels)  20.8 us
    unnamed x15, local copies, waits for them, and re-layouts  10.6 us
    dot_general x1, matrix products, local(): jnp.einsum('efv,ev->ef', picked, entry_weights, preferred_element_type=jn...  7.79 us
  transfers between devices with their start and end apart: 7, of which 3 were waited for; matrix products, arithmetic and copies ran while one was open for 4% of the time, Pallas kernels for 0%

commit v1 on v0

v1 whole, which is shorter than its diff:
```python
import jax
import jax.numpy as jnp
from jax import lax
from jax.experimental import pallas as pl
from jax.experimental.pallas import tpu as pltpu
from jax.sharding import PartitionSpec as P

SWEEPS = 3
AXES = ("planes", "rows")
LANES = 128
CAP = 32
SLOT = 5
CHUNKS = 8


def from_behind(block, distance):
    devices = range(lax.axis_size(AXES))
    route = [(i - distance, i) for i in devices if i - distance in devices]
    return lax.ppermute(block, AXES, route)


def swap_blocks(x):
    row = lax.broadcasted_iota(jnp.int32, x.shape, 0) // 4
    col = lax.broadcasted_iota(jnp.int32, x.shape, 1) // CAP
    out = x
    for d in range(1, 4):
        moved = pltpu.roll(pltpu.roll(x, CAP * d, 1), 16 - 4 * d, 0)
        out = jnp.where((col - row) % 4 == d, moved, out)
    return out


def contrib_kernel(tile_ref, neuron_ref, movie_ref, weight_ref, names_ref, out_ref, raw, slab, wide, sem):
    rows = movie_ref.shape[0] // CHUNKS

    def fetch(c):
        return pltpu.make_async_copy(movie_ref.at[pl.ds(c * rows, rows)], raw.at[c], sem.at[c])

    for c in range(CHUNKS):
        fetch(c).start()
    out_ref[...] = jnp.zeros_like(out_ref)
    for c in range(CHUNKS):
        fetch(c).wait()

        @pl.loop(0, rows // 16)
        def _(r):
            base = pl.multiple_of((c * rows + r * 16) * 16, 256)
            for f in range(16):
                x = raw[c, pl.ds(pl.multiple_of(r * 16, 16), 16), pl.ds(f * LANES, LANES)].astype(jnp.float32)
                slab[pl.ds(base + f * 8, 8), :] = x[:8]
                slab[pl.ds(base + 128 + f * 8, 8), :] = x[8:]

    lane = lax.broadcasted_iota(jnp.int32, (16, LANES), 1)

    @pl.loop(0, tile_ref.shape[0] // LANES)
    def _(b):
        start = pl.multiple_of(b * LANES, LANES)
        wide[...] = weight_ref[pl.ds(start, LANES), :].astype(jnp.float32)
        acc = jnp.zeros((16, LANES), jnp.float32)
        for e in range(LANES):
            t = tile_ref[start + e]
            at = (t // 8) * 128 + t % 8
            x = slab[pl.ds(at, 16, stride=8), :]
            s = jnp.sum(x * wide[pl.ds(e, 1), :], axis=1, keepdims=True)
            acc = jnp.where(lane == e, s, acc)
        slots = swap_blocks(acc)
        names = swap_blocks(jnp.broadcast_to(names_ref[pl.ds(b, 1), :].astype(jnp.float32), (16, LANES)))
        for g in range(4):
            owner = neuron_ref[start + g * CAP] // 768
            out_ref[pl.ds(owner * SLOT, 4), :] = slots[4 * g : 4 * g + 4]
            out_ref[pl.ds(owner * SLOT + 4, 1), :] = names[4 * g : 4 * g + 1]


def contributions(movie, entry_tile, entry_neuron, entry_weights, devices):
    tiles = movie.shape[0]
    entries = entry_tile.shape[0]
    return pl.pallas_call(
        contrib_kernel,
        out_shape=jax.ShapeDtypeStruct((devices * SLOT, LANES), jnp.float32),
        grid_spec=pltpu.PrefetchScalarGridSpec(
            num_scalar_prefetch=2,
            grid=(1,),
            in_specs=[
                pl.BlockSpec(memory_space=pl.ANY),
                pl.BlockSpec((entries, LANES), lambda i, *_: (0, 0)),
                pl.BlockSpec((entries // LANES, LANES), lambda i, *_: (0, 0)),
            ],
            out_specs=pl.BlockSpec((devices * SLOT, LANES), lambda i, *_: (0, 0)),
            scratch_shapes=[
                pltpu.VMEM((CHUNKS, tiles // CHUNKS, movie.shape[1]), jnp.bfloat16),
                pltpu.VMEM((tiles * 16, LANES), jnp.float32),
                pltpu.VMEM((LANES, LANES), jnp.float32),
                pltpu.SemaphoreType.DMA((CHUNKS,)),
            ],
        ),
        compiler_params=pltpu.CompilerParams(vmem_limit_bytes=40 << 20),
    )(entry_tile, entry_neuron, movie, entry_weights, entry_neuron.reshape(entries // LANES, LANES))


def combine_kernel(me_ref, got_ref, out_ref, left, hot):
    sources = got_ref.shape[0] // SLOT
    first = me_ref[0] * 768
    lane4 = lax.broadcasted_iota(jnp.int32, (1, LANES), 1) // CAP
    sub = lax.broadcasted_iota(jnp.int32, (256, LANES), 0).astype(jnp.float32)

    @pl.loop(0, sources // 4)
    def _(b):
        row = b * 4 * SLOT
        x = jnp.concatenate([got_ref[pl.ds(row + s * SLOT, 4), :] for s in range(4)], axis=0)
        x = swap_blocks(x)
        name = got_ref[pl.ds(row + 4, 1), :]
        for s in range(1, 4):
            name = jnp.where(lane4 == s, got_ref[pl.ds(row + s * SLOT + 4, 1), :], name)
        name = name - first.astype(jnp.float32)
        high = jnp.where(name >= 512.0, 2.0, jnp.where(name >= 256.0, 1.0, 0.0))
        low = name - 256.0 * high
        big = x.astype(jnp.bfloat16).astype(jnp.float32)
        rest = x - big
        at = pl.ds(pl.multiple_of(b * LANES, LANES), LANES)
        for h in range(3):
            here = high == float(h)
            left[pl.ds(h * 32, 16), at] = jnp.where(here, big, 0.0).astype(jnp.bfloat16)
            left[pl.ds(h * 32 + 16, 16), at] = jnp.where(here, rest, 0.0).astype(jnp.bfloat16)
        hot[:, at] = jnp.where(sub == low, 1.0, 0.0).astype(jnp.bfloat16)

    sums = lax.dot_general(left[...], hot[...], (((1,), (1,)), ((), ())), preferred_element_type=jnp.float32)
    for h in range(3):
        out_ref[:, pl.ds(h * 256, 256)] = sums[h * 32 : h * 32 + 16] + sums[h * 32 + 16 : h * 32 + 32]


def combine(me, got):
    sources = got.shape[0] // SLOT
    return pl.pallas_call(
        combine_kernel,
        out_shape=jax.ShapeDtypeStruct((16, 768), jnp.float32),
        in_specs=[pl.BlockSpec(memory_space=pltpu.SMEM), pl.BlockSpec(memory_space=pltpu.VMEM)],
        out_specs=pl.BlockSpec(memory_space=pltpu.VMEM),
        scratch_shapes=[
            pltpu.VMEM((96, sources * CAP), jnp.bfloat16),
            pltpu.VMEM((256, sources * CAP), jnp.bfloat16),
        ],
        compiler_params=pltpu.CompilerParams(vmem_limit_bytes=16 << 20),
    )(me, got)


def local(
    movie,
    entry_tile,
    entry_neuron,
    entry_weights,
    intersection_self,
    intersection_prev,
    intersection_next,
    prev_traces,
):
    devices = lax.axis_size(AXES)
    neur_dev = prev_traces.shape[1]
    me = lax.axis_index(AXES).reshape(1).astype(jnp.int32)
    send = contributions(movie, entry_tile, entry_neuron, entry_weights, devices)
    got = lax.all_to_all(send.reshape(devices, 1, SLOT * LANES), AXES, 0, 0)
    projected = combine(me, got.reshape(devices * SLOT, LANES))
    eye = jnp.arange(neur_dev)[:, None] == jnp.arange(neur_dev)[None, :]
    diagonal = jnp.sum(jnp.where(eye, intersection_self, 0.0), axis=0)
    highest = lax.Precision.HIGHEST
    current = prev_traces
    for sweep in range(SWEEPS):
        before = from_behind(current, 1)
        after = from_behind(current, -1)
        coupled = jnp.dot(current, intersection_self, precision=highest)
        coupled = coupled + jnp.dot(before, intersection_prev, precision=highest)
        coupled = coupled + jnp.dot(after, intersection_next, precision=highest)
        current = jnp.maximum(current + (projected - coupled) / diagonal, 0.0)
    return current


def solution(mesh):
    return jax.shard_map(
        local,
        mesh=mesh,
        in_specs=(
            P(AXES, None),
            P(AXES),
            P(AXES),
            P(AXES, None),
            P(AXES, None),
            P(AXES, None),
            P(AXES, None),
            P(None, AXES),
        ),
        out_specs=P(None, AXES),
        check_vma=False,
    )
```

time: 358 us -> 88.2 us (0.25)
  waiting for transfers between devices: 194 us -> 7.72 us
  local copies, waits for them, and re-layouts: 65.5 us -> 5.83 us
  other arithmetic: 32.3 us -> 0.07 us
  Pallas kernels: 0 us -> 22.8 us
  between operations: 13.5 us -> 0.19 us
  matrix products: 22.9 us -> 15.1 us
  starting transfers between devices: 29.7 us -> 35.9 us
    reduce_scatter x1 -> x0, waiting for transfers between devices: 193 us -> none  [local(): lax.psum_scatter(partial_value, ('planes', 'rows'), scatter_dimension=1,...]
    scatter-add x1 -> x0, other arithmetic: 31.4 us -> none  [local(): jnp.zeros((frames, neur_dev * devices), jnp.float32).at[:, entry_neuron]]
    scatter-add x1 -> x0, local copies, waits for them, and re-layouts: 27.7 us -> none  [local(): jnp.zeros((frames, neur_dev * devices), jnp.float32).at[:, entry_neuron]]
    gather x2 -> x0, local copies, waits for them, and re-layouts: 27.1 us -> none  [the longest x1 20.8 us: local(): picked = movie[entry_tile].reshape(entries, frames, voxels)]
    pallas_call x0 -> x2, Pallas kernels: none -> 22.8 us  [the longest x1 19.2 us: contributions(): pl.pallas_call(contrib_kernel, out_shape=jax.ShapeDtypeStruct((devices *...]
    dot_general x1 -> x0, matrix products: 7.79 us -> none  [local(): jnp.einsum('efv,ev->ef', picked, entry_weights, preferred_element_type=jn...]
    all_to_all x0 -> x1, waiting for transfers between devices: none -> 6.7 us  [local(): got = lax.all_to_all(send.reshape(devices, 1, SLOT * LANES), AXES, 0, 0)]
    all_to_all x0 -> x1, starting transfers between devices: none -> 6.31 us  [local(): got = lax.all_to_all(send.reshape(devices, 1, SLOT * LANES), AXES, 0, 0)]
  transfers between devices with their start and end apart: 7 -> 7, of which waited for: 3 -> 3; matrix products, arithmetic and copies ran while one was open for 4% -> 11% of each run, Pallas kernels for 0% -> 26%
where the time goes in v1:
time: 88.2 us; the launch traced here: 87.6 us
  starting transfers between devices  35.9 us (41%)
  Pallas kernels  22.8 us (26%)
  matrix products  15.1 us (17%)
  waiting for transfers between devices  7.72 us (9%)
  local copies, waits for them, and re-layouts  5.83 us (7%)
    ppermute x6, starting transfers between devices, from_behind(): return lax.ppermute(block, AXES, route)  29.6 us
    pallas_call x1, Pallas kernels, contributions(): pl.pallas_call(contrib_kernel, out_shape=jax.ShapeDtypeStruct((devices *...  19.2 us
    all_to_all x1, waiting for transfers between devices, local(): got = lax.all_to_all(send.reshape(devices, 1, SLOT * LANES), AXES, 0, 0)  6.7 us
    all_to_all x1, starting transfers between devices, local(): got = lax.all_to_all(send.reshape(devices, 1, SLOT * LANES), AXES, 0, 0)  6.31 us
    dot_general x3, matrix products, local(): coupled = coupled + jnp.dot(after, intersection_next, precision=highest)  5.96 us
    unnamed x18, local copies, waits for them, and re-layouts  5.83 us
    dot_general x3, matrix products, local(): coupled = jnp.dot(current, intersection_self, precision=highest)  5.47 us
    dot_general x3, matrix products, local(): coupled = coupled + jnp.dot(before, intersection_prev, precision=highest)  3.66 us
  transfers between devices with their start and end apart: 7, of which 3 were waited for; matrix products, arithmetic and copies ran while one was open for 11% of the time, Pallas kernels for 26%

profile of v1, /device:TPU:2, one launch (start us, length us, event | category | flops | bytes accessed | tf_op | source)
XLA Modules:
  0.0 87.6 jit_solution(16588253188528724514)
XLA Ops:
  0.0 0.0 copy-start
  0.0 2.0 %collective-permute-start = (f32[16,768]{1,0:T(8,128)}, f32[16,768]{1,0:T(8,128)S(1)}, u32[]{:S(2)}, u32[]{:S(2)}) collective-permute-start(f32[16,768]{1,0:T(8,128)} %param.15), channel_id=1, source_target_pairs={{0,1},{1,2},{2,3},{3,4},{4,5},{5,6},{6,7},{7,8},{8,9},{9,10},{10,1... | collective-permute-start | bytes 147464 | tf_op jit(solution)/shard_map/ppermute | solution.py:19
  2.1 7.9 %collective-permute-start.1 = (f32[16,768]{1,0:T(8,128)}, f32[16,768]{1,0:T(8,128)S(1)}, u32[]{:S(2)}, u32[]{:S(2)}) collective-permute-start(f32[16,768]{1,0:T(8,128)} %param.15), channel_id=1, source_target_pairs={{1,0},{2,1},{3,2},{4,3},{5,4},{6,5},{7,6},{8,7},{9,8},{10,9},{11,1... | collective-permute-start | bytes 147464 | tf_op jit(solution)/shard_map/ppermute | solution.py:19
  9.9 0.0 copy-start.1
  9.9 3.4 %copy-done.1 = bf16[2048,2048]{1,0:T(8,128)(2,1)S(1)} copy-done((bf16[2048,2048]{1,0:T(8,128)(2,1)S(1)}, bf16[2048,2048]{1,0:T(8,128)(2,1)}, u32[]{:S(2)}) %copy-start.1) | copy-done | bytes 8388632
  13.3 0.0 copy-start.2
  13.3 1.0 %copy-done.2 = bf16[2048,128]{1,0:T(8,128)(2,1)S(1)} copy-done((bf16[2048,128]{1,0:T(8,128)(2,1)S(1)}, bf16[2048,128]{1,0:T(8,128)(2,1)}, u32[]{:S(2)}) %copy-start.2) | copy-done | bytes 524312
  14.3 0.0 copy-start.3
  14.3 0.7 copy-done.3
  15.0 0.0 copy-start.4
  15.0 0.7 copy-done.4
  15.7 0.0 copy-start.8
  15.7 19.2 %shard_map.82 = f32[640,128]{1,0:T(8,128)} custom-call(s32[2048]{0:T(1024)S(1)} %copy-done.4, s32[2048]{0:T(1024)S(1)} %copy-done.3, bf16[2048,2048]{1,0:T(8,128)(2,1)S(1)} %copy-done.1, bf16[2048,128]{1,0:T(8,128)(2,1)S(1)} %copy-done.2, s32[16,128]{1,0:T(8,128)S(1)} %bitcast.23), custom_call_target="tpu_custom_call" | custom-call | tf_op jit(solution)/shard_map/pallas_call | solution.py:76
  35.0 6.3 %all-to-all-start = ((f32[128,1,640]{2,1,0:T(1,128)}), f32[128,1,640]{2,1,0:T(1,128)S(1)}, u32[]{:S(2)}, u32[]{:S(2)}) async-start(f32[128,1,640]{2,1,0:T(1,128)} %bitcast.2), calls=%async_computation | async-start | bytes 655360 | tf_op jit(solution)/shard_map/all_to_all | solution.py:159
  41.3 0.0 copy-done.8
  41.3 0.0 copy-start.5
  41.3 3.0 %fusion.12 = f32[16,768]{1,0:T(8,128)S(1)} fusion(f32[16,768]{1,0:T(8,128)S(1)} %copy-done.8, f32[768,768]{1,0:T(8,128)} %param.12), kind=kOutput, calls=%fused_computation.20 | convolution fusion | flops 113246208 | bytes 2457600 | tf_op jit(solution)/shard_map/dot_general | solution.py:168
  44.3 0.0 copy-done.5
  44.4 0.1 select_reduce_fusion
  44.4 0.0 collective-permute-done
  44.4 0.0 copy-done
  44.5 1.2 %convolution_add_fusion.5 = f32[16,768]{1,0:T(8,128)S(1)} fusion(f32[16,768]{1,0:T(8,128)S(1)} %fusion.12, f32[16,768]{1,0:T(8,128)S(1)} %collective-permute-done, f32[768,768]{1,0:T(8,128)S(1)} %copy-done), kind=kOutput, calls=%fused_computation.19 | convolution fusion | flops 113258496 | bytes 2506752 | tf_op jit(solution)/shard_map/dot_general | solution.py:169
  45.7 6.7 %all-to-all-done = f32[128,1,640]{2,1,0:T(1,128)S(1)} async-done(((f32[128,1,640]{2,1,0:T(1,128)}), f32[128,1,640]{2,1,0:T(1,128)S(1)}, u32[]{:S(2)}, u32[]{:S(2)}) %all-to-all-start) | async-done | bytes 327712 | tf_op jit(solution)/shard_map/all_to_all | solution.py:159
  52.4 0.0 copy-start.6
  52.4 3.6 %shard_map.83 = f32[16,768]{1,0:T(8,128)S(1)} custom-call(s32[1]{0:T(128)} %bitcast.me_ref, f32[640,128]{1,0:T(8,128)S(1)} %bitcast.22), custom_call_target="tpu_custom_call" | custom-call | tf_op jit(solution)/shard_map/pallas_call | solution.py:132
  55.9 0.0 collective-permute-done.1
  56.0 2.9 %fusion.11 = f32[16,768]{1,0:T(8,128)S(1)} fusion(f32[16,768]{1,0:T(8,128)S(1)} %copy-done.8, f32[16,768]{1,0:T(8,128)S(1)} %shard_map.83, f32[16,768]{1,0:T(8,128)S(1)} %convolution_add_fusion.5, f32[16,768]{1,0:T(8,128)S(1)} %collective-permute-done.1, f32[768,768]{1,0:T(8,128)} %param.14, f32[768]{0:T(1024)S(1)} %select_reduce_fusion), kind=kOutput, calls=%fused_computation.18 | convolution fusion | flops 113307648 | bytes 2608128 | tf_op jit(solution)/shard_map/dot_general | solution.py:170
  58.9 0.0 copy-start.7
  58.9 2.1 %collective-permute-start.2 = (f32[16,768]{1,0:T(8,128)S(1)}, f32[16,768]{1,0:T(8,128)S(1)}, u32[]{:S(2)}, u32[]{:S(2)}) collective-permute-start(f32[16,768]{1,0:T(8,128)S(1)} %fusion.11), channel_id=1, source_target_pairs={{0,1},{1,2},{2,3},{3,4},{4,5},{5,6},{6,7},{7,8},{8,9},{9,10},{10,1... | collective-permute-start | bytes 147464 | tf_op jit(solution)/shard_map/ppermute | solution.py:19
  60.9 0.0 copy-done.6
  60.9 1.2 %fusion.13 = f32[16,768]{1,0:T(8,128)S(1)} fusion(f32[16,768]{1,0:T(8,128)S(1)} %fusion.11, f32[768,768]{1,0:T(8,128)S(1)} %copy-done.6), kind=kOutput, calls=%fused_computation.21 | convolution fusion | flops 113246208 | bytes 2457600 | tf_op jit(solution)/shard_map/dot_general | solution.py:168
  62.2 7.9 %collective-permute-start.3 = (f32[16,768]{1,0:T(8,128)S(1)}, f32[16,768]{1,0:T(8,128)S(1)}, u32[]{:S(2)}, u32[]{:S(2)}) collective-permute-start(f32[16,768]{1,0:T(8,128)S(1)} %fusion.11), channel_id=1, source_target_pairs={{1,0},{2,1},{3,2},{4,3},{5,4},{6,5},{7,6},{8,7},{9,8},{10,9},{11,1... | collective-permute-start | bytes 147464 | tf_op jit(solution)/shard_map/ppermute | solution.py:19
  70.0 0.0 collective-permute-done.2
  70.0 1.2 %convolution_add_fusion.3 = f32[16,768]{1,0:T(8,128)S(1)} fusion(f32[16,768]{1,0:T(8,128)S(1)} %fusion.13, f32[16,768]{1,0:T(8,128)S(1)} %collective-permute-done.2, f32[768,768]{1,0:T(8,128)S(1)} %copy-done), kind=kOutput, calls=%fused_computation.13 | convolution fusion | flops 113258496 | bytes 2506752 | tf_op jit(solution)/shard_map/dot_general | solution.py:169
  71.3 0.5 collective-permute-done.3
  71.8 0.0 copy-done.7
  71.8 1.2 %fusion.7 = f32[16,768]{1,0:T(8,128)S(1)} fusion(f32[16,768]{1,0:T(8,128)S(1)} %fusion.11, f32[16,768]{1,0:T(8,128)S(1)} %shard_map.83, f32[16,768]{1,0:T(8,128)S(1)} %convolution_add_fusion.3, f32[16,768]{1,0:T(8,128)S(1)} %collective-permute-done.3, f32[768,768]{1,0:T(8,128)S(1)} %copy-done.7, f32[768]{0:T(1024)S(1)} %select_reduce_fusion), kind=kOutput, calls=%fused_computation.12 | convolution fusion | flops 113307648 | bytes 2608128 | tf_op jit(solution)/shard_map/dot_general | solution.py:170
  73.0 1.9 %collective-permute-start.4 = (f32[16,768]{1,0:T(8,128)S(1)}, f32[16,768]{1,0:T(8,128)S(1)}, u32[]{:S(2)}, u32[]{:S(2)}) collective-permute-start(f32[16,768]{1,0:T(8,128)S(1)} %fusion.7), channel_id=1, source_target_pairs={{0,1},{1,2},{2,3},{3,4},{4,5},{5,6},{6,7},{7,8},{8,9},{9,10},{10,1... | collective-permute-start | bytes 147464 | tf_op jit(solution)/shard_map/ppermute | solution.py:19
  74.9 1.2 %fusion.14 = f32[16,768]{1,0:T(8,128)S(1)} fusion(f32[16,768]{1,0:T(8,128)S(1)} %fusion.7, f32[768,768]{1,0:T(8,128)S(1)} %copy-done.6), kind=kOutput, calls=%fused_computation.22 | convolution fusion | flops 113246208 | bytes 2457600 | tf_op jit(solution)/shard_map/dot_general | solution.py:168
  76.1 7.9 %collective-permute-start.5 = (f32[16,768]{1,0:T(8,128)S(1)}, f32[16,768]{1,0:T(8,128)S(1)}, u32[]{:S(2)}, u32[]{:S(2)}) collective-permute-start(f32[16,768]{1,0:T(8,128)S(1)} %fusion.7), channel_id=1, source_target_pairs={{1,0},{2,1},{3,2},{4,3},{5,4},{6,5},{7,6},{8,7},{9,8},{10,9},{11,1... | collective-permute-start | bytes 147464 | tf_op jit(solution)/shard_map/ppermute | solution.py:19
  84.0 0.0 collective-permute-done.4
  84.0 1.2 %convolution_add_fusion.1 = f32[16,768]{1,0:T(8,128)S(1)} fusion(f32[16,768]{1,0:T(8,128)S(1)} %fusion.14, f32[16,768]{1,0:T(8,128)S(1)} %collective-permute-done.4, f32[768,768]{1,0:T(8,128)S(1)} %copy-done), kind=kOutput, calls=%fused_computation.7 | convolution fusion | flops 113258496 | bytes 2506752 | tf_op jit(solution)/shard_map/dot_general | solution.py:169
  85.3 0.5 collective-permute-done.5
  85.8 1.8 %fusion.3 = f32[16,768]{1,0:T(8,128)} fusion(f32[16,768]{1,0:T(8,128)S(1)} %fusion.7, f32[16,768]{1,0:T(8,128)S(1)} %shard_map.83, f32[16,768]{1,0:T(8,128)S(1)} %convolution_add_fusion.1, f32[16,768]{1,0:T(8,128)S(1)} %collective-permute-done.5, f32[768,768]{1,0:T(8,128)S(1)} %copy-done.7, f32[768]{0:T(1024)S(1)} %select_reduce_fusion), kind=kOutput, calls=%fused_computation.6 | convolution fusion | flops 113307648 | bytes 2608128 | tf_op jit(solution)/shard_map/dot_general | solution.py:170
Async XLA Ops:
  0.0 44.4 %copy-start = (f32[768,768]{1,0:T(8,128)S(1)}, f32[768,768]{1,0:T(8,128)}, u32[]{:S(2)}) copy-start(f32[768,768]{1,0:T(8,128)} %param.13) | copy-start | bytes 7077892
  0.0 44.4 %collective-permute-start = (f32[16,768]{1,0:T(8,128)}, f32[16,768]{1,0:T(8,128)S(1)}, u32[]{:S(2)}, u32[]{:S(2)}) collective-permute-start(f32[16,768]{1,0:T(8,128)} %param.15), channel_id=1, source_target_pairs={{0,1},{1,2},{2,3},{3,4},{4,5},{5,6},{6,7},{7,8},{8,9},{9,10},{10,1... | collective-permute-start | bytes 147464 | tf_op jit(solution)/shard_map/ppermute | solution.py:19
  2.1 53.9 %collective-permute-start.1 = (f32[16,768]{1,0:T(8,128)}, f32[16,768]{1,0:T(8,128)S(1)}, u32[]{:S(2)}, u32[]{:S(2)}) collective-permute-start(f32[16,768]{1,0:T(8,128)} %param.15), channel_id=1, source_target_pairs={{1,0},{2,1},{3,2},{4,3},{5,4},{6,5},{7,6},{8,7},{9,8},{10,9},{11,1... | collective-permute-start | bytes 147464 | tf_op jit(solution)/shard_map/ppermute | solution.py:19
  9.9 3.4 %copy-start.1 = (bf16[2048,2048]{1,0:T(8,128)(2,1)S(1)}, bf16[2048,2048]{1,0:T(8,128)(2,1)}, u32[]{:S(2)}) copy-start(bf16[2048,2048]{1,0:T(8,128)(2,1)} %movie_ref.1) | copy-start | bytes 25165828
  13.3 1.0 %copy-start.2 = (bf16[2048,128]{1,0:T(8,128)(2,1)S(1)}, bf16[2048,128]{1,0:T(8,128)(2,1)}, u32[]{:S(2)}) copy-start(bf16[2048,128]{1,0:T(8,128)(2,1)} %weight_ref.1) | copy-start | bytes 1572868
  14.3 0.7 copy-start.3
  15.0 0.7 copy-start.4
  15.7 25.6 %copy-start.8 = (f32[16,768]{1,0:T(8,128)S(1)}, f32[16,768]{1,0:T(8,128)}, u32[]{:S(2)}) copy-start(f32[16,768]{1,0:T(8,128)} %param.15) | copy-start | bytes 147460
  35.0 17.4 %all-to-all-start = ((f32[128,1,640]{2,1,0:T(1,128)}), f32[128,1,640]{2,1,0:T(1,128)S(1)}, u32[]{:S(2)}, u32[]{:S(2)}) async-start(f32[128,1,640]{2,1,0:T(1,128)} %bitcast.2), calls=%async_computation | async-start | bytes 655360 | tf_op jit(solution)/shard_map/all_to_all | solution.py:159
  41.3 3.0 %copy-start.5 = (f32[768,768]{1,0:T(8,128)S(1)}, f32[768,768]{1,0:T(8,128)}, u32[]{:S(2)}) copy-start(f32[768,768]{1,0:T(8,128)} %param.12) | copy-start | bytes 7077892
  52.4 8.6 %copy-start.6 = (f32[768,768]{1,0:T(8,128)S(1)}, f32[768,768]{1,0:T(8,128)}, u32[]{:S(2)}) copy-start(f32[768,768]{1,0:T(8,128)} %param.12) | copy-start | bytes 7077892
  58.9 12.9 %copy-start.7 = (f32[768,768]{1,0:T(8,128)S(1)}, f32[768,768]{1,0:T(8,128)}, u32[]{:S(2)}) copy-start(f32[768,768]{1,0:T(8,128)} %param.14) | copy-start | bytes 7077892
  58.9 11.2 %collective-permute-start.2 = (f32[16,768]{1,0:T(8,128)S(1)}, f32[16,768]{1,0:T(8,128)S(1)}, u32[]{:S(2)}, u32[]{:S(2)}) collective-permute-start(f32[16,768]{1,0:T(8,128)S(1)} %fusion.11), channel_id=1, source_target_pairs={{0,1},{1,2},{2,3},{3,4},{4,5},{5,6},{6,7},{7,8},{8,9},{9,10},{10,1... | collective-permute-start | bytes 147464 | tf_op jit(solution)/shard_map/ppermute | solution.py:19
  62.2 9.6 %collective-permute-start.3 = (f32[16,768]{1,0:T(8,128)S(1)}, f32[16,768]{1,0:T(8,128)S(1)}, u32[]{:S(2)}, u32[]{:S(2)}) collective-permute-start(f32[16,768]{1,0:T(8,128)S(1)} %fusion.11), channel_id=1, source_target_pairs={{1,0},{2,1},{3,2},{4,3},{5,4},{6,5},{7,6},{8,7},{9,8},{10,9},{11,1... | collective-permute-start | bytes 147464 | tf_op jit(solution)/shard_map/ppermute | solution.py:19
  73.0 11.0 %collective-permute-start.4 = (f32[16,768]{1,0:T(8,128)S(1)}, f32[16,768]{1,0:T(8,128)S(1)}, u32[]{:S(2)}, u32[]{:S(2)}) collective-permute-start(f32[16,768]{1,0:T(8,128)S(1)} %fusion.7), channel_id=1, source_target_pairs={{0,1},{1,2},{2,3},{3,4},{4,5},{5,6},{6,7},{7,8},{8,9},{9,10},{10,1... | collective-permute-start | bytes 147464 | tf_op jit(solution)/shard_map/ppermute | solution.py:19
  76.1 9.6 %collective-permute-start.5 = (f32[16,768]{1,0:T(8,128)S(1)}, f32[16,768]{1,0:T(8,128)S(1)}, u32[]{:S(2)}, u32[]{:S(2)}) collective-permute-start(f32[16,768]{1,0:T(8,128)S(1)} %fusion.7), channel_id=1, source_target_pairs={{1,0},{2,1},{3,2},{4,3},{5,4},{6,5},{7,6},{8,7},{9,8},{10,9},{11,1... | collective-permute-start | bytes 147464 | tf_op jit(solution)/shard_map/ppermute | solution.py:19

commit v2 on v0

v2 whole, which is shorter than its diff:
```python
import jax
import jax.numpy as jnp
from jax import lax
from jax.experimental import pallas as pl
from jax.experimental.pallas import tpu as pltpu
from jax.sharding import PartitionSpec as P

SWEEPS = 3
AXES = ("planes", "rows")
LANES = 128
CAP = 32
SLOT = 5
PREPARE_MB = 50
PITCH = 9
WIDE = 256
PARTS = 8
PIECE = WIDE // PARTS
HBM = pl.BlockSpec(memory_space=pltpu.HBM)
VMEM = pl.BlockSpec(memory_space=pltpu.VMEM)


def place():
    return lax.axis_index(AXES)


def update(coupled, c, projected, diag):
    return jnp.maximum(c + (projected - coupled) / diag, 0.0)


def swap_blocks(x):
    row = lax.broadcasted_iota(jnp.int32, x.shape, 0) // 4
    col = lax.broadcasted_iota(jnp.int32, x.shape, 1) // CAP
    out = x
    for d in range(1, 4):
        moved = pltpu.roll(pltpu.roll(x, CAP * d, 1), 16 - 4 * d, 0)
        out = jnp.where((col - row) % 4 == d, moved, out)
    return out


def contrib_kernel(
    movie_ref, tile_hbm, neuron_hbm, weight_hbm,
    out_ref,
    slab, left, fan, weight, tile, neuron, row, row_s, neuron_s, sem2,
):
    group = 16 * PITCH
    small = [
        pltpu.make_async_copy(source, target, sem2.at[i])
        for i, (source, target) in enumerate(
            [
                (tile_hbm, tile),
                (neuron_hbm, neuron),
                (neuron_hbm, neuron_s),
                (weight_hbm, weight),
            ]
        )
    ]
    for copy in small:
        copy.start()
    out_ref[...] = jnp.zeros_like(out_ref)
    for copy in small:
        copy.wait()
    row[...] = (tile[...] >> 3) * group + (tile[...] & 7)
    to_scalar = pltpu.make_async_copy(row, row_s, sem2.at[5])
    to_scalar.start()

    @pl.loop(0, movie_ref.shape[0] // 16, unroll=2)
    def _(r):
        base = r * 2 * group
        for f in range(16):
            x = movie_ref[pl.ds(pl.multiple_of(r * 16, 16), 16), pl.ds(f * LANES, LANES)].astype(jnp.float32)
            slab[pl.ds(base + f * PITCH, 8), :] = x[:8]
            slab[pl.ds(base + group + f * PITCH, 8), :] = x[8:]

    to_scalar.wait()
    fan[...] = jnp.zeros_like(fan)
    eighth = lax.broadcasted_iota(jnp.int32, (16, WIDE), 1) % PIECE

    @pl.loop(0, tile.shape[0] * LANES // WIDE, unroll=tile.shape[0] * LANES // WIDE)
    def _(b):
        start = pl.multiple_of(b * WIDE, WIDE)
        for i in range(PARTS):
            fan[pl.ds(PIECE * i, PIECE), pl.ds(i * LANES, LANES)] = weight[pl.ds(start + PIECE * i, PIECE), :]
        for o in range(PIECE):
            entries = [PIECE * i + o for i in range(PARTS)]
            xs = [
                slab[pl.ds(row_s[2 * b + e // LANES, e % LANES], 16, stride=PITCH), :].astype(jnp.bfloat16)
                for e in entries
            ]
            for i, x in enumerate(xs):
                left[pl.ds(o * 16, 16), pl.ds(i * LANES, LANES)] = x
        every = lax.dot_general(
            left[...], fan[...], (((1,), (1,)), ((), ())), preferred_element_type=jnp.float32
        )
        sums = jnp.zeros((16, WIDE), jnp.float32)
        for o in range(PIECE):
            sums = jnp.where(eighth == o, every[o * 16 : o * 16 + 16], sums)
        for h in range(2):
            slots = swap_blocks(sums[:, h * LANES : (h + 1) * LANES])
            names = neuron[pl.ds(2 * b + h, 1), :].astype(jnp.float32)
            names = swap_blocks(jnp.broadcast_to(names, (16, LANES)))
            for g in range(4):
                owner = lax.div(neuron_s[2 * b + h, g * CAP], 768)
                out_ref[pl.ds(owner * SLOT, 4), :] = slots[4 * g : 4 * g + 4]
                out_ref[pl.ds(owner * SLOT + 4, 1), :] = names[4 * g : 4 * g + 1]


def open_kernel(out_ref):
    out_ref[...] = jnp.zeros_like(out_ref)


def opening():
    return pl.pallas_call(
        open_kernel,
        out_shape=jax.ShapeDtypeStruct((8, LANES), jnp.float32),
        out_specs=VMEM,
        compiler_params=pltpu.CompilerParams(vmem_limit_bytes=1 << 20, has_side_effects=True),
        cost_estimate=pl.CostEstimate(flops=10**10, bytes_accessed=10**7, transcendentals=0),
    )()


def contributions(movie, entry_tile, entry_neuron, entry_weights, devices):
    tiles = movie.shape[0]
    entries = entry_tile.shape[0]
    table = (entries // LANES, LANES)
    return pl.pallas_call(
        contrib_kernel,
        out_shape=jax.ShapeDtypeStruct((devices * SLOT, LANES), jnp.float32),
        in_specs=[VMEM] + [HBM] * 3,
        out_specs=VMEM,
        scratch_shapes=[
            pltpu.VMEM((tiles * 2 * PITCH + 16, LANES), jnp.float32),
            pltpu.VMEM((PIECE * 16, PARTS * LANES), jnp.bfloat16),
            pltpu.VMEM((WIDE, PARTS * LANES), jnp.bfloat16),
            pltpu.VMEM((entries, LANES), jnp.bfloat16),
            pltpu.VMEM(table, jnp.int32),
            pltpu.VMEM(table, jnp.int32),
            pltpu.VMEM(table, jnp.int32),
            pltpu.SMEM(table, jnp.int32),
            pltpu.SMEM(table, jnp.int32),
            pltpu.SemaphoreType.DMA((6,)),
        ],
        compiler_params=pltpu.CompilerParams(vmem_limit_bytes=48 << 20),
        cost_estimate=pl.CostEstimate(flops=10**10, bytes_accessed=10**7, transcendentals=0),
    )(movie, entry_tile.reshape(table), entry_neuron.reshape(table), entry_weights)


def combine_kernel(got_ref, ready_ref, out_ref, first_ref):
    sources = got_ref.shape[0] // SLOT
    first = (place() * 768).astype(jnp.float32)
    lane4 = lax.broadcasted_iota(jnp.int32, (1, LANES), 1) // CAP
    sub = lax.broadcasted_iota(jnp.int32, (256, LANES), 0).astype(jnp.float32)
    sums = jnp.zeros((96, 256), jnp.float32)
    for b in range(sources // 8):
        lefts, hots = [], []
        for i in range(2):
            row = (2 * b + i) * 4 * SLOT
            x = jnp.concatenate([got_ref[row + s * SLOT : row + s * SLOT + 4, :] for s in range(4)], axis=0)
            x = swap_blocks(x)
            name = got_ref[row + 4 : row + 5, :]
            for s in range(1, 4):
                name = jnp.where(lane4 == s, got_ref[row + s * SLOT + 4 : row + s * SLOT + 5, :], name)
            name = name - first
            high = jnp.where(name >= 512.0, 2.0, jnp.where(name >= 256.0, 1.0, 0.0))
            low = name - 256.0 * high
            big = x.astype(jnp.bfloat16).astype(jnp.float32)
            rest = x - big
            both = jnp.concatenate([big, rest], axis=0)
            lefts.append(
                jnp.concatenate([jnp.where(high == float(h), both, 0.0) for h in range(3)], axis=0).astype(jnp.bfloat16)
            )
            hots.append(jnp.where(sub == low, 1.0, 0.0).astype(jnp.bfloat16))
        sums = sums + lax.dot_general(
            jnp.concatenate(lefts, axis=1), jnp.concatenate(hots, axis=1), (((1,), (1,)), ((), ())),
            preferred_element_type=jnp.float32,
        )
    for h in range(3):
        out_ref[:, h * 256 : h * 256 + 256] = sums[h * 32 : h * 32 + 16] + sums[h * 32 + 16 : h * 32 + 32]
    first_ref[...] = update(ready_ref[0:16, :], ready_ref[16:32, :], out_ref[...], ready_ref[32:33, :])


def combine(got, ready):
    out = jax.ShapeDtypeStruct((16, ready.shape[1]), jnp.float32)
    return pl.pallas_call(
        combine_kernel,
        out_shape=(out, out),
        in_specs=[VMEM] * 2,
        out_specs=(VMEM, VMEM),
        compiler_params=pltpu.CompilerParams(vmem_limit_bytes=16 << 20),
        cost_estimate=pl.CostEstimate(flops=10**10, bytes_accessed=10**6, transcendentals=0),
    )(got, ready)


def halves(x):
    big = x.astype(jnp.bfloat16)
    return big, (x - big.astype(jnp.float32)).astype(jnp.bfloat16)


def times(c, high, low):
    big, rest = halves(c)
    main = jnp.dot(jnp.concatenate([big, rest], 0), high, preferred_element_type=jnp.float32)
    minor = jnp.dot(big, low, preferred_element_type=jnp.float32)
    return (minor + main[16:]) + main[:16]


def prepare_kernel(
    c_hbm, a_ref, b_ref, self_hbm, prev_hbm, next_hbm, out_ref, high_ref, low_ref, c, own, close, far, sem
):
    even = place() % 2 == 0

    def fetch(source, target, i):
        return pltpu.make_async_copy(source, target, sem.at[i])

    def fetch_both(close_hbm, far_hbm):
        fetch(close_hbm, close, 2).start()
        fetch(far_hbm, far, 3).start()

    fetch(c_hbm, c, 0).start()
    fetch(self_hbm, own, 1).start()
    pl.when(even)(lambda: fetch_both(next_hbm, prev_hbm))
    pl.when(jnp.logical_not(even))(lambda: fetch_both(prev_hbm, next_hbm))
    fetch(c_hbm, c, 0).wait()
    fetch(self_hbm, own, 1).wait()
    eye = lax.broadcasted_iota(jnp.int32, (LANES, LANES), 0) == lax.broadcasted_iota(jnp.int32, (LANES, LANES), 1)
    for i in range(own.shape[0] // LANES):
        at = pl.ds(i * LANES, LANES)
        diag = jnp.sum(jnp.where(eye, own[at, at], 0.0), axis=0, keepdims=True)
        out_ref[32:40, at] = jnp.broadcast_to(diag, (8, LANES))
    out_ref[16:32, :] = c[...]
    total = times(c[...], *halves(own[...]))
    fetch(next_hbm, close, 2).wait()
    total = total + times(a_ref[...], *halves(close[...]))
    fetch(prev_hbm, far, 3).wait()
    high_ref[...], low_ref[...] = halves(far[...])
    out_ref[0:16, :] = total + times(b_ref[...], high_ref[...], low_ref[...])


def prepare(c, a, b, matrices):
    n = c.shape[1]
    half = jax.ShapeDtypeStruct((n, n), jnp.bfloat16)
    return pl.pallas_call(
        prepare_kernel,
        out_shape=(jax.ShapeDtypeStruct((40, n), jnp.float32), half, half),
        in_specs=[HBM, VMEM, VMEM, HBM, HBM, HBM],
        out_specs=(VMEM,) * 3,
        scratch_shapes=[pltpu.VMEM(c.shape, jnp.float32)]
        + [pltpu.VMEM((n, n), jnp.float32)] * 3
        + [pltpu.SemaphoreType.DMA((4,))],
        compiler_params=pltpu.CompilerParams(vmem_limit_bytes=PREPARE_MB << 20),
        cost_estimate=pl.CostEstimate(flops=5 * 10**9, bytes_accessed=10**7, transcendentals=0),
    )(c, a, b, *matrices)


def near_kernel(c_ref, a_ref, self_ref, prev_ref, next_ref, out_ref):
    own = times(c_ref[...], *halves(self_ref[...]))

    def rest(near_ref):
        out_ref[...] = own + times(a_ref[...], *halves(near_ref[...]))

    even = place() % 2 == 0
    pl.when(even)(lambda: rest(next_ref))
    pl.when(jnp.logical_not(even))(lambda: rest(prev_ref))


def near(c, a, matrices):
    return pl.pallas_call(
        near_kernel,
        out_shape=jax.ShapeDtypeStruct(c.shape, jnp.float32),
        in_specs=[VMEM] * 5,
        out_specs=VMEM,
        compiler_params=pltpu.CompilerParams(vmem_limit_bytes=16 << 20),
        cost_estimate=pl.CostEstimate(flops=5 * 10**8, bytes_accessed=10**6, transcendentals=0),
    )(c, a, *matrices)


def step_kernel(part_ref, b_ref, high_ref, low_ref, c_ref, projected_ref, ready_ref, out_ref):
    far = times(b_ref[...], high_ref[...], low_ref[...])
    out_ref[...] = update(part_ref[...] + far, c_ref[...], projected_ref[...], ready_ref[32:33, :])


def step(part, b, weights, c, projected, ready):
    return pl.pallas_call(
        step_kernel,
        out_shape=jax.ShapeDtypeStruct(c.shape, jnp.float32),
        in_specs=[VMEM] * 7,
        out_specs=VMEM,
        compiler_params=pltpu.CompilerParams(vmem_limit_bytes=16 << 20),
        cost_estimate=pl.CostEstimate(flops=3 * 10**8, bytes_accessed=10**6, transcendentals=0),
    )(part, b, *weights, c, projected, ready)


def exchange(c):
    n = lax.axis_size(AXES)
    a = lax.ppermute(c, AXES, [(i, i ^ 1) for i in range(n)])
    b = lax.ppermute(c, AXES, [(i, i + 1) for i in range(1, n - 1, 2)] + [(i + 1, i) for i in range(1, n - 1, 2)])
    return a, b


def local(
    movie,
    entry_tile,
    entry_neuron,
    entry_weights,
    intersection_self,
    intersection_prev,
    intersection_next,
    prev_traces,
):
    devices = lax.axis_size(AXES)
    matrices = (intersection_self, intersection_prev, intersection_next)
    c, _ = lax.optimization_barrier((prev_traces, opening()))
    a, b = exchange(c)
    here = pltpu.with_memory_space_constraint(movie, pltpu.VMEM)
    send = contributions(here, entry_tile, entry_neuron, entry_weights, devices)
    got = lax.all_to_all(send.reshape(devices, 1, SLOT * LANES), AXES, 0, 0)
    ready, *split = prepare(c, a, b, matrices)
    projected, c = combine(got.reshape(devices * SLOT, LANES), ready)
    for _ in range(SWEEPS - 1):
        a, b = exchange(c)
        part = near(c, a, matrices)
        c = step(part, b, split, c, projected, ready)
    return c


def solution(mesh):
    return jax.shard_map(
        local,
        mesh=mesh,
        in_specs=(
            P(AXES, None),
            P(AXES),
            P(AXES),
            P(AXES, None),
            P(AXES, None),
            P(AXES, None),
            P(AXES, None),
            P(None, AXES),
        ),
        out_specs=P(None, AXES),
        check_vma=False,
    )
```

time: 358 us -> 54.2 us (0.15)
  waiting for transfers between devices: 194 us -> 17.4 us
  local copies, waits for them, and re-layouts: 65.5 us -> 0.22 us
  other arithmetic: 32.3 us -> 0 us
  matrix products: 22.9 us -> 0 us
  Pallas kernels: 0 us -> 14.4 us
  between operations: 13.5 us -> 0.15 us
  starting transfers between devices: 29.7 us -> 21.7 us
    reduce_scatter x1 -> x0, waiting for transfers between devices: 193 us -> none  [local(): lax.psum_scatter(partial_value, ('planes', 'rows'), scatter_dimension=1,...]
    scatter-add x1 -> x0, other arithmetic: 31.4 us -> none  [local(): jnp.zeros((frames, neur_dev * devices), jnp.float32).at[:, entry_neuron]]
    scatter-add x1 -> x0, local copies, waits for them, and re-layouts: 27.7 us -> none  [local(): jnp.zeros((frames, neur_dev * devices), jnp.float32).at[:, entry_neuron]]
    gather x2 -> x0, local copies, waits for them, and re-layouts: 27.1 us -> none  [the longest x1 20.8 us: local(): picked = movie[entry_tile].reshape(entries, frames, voxels)]
    dot_general x10 -> x0, matrix products: 22.9 us -> none  [the longest x1 7.79 us: local(): jnp.einsum('efv,ev->ef', picked, entry_weights, preferred_element_type=jn...]
    pallas_call x0 -> x8, Pallas kernels: none -> 14.4 us  [the longest x1 5.79 us: contributions(): pl.pallas_call(contrib_kernel, out_shape=jax.ShapeDtypeStruct((devices *...]
    ppermute x6, starting transfers between devices: 29.7 us -> 15.7 us  [the longest x3 15.5 us: exchange(): lax.ppermute(c, AXES, [(i, i + 1) for i in range(1, n - 1, 2)] + [(i + 1,...]
    unnamed x15 -> x10, local copies, waits for them, and re-layouts: 10.6 us -> 0.22 us
  transfers between devices with their start and end apart: 7 -> 7, of which waited for: 3 -> 3; matrix products, arithmetic and copies ran while one was open for 4% -> 0% of each run, Pallas kernels for 0% -> 21%
where the time goes in v2:
time: 54.2 us; the launch traced here: 53.9 us
  starting transfers between devices  21.7 us (40%)
  waiting for transfers between devices  17.4 us (32%)
  Pallas kernels  14.4 us (27%)
    ppermute x3, starting transfers between devices, exchange(): lax.ppermute(c, AXES, [(i, i + 1) for i in range(1, n - 1, 2)] + [(i + 1,...  15.5 us
    ppermute x3, waiting for transfers between devices, exchange(): lax.ppermute(c, AXES, [(i, i + 1) for i in range(1, n - 1, 2)] + [(i + 1,...  10.1 us
    all_to_all x1, waiting for transfers between devices, local(): got = lax.all_to_all(send.reshape(devices, 1, SLOT * LANES), AXES, 0, 0)  7.28 us
    all_to_all x1, starting transfers between devices, local(): got = lax.all_to_all(send.reshape(devices, 1, SLOT * LANES), AXES, 0, 0)  6.01 us
    pallas_call x1, Pallas kernels, contributions(): pl.pallas_call(contrib_kernel, out_shape=jax.ShapeDtypeStruct((devices *...  5.79 us
    pallas_call x1, Pallas kernels, prepare(): pl.pallas_call(prepare_kernel, out_shape=(jax.ShapeDtypeStruct((40, n), j...  3.78 us
    pallas_call x2, Pallas kernels, near(): pl.pallas_call(near_kernel, out_shape=jax.ShapeDtypeStruct(c.shape, jnp.f...  1.91 us
    pallas_call x2, Pallas kernels, step(): pl.pallas_call(step_kernel, out_shape=jax.ShapeDtypeStruct(c.shape, jnp.f...  1.51 us
  transfers between devices with their start and end apart: 7, of which 3 were waited for; matrix products, arithmetic and copies ran while one was open for 0% of the time, Pallas kernels for 21%

profile of v2, /device:TPU:2, one launch (start us, length us, event | category | flops | bytes accessed | tf_op | source)
XLA Modules:
  0.0 53.9 jit_solution(2426788566228980062)
XLA Ops:
  0.0 0.0 copy-start.4
  0.0 0.0 copy-start.3
  0.0 0.6 %shard_map.83 = f32[8,128]{1,0:T(8,128)} custom-call(), custom_call_target="tpu_custom_call" | custom-call | flops 10000000000 | bytes 10000000 | tf_op jit(solution)/shard_map/pallas_call | solution.py:112
  0.6 0.2 copy-done.4
  0.8 8.1 %collective-permute-start.1 = (f32[16,768]{1,0:T(8,128)S(1)}, f32[16,768]{1,0:T(8,128)S(1)}, u32[]{:S(2)}, u32[]{:S(2)}) collective-permute-start(f32[16,768]{1,0:T(8,128)S(1)} %copy-done.4), channel_id=1, source_target_pairs={{1,2},{3,4},{5,6},{7,8},{9,10},{11,12},{13,14},{15,16},{17,18},{19... | collective-permute-start | bytes 147464 | tf_op jit(solution)/shard_map/ppermute | solution.py:294
  8.9 0.1 collective-permute-start
  9.0 0.0 copy-done.3
  9.0 5.8 %shard_map.82 = f32[640,128]{1,0:T(8,128)} custom-call(bf16[2048,2048]{1,0:T(8,128)(2,1)S(1)} %copy-done.3, s32[16,128]{1,0:T(8,128)} %bitcast.6, s32[16,128]{1,0:T(8,128)} %bitcast.7, bf16[2048,128]{1,0:T(8,128)(2,1)} %weight_hbm.1), custom_call_target="tpu_custom_call" | custom-call | flops 10000000000 | bytes 10000000 | tf_op jit(solution)/shard_map/pallas_call | solution.py:125
  14.8 6.0 %all-to-all-start = ((f32[128,1,640]{2,1,0:T(1,128)}), f32[128,1,640]{2,1,0:T(1,128)S(1)}, u32[]{:S(2)}, u32[]{:S(2)}) async-start(f32[128,1,640]{2,1,0:T(1,128)} %bitcast.5), calls=%async_computation | async-start | bytes 655360 | tf_op jit(solution)/shard_map/all_to_all | solution.py:314
  20.8 0.0 collective-permute-done.1.b_ref
  20.8 0.0 collective-permute-done.a_ref
  20.8 3.8 %shard_map.84 = (f32[40,768]{1,0:T(8,128)S(1)}, bf16[768,768]{1,0:T(8,128)(2,1)S(1)}, bf16[768,768]{1,0:T(8,128)(2,1)S(1)}) custom-call(f32[16,768]{1,0:T(8,128)S(1)} %copy-done.4, f32[16,768]{1,0:T(8,128)S(1)} %collective-permute-done.a_ref, f32[16,768]{1,0:T(8,128)S(1)} %collective-permute-done.1.b_ref, f32[768,768]{1,0:T(8,128)} %self_ref.3, ...), custom_call_target="tpu_custom_call" | custom-call | flops 5000000000 | bytes 10000000 | tf_op jit(solution)/shard_map/pallas_call | solution.py:240
  24.6 7.3 %all-to-all-done = f32[128,1,640]{2,1,0:T(1,128)S(1)} async-done(((f32[128,1,640]{2,1,0:T(1,128)}), f32[128,1,640]{2,1,0:T(1,128)S(1)}, u32[]{:S(2)}, u32[]{:S(2)}) %all-to-all-start) | async-done | bytes 327712 | tf_op jit(solution)/shard_map/all_to_all | solution.py:314
  31.9 0.0 copy-start
  31.9 0.0 copy-start.1
  31.9 0.0 copy-start.2
  31.9 0.8 %shard_map.85 = (f32[16,768]{1,0:T(8,128)S(1)}, f32[16,768]{1,0:T(8,128)S(1)}) custom-call(f32[640,128]{1,0:T(8,128)S(1)} %bitcast.4, f32[40,768]{1,0:T(8,128)S(1)} %get-tuple-element.12.ready_ref), custom_call_target="tpu_custom_call" | custom-call | flops 10000000000 | bytes 1000000 | tf_op jit(solution)/shard_map/pallas_call | solution.py:183
  32.7 0.1 collective-permute-start.2
  32.8 3.9 %collective-permute-start.3 = (f32[16,768]{1,0:T(8,128)S(1)}, f32[16,768]{1,0:T(8,128)S(1)}, u32[]{:S(2)}, u32[]{:S(2)}) collective-permute-start(f32[16,768]{1,0:T(8,128)S(1)} %get-tuple-element.13.c_ref), channel_id=1, source_target_pairs={{1,2},{3,4},{5,6},{7,8},{9,10},{11,12},{13,14},{15,16},{17,18},{19... | collective-permute-start | bytes 147464 | tf_op jit(solution)/shard_map/ppermute | solution.py:294
  36.7 0.0 collective-permute-done.2.a_ref
  36.7 0.0 copy-done
  36.7 0.0 copy-done.1
  36.7 0.0 copy-done.2
  36.7 1.0 %shard_map.86.part_ref = f32[16,768]{1,0:T(8,128)S(1)} custom-call(f32[16,768]{1,0:T(8,128)S(1)} %get-tuple-element.13.c_ref, f32[16,768]{1,0:T(8,128)S(1)} %collective-permute-done.2.a_ref, f32[768,768]{1,0:T(8,128)S(1)} %copy-done, f32[768,768]{1,0:T(8,128)S(1)} %copy-done.1, f32[768,768]{1,0:T(8,128)S(1)} %copy-done.2), custom_call_target="tpu_custom_call" | custom-call | flops 500000000 | bytes 1000000 | tf_op jit(solution)/shard_map/pallas_call | solution.py:265
  37.7 5.0 %collective-permute-done.3.b_ref = f32[16,768]{1,0:T(8,128)S(1)} collective-permute-done((f32[16,768]{1,0:T(8,128)S(1)}, f32[16,768]{1,0:T(8,128)S(1)}, u32[]{:S(2)}, u32[]{:S(2)}) %collective-permute-start.3) | collective-permute-done | bytes 49184 | tf_op jit(solution)/shard_map/ppermute | solution.py:294
  42.7 0.4 shard_map.87.c_ref
  43.1 0.0 collective-permute-start.4
  43.2 3.6 %collective-permute-start.5 = (f32[16,768]{1,0:T(8,128)S(1)}, f32[16,768]{1,0:T(8,128)S(1)}, u32[]{:S(2)}, u32[]{:S(2)}) collective-permute-start(f32[16,768]{1,0:T(8,128)S(1)} %shard_map.87.c_ref), channel_id=1, source_target_pairs={{1,2},{3,4},{5,6},{7,8},{9,10},{11,12},{13,14},{15,16},{17,18},{19... | collective-permute-start | bytes 147464 | tf_op jit(solution)/shard_map/ppermute | solution.py:294
  46.8 0.0 collective-permute-done.4.a_ref
  46.8 1.0 %shard_map.88.part_ref = f32[16,768]{1,0:T(8,128)S(1)} custom-call(f32[16,768]{1,0:T(8,128)S(1)} %shard_map.87.c_ref, f32[16,768]{1,0:T(8,128)S(1)} %collective-permute-done.4.a_ref, f32[768,768]{1,0:T(8,128)S(1)} %copy-done, f32[768,768]{1,0:T(8,128)S(1)} %copy-done.1, f32[768,768]{1,0:T(8,128)S(1)} %copy-done.2), custom_call_target="tpu_custom_call" | custom-call | flops 500000000 | bytes 1000000 | tf_op jit(solution)/shard_map/pallas_call | solution.py:265
  47.8 5.1 %collective-permute-done.5.b_ref = f32[16,768]{1,0:T(8,128)S(1)} collective-permute-done((f32[16,768]{1,0:T(8,128)S(1)}, f32[16,768]{1,0:T(8,128)S(1)}, u32[]{:S(2)}, u32[]{:S(2)}) %collective-permute-start.5) | collective-permute-done | bytes 49184 | tf_op jit(solution)/shard_map/ppermute | solution.py:294
  52.8 1.1 %shard_map.89 = f32[16,768]{1,0:T(8,128)} custom-call(f32[16,768]{1,0:T(8,128)S(1)} %shard_map.88.part_ref, f32[16,768]{1,0:T(8,128)S(1)} %collective-permute-done.5.b_ref, bf16[768,768]{1,0:T(8,128)(2,1)S(1)} %get-tuple-element.14.high_ref, bf16[768,768]{1,0:T(8,128)(2,1)S(1)} %get-tuple-element.15.low_ref, f32[16,768]{1,0:T(8,128)S(1)} %shard_map.87.c_ref, ...), custom_call_target="tpu_custom_call" | custom-call | flops 300000000 | bytes 1000000 | tf_op jit(solution)/shard_map/pallas_call | solution.py:281
Async XLA Ops:
  0.0 0.8 %copy-start.4 = (f32[16,768]{1,0:T(8,128)S(1)}, f32[16,768]{1,0:T(8,128)}, u32[]{:S(2)}) copy-start(f32[16,768]{1,0:T(8,128)} %c_hbm) | copy-start | bytes 147460
  0.0 9.0 %copy-start.3 = (bf16[2048,2048]{1,0:T(8,128)(2,1)S(1)}, bf16[2048,2048]{1,0:T(8,128)(2,1)}, u32[]{:S(2)}) copy-start(bf16[2048,2048]{1,0:T(8,128)(2,1)} %movie_ref.1) | copy-start | bytes 25165828
  0.8 20.0 %collective-permute-start.1 = (f32[16,768]{1,0:T(8,128)S(1)}, f32[16,768]{1,0:T(8,128)S(1)}, u32[]{:S(2)}, u32[]{:S(2)}) collective-permute-start(f32[16,768]{1,0:T(8,128)S(1)} %copy-done.4), channel_id=1, source_target_pairs={{1,2},{3,4},{5,6},{7,8},{9,10},{11,12},{13,14},{15,16},{17,18},{19... | collective-permute-start | bytes 147464 | tf_op jit(solution)/shard_map/ppermute | solution.py:294
  8.9 11.9 %collective-permute-start = (f32[16,768]{1,0:T(8,128)S(1)}, f32[16,768]{1,0:T(8,128)S(1)}, u32[]{:S(2)}, u32[]{:S(2)}) collective-permute-start(f32[16,768]{1,0:T(8,128)S(1)} %copy-done.4), channel_id=1, source_target_pairs={{0,1},{1,0},{2,3},{3,2},{4,5},{5,4},{6,7},{7,6},{8,9},{9,8},{10,11... | collective-permute-start | bytes 147464 | tf_op jit(solution)/shard_map/ppermute | solution.py:293
  14.8 17.1 %all-to-all-start = ((f32[128,1,640]{2,1,0:T(1,128)}), f32[128,1,640]{2,1,0:T(1,128)S(1)}, u32[]{:S(2)}, u32[]{:S(2)}) async-start(f32[128,1,640]{2,1,0:T(1,128)} %bitcast.5), calls=%async_computation | async-start | bytes 655360 | tf_op jit(solution)/shard_map/all_to_all | solution.py:314
  31.9 4.8 %copy-start = (f32[768,768]{1,0:T(8,128)S(1)}, f32[768,768]{1,0:T(8,128)}, u32[]{:S(2)}) copy-start(f32[768,768]{1,0:T(8,128)} %self_ref.3) | copy-start | bytes 7077892
  31.9 4.8 %copy-start.1 = (f32[768,768]{1,0:T(8,128)S(1)}, f32[768,768]{1,0:T(8,128)}, u32[]{:S(2)}) copy-start(f32[768,768]{1,0:T(8,128)} %prev_ref.3) | copy-start | bytes 7077892
  31.9 4.8 %copy-start.2 = (f32[768,768]{1,0:T(8,128)S(1)}, f32[768,768]{1,0:T(8,128)}, u32[]{:S(2)}) copy-start(f32[768,768]{1,0:T(8,128)} %next_ref.3) | copy-start | bytes 7077892
  32.7 4.0 %collective-permute-start.2 = (f32[16,768]{1,0:T(8,128)S(1)}, f32[16,768]{1,0:T(8,128)S(1)}, u32[]{:S(2)}, u32[]{:S(2)}) collective-permute-start(f32[16,768]{1,0:T(8,128)S(1)} %get-tuple-element.13.c_ref), channel_id=1, source_target_pairs={{0,1},{1,0},{2,3},{3,2},{4,5},{5,4},{6,7},{7,6},{8,9},{9,8},{10,11... | collective-permute-start | bytes 147464 | tf_op jit(solution)/shard_map/ppermute | solution.py:293
  32.8 9.9 %collective-permute-start.3 = (f32[16,768]{1,0:T(8,128)S(1)}, f32[16,768]{1,0:T(8,128)S(1)}, u32[]{:S(2)}, u32[]{:S(2)}) collective-permute-start(f32[16,768]{1,0:T(8,128)S(1)} %get-tuple-element.13.c_ref), channel_id=1, source_target_pairs={{1,2},{3,4},{5,6},{7,8},{9,10},{11,12},{13,14},{15,16},{17,18},{19... | collective-permute-start | bytes 147464 | tf_op jit(solution)/shard_map/ppermute | solution.py:294
  43.1 3.7 %collective-permute-start.4 = (f32[16,768]{1,0:T(8,128)S(1)}, f32[16,768]{1,0:T(8,128)S(1)}, u32[]{:S(2)}, u32[]{:S(2)}) collective-permute-start(f32[16,768]{1,0:T(8,128)S(1)} %shard_map.87.c_ref), channel_id=1, source_target_pairs={{0,1},{1,0},{2,3},{3,2},{4,5},{5,4},{6,7},{7,6},{8,9},{9,8},{10,11... | collective-permute-start | bytes 147464 | tf_op jit(solution)/shard_map/ppermute | solution.py:293
  43.2 9.6 %collective-permute-start.5 = (f32[16,768]{1,0:T(8,128)S(1)}, f32[16,768]{1,0:T(8,128)S(1)}, u32[]{:S(2)}, u32[]{:S(2)}) collective-permute-start(f32[16,768]{1,0:T(8,128)S(1)} %shard_map.87.c_ref), channel_id=1, source_target_pairs={{1,2},{3,4},{5,6},{7,8},{9,10},{11,12},{13,14},{15,16},{17,18},{19... | collective-permute-start | bytes 147464 | tf_op jit(solution)/shard_map/ppermute | solution.py:294

commit v3 on v2

--- a/solution.py
+++ b/solution.py
@@ -9,7 +9,7 @@
 AXES = ("planes", "rows")
 LANES = 128
 CAP = 32
-SLOT = 5
+SLOT = 9
 PREPARE_MB = 50
 PITCH = 9
 WIDE = 256
@@ -21,6 +21,10 @@
 
 def place():
     return lax.axis_index(AXES)
+
+
+def across(block):
+    return block + 2 * (block & 1) - 1
 
 
 def update(coupled, c, projected, diag):
@@ -43,6 +47,7 @@
     slab, left, fan, weight, tile, neuron, row, row_s, neuron_s, sem2,
 ):
     group = 16 * PITCH
+    devices = out_ref.shape[0] // SLOT
     small = [
         pltpu.make_async_copy(source, target, sem2.at[i])
         for i, (source, target) in enumerate(
@@ -100,8 +105,12 @@
             names = swap_blocks(jnp.broadcast_to(names, (16, LANES)))
             for g in range(4):
                 owner = lax.div(neuron_s[2 * b + h, g * CAP], 768)
-                out_ref[pl.ds(owner * SLOT, 4), :] = slots[4 * g : 4 * g + 4]
-                out_ref[pl.ds(owner * SLOT + 4, 1), :] = names[4 * g : 4 * g + 1]
+                other = across(owner)
+                other = jnp.where((other < 0) | (other >= devices), owner, other)
+                for to, half in ((owner, 0), (other, 1)):
+                    out_ref[pl.ds(to * SLOT + 4 * half, 4), :] = slots[4 * g : 4 * g + 4]
+                    at = pl.ds(half * 64, 64)
+                    out_ref[pl.ds(to * SLOT + 8, 1), at] = names[4 * g : 4 * g + 1, half * 64 : half * 64 + 64]
 
 
 def open_kernel(out_ref):
@@ -144,50 +153,67 @@
     )(movie, entry_tile.reshape(table), entry_neuron.reshape(table), entry_weights)
 
 
-def combine_kernel(got_ref, ready_ref, out_ref, first_ref):
+def combine_kernel(got_ref, ready_ref, other_ref, out_ref, first_ref, beyond_ref):
     sources = got_ref.shape[0] // SLOT
-    first = (place() * 768).astype(jnp.float32)
-    lane4 = lax.broadcasted_iota(jnp.int32, (1, LANES), 1) // CAP
+    me = place()
+    blocks = (me, across(me))
+    lane = lax.broadcasted_iota(jnp.int32, (1, LANES), 1)
     sub = lax.broadcasted_iota(jnp.int32, (256, LANES), 0).astype(jnp.float32)
-    sums = jnp.zeros((96, 256), jnp.float32)
+    sums = [jnp.zeros((96, 256), jnp.float32)] * 2
+
     for b in range(sources // 8):
-        lefts, hots = [], []
+        lefts, hots = ([], []), ([], [])
         for i in range(2):
             row = (2 * b + i) * 4 * SLOT
-            x = jnp.concatenate([got_ref[row + s * SLOT : row + s * SLOT + 4, :] for s in range(4)], axis=0)
-            x = swap_blocks(x)
-            name = got_ref[row + 4 : row + 5, :]
-            for s in range(1, 4):
-                name = jnp.where(lane4 == s, got_ref[row + s * SLOT + 4 : row + s * SLOT + 5, :], name)
-            name = name - first
-            high = jnp.where(name >= 512.0, 2.0, jnp.where(name >= 256.0, 1.0, 0.0))
-            low = name - 256.0 * high
-            big = x.astype(jnp.bfloat16).astype(jnp.float32)
-            rest = x - big
-            both = jnp.concatenate([big, rest], axis=0)
-            lefts.append(
-                jnp.concatenate([jnp.where(high == float(h), both, 0.0) for h in range(3)], axis=0).astype(jnp.bfloat16)
+            r0, r1, r2, r3 = (got_ref[row + s * SLOT + 8 : row + s * SLOT + 9, :] for s in range(4))
+            low_pair = jnp.where(lane % 64 < 32, r0, r1)
+            high_pair = jnp.where(lane % 64 < 32, r2, r3)
+            listed = (
+                jnp.where(lane < 64, low_pair, pltpu.roll(high_pair, 64, 1)),
+                jnp.where(lane < 64, pltpu.roll(low_pair, 64, 1), high_pair),
             )
-            hots.append(jnp.where(sub == low, 1.0, 0.0).astype(jnp.bfloat16))
-        sums = sums + lax.dot_general(
-            jnp.concatenate(lefts, axis=1), jnp.concatenate(hots, axis=1), (((1,), (1,)), ((), ())),
-            preferred_element_type=jnp.float32,
-        )
+            for k in range(2):
+                x = jnp.concatenate(
+                    [got_ref[row + s * SLOT + 4 * k : row + s * SLOT + 4 * k + 4, :] for s in range(4)], axis=0
+                )
+                x = swap_blocks(x)
+                name = listed[k] - (blocks[k] * 768).astype(jnp.float32)
+                high = jnp.where(name >= 512.0, 2.0, jnp.where(name >= 256.0, 1.0, 0.0))
+                low = name - 256.0 * high
+                big = x.astype(jnp.bfloat16).astype(jnp.float32)
+                both = jnp.concatenate([big, x - big], axis=0)
+                lefts[k].append(
+                    jnp.concatenate([jnp.where(high == float(h), both, 0.0) for h in range(3)], axis=0).astype(jnp.bfloat16)
+                )
+                hots[k].append(jnp.where(sub == low, 1.0, 0.0).astype(jnp.bfloat16))
+        for k in range(2):
+            sums[k] = sums[k] + lax.dot_general(
+                jnp.concatenate(lefts[k], axis=1), jnp.concatenate(hots[k], axis=1), (((1,), (1,)), ((), ())),
+                preferred_element_type=jnp.float32,
+            )
     for h in range(3):
-        out_ref[:, h * 256 : h * 256 + 256] = sums[h * 32 : h * 32 + 16] + sums[h * 32 + 16 : h * 32 + 32]
-    first_ref[...] = update(ready_ref[0:16, :], ready_ref[16:32, :], out_ref[...], ready_ref[32:33, :])
-
-
-def combine(got, ready):
+        at = pl.ds(h * 256, 256)
+        for k, (ref, target) in enumerate([(ready_ref, first_ref), (other_ref, beyond_ref)]):
+            projected = sums[k][h * 32 : h * 32 + 16] + sums[k][h * 32 + 16 : h * 32 + 32]
+            if k == 0:
+                out_ref[:, at] = projected
+            target[:, at] = update(ref[0:16, at], ref[16:32, at], projected, ref[32:33, at])
+
+    @pl.when((blocks[1] < 0) | (blocks[1] >= sources))
+    def _():
+        beyond_ref[...] = jnp.zeros_like(beyond_ref)
+
+
+def combine(got, ready, other):
     out = jax.ShapeDtypeStruct((16, ready.shape[1]), jnp.float32)
     return pl.pallas_call(
         combine_kernel,
-        out_shape=(out, out),
-        in_specs=[VMEM] * 2,
-        out_specs=(VMEM, VMEM),
+        out_shape=(out,) * 3,
+        in_specs=[VMEM] * 3,
+        out_specs=(VMEM,) * 3,
         compiler_params=pltpu.CompilerParams(vmem_limit_bytes=16 << 20),
         cost_estimate=pl.CostEstimate(flops=10**10, bytes_accessed=10**6, transcendentals=0),
-    )(got, ready)
+    )(got, ready, other)
 
 
 def halves(x):
@@ -288,11 +314,14 @@
     )(part, b, *weights, c, projected, ready)
 
 
-def exchange(c):
+def swap_in_chip(c):
     n = lax.axis_size(AXES)
-    a = lax.ppermute(c, AXES, [(i, i ^ 1) for i in range(n)])
-    b = lax.ppermute(c, AXES, [(i, i + 1) for i in range(1, n - 1, 2)] + [(i + 1, i) for i in range(1, n - 1, 2)])
-    return a, b
+    return lax.ppermute(c, AXES, [(i, i ^ 1) for i in range(n)])
+
+
+def swap_across(c):
+    n = lax.axis_size(AXES)
+    return lax.ppermute(c, AXES, [(i, across(i)) for i in range(1, n - 1)])
 
 
 def local(
@@ -308,14 +337,17 @@
     devices = lax.axis_size(AXES)
     matrices = (intersection_self, intersection_prev, intersection_next)
     c, _ = lax.optimization_barrier((prev_traces, opening()))
-    a, b = exchange(c)
+    a, b = swap_in_chip(c), swap_across(c)
     here = pltpu.with_memory_space_constraint(movie, pltpu.VMEM)
     send = contributions(here, entry_tile, entry_neuron, entry_weights, devices)
     got = lax.all_to_all(send.reshape(devices, 1, SLOT * LANES), AXES, 0, 0)
     ready, *split = prepare(c, a, b, matrices)
-    projected, c = combine(got.reshape(devices * SLOT, LANES), ready)
-    for _ in range(SWEEPS - 1):
-        a, b = exchange(c)
+    other = swap_across(ready)
+    projected, c, b = combine(got.reshape(devices * SLOT, LANES), ready, other)
+    for sweep in range(1, SWEEPS):
+        a = swap_in_chip(c)
+        if sweep > 1:
+            b = swap_across(c)
         part = near(c, a, matrices)
         c = step(part, b, split, c, projected, ready)
     return c

time: 54.2 us -> 51 us (0.941)
  waiting for transfers between devices: 17.4 us -> 6.08 us
  starting transfers between devices: 21.7 us -> 28.7 us
  Pallas kernels: 14.4 us -> 15.3 us
    all_to_all x1, waiting for transfers between devices: 7.28 us -> 0.01 us  [local(): got = lax.all_to_all(send.reshape(devices, 1, SLOT * LANES), AXES, 0, 0)]
    ppermute x6, starting transfers between devices: 15.7 us -> 22.7 us  [the longest x3 22.5 us: swap_across(): return lax.ppermute(c, AXES, [(i, across(i)) for i in range(1, n - 1)])]
    ppermute x6, waiting for transfers between devices: 10.1 us -> 6.07 us  [the longest x3 4.85 us: swap_across(): return lax.ppermute(c, AXES, [(i, across(i)) for i in range(1, n - 1)])]
    pallas_call x1, Pallas kernels: 0.82 us -> 1.49 us  [combine(): pl.pallas_call(combine_kernel, out_shape=(out,) * 3, in_specs=[VMEM] * 3,...]
where the time goes in v3:
time: 51 us; the launch traced here: 50.7 us
  starting transfers between devices  28.7 us (56%)
  Pallas kernels  15.3 us (30%)
  waiting for transfers between devices  6.08 us (12%)
    ppermute x3, starting transfers between devices, swap_across(): return lax.ppermute(c, AXES, [(i, across(i)) for i in range(1, n - 1)])  22.5 us
    all_to_all x1, starting transfers between devices, local(): got = lax.all_to_all(send.reshape(devices, 1, SLOT * LANES), AXES, 0, 0)  6.02 us
    pallas_call x1, Pallas kernels, contributions(): pl.pallas_call(contrib_kernel, out_shape=jax.ShapeDtypeStruct((devices *...  6 us
    ppermute x3, waiting for transfers between devices, swap_across(): return lax.ppermute(c, AXES, [(i, across(i)) for i in range(1, n - 1)])  4.85 us
    pallas_call x1, Pallas kernels, prepare(): pl.pallas_call(prepare_kernel, out_shape=(jax.ShapeDtypeStruct((40, n), j...  3.78 us
    pallas_call x2, Pallas kernels, near(): pl.pallas_call(near_kernel, out_shape=jax.ShapeDtypeStruct(c.shape, jnp.f...  1.91 us
    pallas_call x2, Pallas kernels, step(): pl.pallas_call(step_kernel, out_shape=jax.ShapeDtypeStruct(c.shape, jnp.f...  1.52 us
    pallas_call x1, Pallas kernels, combine(): pl.pallas_call(combine_kernel, out_shape=(out,) * 3, in_specs=[VMEM] * 3,...  1.49 us
  transfers between devices with their start and end apart: 7, of which 3 were waited for; matrix products, arithmetic and copies ran while one was open for 0% of the time, Pallas kernels for 21%

profile of v3, /device:TPU:2, one launch (start us, length us, event | category | flops | bytes accessed | tf_op | source)
XLA Modules:
  0.0 50.7 jit_solution(11847257636096096658)
XLA Ops:
  0.0 0.0 copy-start.4
  0.0 0.0 copy-start.3
  0.0 0.6 %shard_map.83 = f32[8,128]{1,0:T(8,128)} custom-call(), custom_call_target="tpu_custom_call" | custom-call | flops 10000000000 | bytes 10000000 | tf_op jit(solution)/shard_map/pallas_call | solution.py:121
  0.6 0.2 copy-done.4
  0.8 8.1 %collective-permute-start.1 = (f32[16,768]{1,0:T(8,128)S(1)}, f32[16,768]{1,0:T(8,128)S(1)}, u32[]{:S(2)}, u32[]{:S(2)}) collective-permute-start(f32[16,768]{1,0:T(8,128)S(1)} %copy-done.4), channel_id=1, source_target_pairs={{1,2},{2,1},{3,4},{4,3},{5,6},{6,5},{7,8},{8,7},{9,10},{10,9},{11,... | collective-permute-start | bytes 147464 | tf_op jit(solution)/shard_map/ppermute | solution.py:324
  8.9 0.1 collective-permute-start
  9.0 0.0 copy-done.3
  9.0 6.0 %shard_map.82 = f32[1152,128]{1,0:T(8,128)} custom-call(bf16[2048,2048]{1,0:T(8,128)(2,1)S(1)} %copy-done.3, s32[16,128]{1,0:T(8,128)} %bitcast.6, s32[16,128]{1,0:T(8,128)} %bitcast.7, bf16[2048,128]{1,0:T(8,128)(2,1)} %weight_hbm.1), custom_call_target="tpu_custom_call" | custom-call | flops 10000000000 | bytes 10000000 | tf_op jit(solution)/shard_map/pallas_call | solution.py:134
  15.0 6.0 %all-to-all-start = ((f32[128,1,1152]{2,1,0:T(1,128)}), f32[128,1,1152]{2,1,0:T(1,128)S(1)}, u32[]{:S(2)}, u32[]{:S(2)}) async-start(f32[128,1,1152]{2,1,0:T(1,128)} %bitcast.5), calls=%async_computation | async-start | bytes 1179648 | tf_op jit(solution)/shard_map/all_to_all | solution.py:343
  21.0 0.0 collective-permute-done.1.b_ref
  21.0 0.0 collective-permute-done.a_ref
  21.0 3.8 %shard_map.84 = (f32[40,768]{1,0:T(8,128)S(1)}, bf16[768,768]{1,0:T(8,128)(2,1)S(1)}, bf16[768,768]{1,0:T(8,128)(2,1)S(1)}) custom-call(f32[16,768]{1,0:T(8,128)S(1)} %copy-done.4, f32[16,768]{1,0:T(8,128)S(1)} %collective-permute-done.a_ref, f32[16,768]{1,0:T(8,128)S(1)} %collective-permute-done.1.b_ref, f32[768,768]{1,0:T(8,128)} %self_ref.3, ...), custom_call_target="tpu_custom_call" | custom-call | flops 5000000000 | bytes 10000000 | tf_op jit(solution)/shard_map/pallas_call | solution.py:266
  24.8 7.3 %collective-permute-start.2 = (f32[40,768]{1,0:T(8,128)S(1)}, f32[40,768]{1,0:T(8,128)S(1)}, u32[]{:S(2)}, u32[]{:S(2)}) collective-permute-start(f32[40,768]{1,0:T(8,128)S(1)} %get-tuple-element.13.ready_ref), channel_id=1, source_target_pairs={{1,2},{2,1},{3,4},{4,3},{5,6},{6,5},{7,8},{8,7},{9,10},{10,9},{11,... | collective-permute-start | bytes 368648 | tf_op jit(solution)/shard_map/ppermute | solution.py:324
  32.1 3.3 %collective-permute-done.2.other_ref = f32[40,768]{1,0:T(8,128)S(1)} collective-permute-done((f32[40,768]{1,0:T(8,128)S(1)}, f32[40,768]{1,0:T(8,128)S(1)}, u32[]{:S(2)}, u32[]{:S(2)}) %collective-permute-start.2) | collective-permute-done | bytes 122912 | tf_op jit(solution)/shard_map/ppermute | solution.py:324
  35.4 0.0 all-to-all-done
  35.4 0.0 copy-start
  35.4 0.0 copy-start.1
  35.5 0.0 copy-start.2
  35.5 1.5 %shard_map.85 = (f32[16,768]{1,0:T(8,128)S(1)}, f32[16,768]{1,0:T(8,128)S(1)}, f32[16,768]{1,0:T(8,128)S(1)}) custom-call(f32[1152,128]{1,0:T(8,128)S(1)} %bitcast.4, f32[40,768]{1,0:T(8,128)S(1)} %get-tuple-element.13.ready_ref, f32[40,768]{1,0:T(8,128)S(1)} %collective-permute-done.2.other_ref), custom_call_target="tpu_custom_call" | custom-call | flops 10000000000 | bytes 1000000 | tf_op jit(solution)/shard_map/pallas_call | solution.py:209
  37.0 0.1 collective-permute-start.3
  37.0 1.2 %collective-permute-done.3.a_ref = f32[16,768]{1,0:T(8,128)S(1)} collective-permute-done((f32[16,768]{1,0:T(8,128)S(1)}, f32[16,768]{1,0:T(8,128)S(1)}, u32[]{:S(2)}, u32[]{:S(2)}) %collective-permute-start.3) | collective-permute-done | bytes 49184 | tf_op jit(solution)/shard_map/ppermute | solution.py:319
  38.3 0.0 copy-done
  38.3 0.0 copy-done.1
  38.3 0.3 copy-done.2
  38.5 1.0 %shard_map.86.part_ref = f32[16,768]{1,0:T(8,128)S(1)} custom-call(f32[16,768]{1,0:T(8,128)S(1)} %get-tuple-element.14.c_ref, f32[16,768]{1,0:T(8,128)S(1)} %collective-permute-done.3.a_ref, f32[768,768]{1,0:T(8,128)S(1)} %copy-done, f32[768,768]{1,0:T(8,128)S(1)} %copy-done.1, f32[768,768]{1,0:T(8,128)S(1)} %copy-done.2), custom_call_target="tpu_custom_call" | custom-call | flops 500000000 | bytes 1000000 | tf_op jit(solution)/shard_map/pallas_call | solution.py:291
  39.5 0.4 shard_map.87.c_ref
  39.9 0.0 collective-permute-start.4
  40.0 7.1 %collective-permute-start.5 = (f32[16,768]{1,0:T(8,128)S(1)}, f32[16,768]{1,0:T(8,128)S(1)}, u32[]{:S(2)}, u32[]{:S(2)}) collective-permute-start(f32[16,768]{1,0:T(8,128)S(1)} %shard_map.87.c_ref), channel_id=1, source_target_pairs={{1,2},{2,1},{3,4},{4,3},{5,6},{6,5},{7,8},{8,7},{9,10},{10,9},{11,... | collective-permute-start | bytes 147464 | tf_op jit(solution)/shard_map/ppermute | solution.py:324
  47.1 0.0 collective-permute-done.4.a_ref
  47.1 1.0 %shard_map.88.part_ref = f32[16,768]{1,0:T(8,128)S(1)} custom-call(f32[16,768]{1,0:T(8,128)S(1)} %shard_map.87.c_ref, f32[16,768]{1,0:T(8,128)S(1)} %collective-permute-done.4.a_ref, f32[768,768]{1,0:T(8,128)S(1)} %copy-done, f32[768,768]{1,0:T(8,128)S(1)} %copy-done.1, f32[768,768]{1,0:T(8,128)S(1)} %copy-done.2), custom_call_target="tpu_custom_call" | custom-call | flops 500000000 | bytes 1000000 | tf_op jit(solution)/shard_map/pallas_call | solution.py:291
  48.1 1.5 %collective-permute-done.5.b_ref = f32[16,768]{1,0:T(8,128)S(1)} collective-permute-done((f32[16,768]{1,0:T(8,128)S(1)}, f32[16,768]{1,0:T(8,128)S(1)}, u32[]{:S(2)}, u32[]{:S(2)}) %collective-permute-start.5) | collective-permute-done | bytes 49184 | tf_op jit(solution)/shard_map/ppermute | solution.py:324
  49.6 1.1 %shard_map.89 = f32[16,768]{1,0:T(8,128)} custom-call(f32[16,768]{1,0:T(8,128)S(1)} %shard_map.88.part_ref, f32[16,768]{1,0:T(8,128)S(1)} %collective-permute-done.5.b_ref, bf16[768,768]{1,0:T(8,128)(2,1)S(1)} %get-tuple-element.16.high_ref, bf16[768,768]{1,0:T(8,128)(2,1)S(1)} %get-tuple-element.17.low_ref, f32[16,768]{1,0:T(8,128)S(1)} %shard_map.87.c_ref, ...), custom_call_target="tpu_custom_call" | custom-call | flops 300000000 | bytes 1000000 | tf_op jit(solution)/shard_map/pallas_call | solution.py:307
Async XLA Ops:
  0.0 0.8 %copy-start.4 = (f32[16,768]{1,0:T(8,128)S(1)}, f32[16,768]{1,0:T(8,128)}, u32[]{:S(2)}) copy-start(f32[16,768]{1,0:T(8,128)} %c_hbm) | copy-start | bytes 147460
  0.0 9.0 %copy-start.3 = (bf16[2048,2048]{1,0:T(8,128)(2,1)S(1)}, bf16[2048,2048]{1,0:T(8,128)(2,1)}, u32[]{:S(2)}) copy-start(bf16[2048,2048]{1,0:T(8,128)(2,1)} %movie_ref.1) | copy-start | bytes 25165828
  0.8 20.2 %collective-permute-start.1 = (f32[16,768]{1,0:T(8,128)S(1)}, f32[16,768]{1,0:T(8,128)S(1)}, u32[]{:S(2)}, u32[]{:S(2)}) collective-permute-start(f32[16,768]{1,0:T(8,128)S(1)} %copy-done.4), channel_id=1, source_target_pairs={{1,2},{2,1},{3,4},{4,3},{5,6},{6,5},{7,8},{8,7},{9,10},{10,9},{11,... | collective-permute-start | bytes 147464 | tf_op jit(solution)/shard_map/ppermute | solution.py:324
  8.9 12.2 %collective-permute-start = (f32[16,768]{1,0:T(8,128)S(1)}, f32[16,768]{1,0:T(8,128)S(1)}, u32[]{:S(2)}, u32[]{:S(2)}) collective-permute-start(f32[16,768]{1,0:T(8,128)S(1)} %copy-done.4), channel_id=1, source_target_pairs={{0,1},{1,0},{2,3},{3,2},{4,5},{5,4},{6,7},{7,6},{8,9},{9,8},{10,11... | collective-permute-start | bytes 147464 | tf_op jit(solution)/shard_map/ppermute | solution.py:319
  15.0 20.5 %all-to-all-start = ((f32[128,1,1152]{2,1,0:T(1,128)}), f32[128,1,1152]{2,1,0:T(1,128)S(1)}, u32[]{:S(2)}, u32[]{:S(2)}) async-start(f32[128,1,1152]{2,1,0:T(1,128)} %bitcast.5), calls=%async_computation | async-start | bytes 1179648 | tf_op jit(solution)/shard_map/all_to_all | solution.py:343
  24.8 10.6 %collective-permute-start.2 = (f32[40,768]{1,0:T(8,128)S(1)}, f32[40,768]{1,0:T(8,128)S(1)}, u32[]{:S(2)}, u32[]{:S(2)}) collective-permute-start(f32[40,768]{1,0:T(8,128)S(1)} %get-tuple-element.13.ready_ref), channel_id=1, source_target_pairs={{1,2},{2,1},{3,4},{4,3},{5,6},{6,5},{7,8},{8,7},{9,10},{10,9},{11,... | collective-permute-start | bytes 368648 | tf_op jit(solution)/shard_map/ppermute | solution.py:324
  35.4 2.8 %copy-start = (f32[768,768]{1,0:T(8,128)S(1)}, f32[768,768]{1,0:T(8,128)}, u32[]{:S(2)}) copy-start(f32[768,768]{1,0:T(8,128)} %self_ref.3) | copy-start | bytes 7077892
  35.4 2.8 %copy-start.1 = (f32[768,768]{1,0:T(8,128)S(1)}, f32[768,768]{1,0:T(8,128)}, u32[]{:S(2)}) copy-start(f32[768,768]{1,0:T(8,128)} %prev_ref.3) | copy-start | bytes 7077892
  35.5 3.1 %copy-start.2 = (f32[768,768]{1,0:T(8,128)S(1)}, f32[768,768]{1,0:T(8,128)}, u32[]{:S(2)}) copy-start(f32[768,768]{1,0:T(8,128)} %next_ref.3) | copy-start | bytes 7077892
  37.0 1.3 %collective-permute-start.3 = (f32[16,768]{1,0:T(8,128)S(1)}, f32[16,768]{1,0:T(8,128)S(1)}, u32[]{:S(2)}, u32[]{:S(2)}) collective-permute-start(f32[16,768]{1,0:T(8,128)S(1)} %get-tuple-element.14.c_ref), channel_id=1, source_target_pairs={{0,1},{1,0},{2,3},{3,2},{4,5},{5,4},{6,7},{7,6},{8,9},{9,8},{10,11... | collective-permute-start | bytes 147464 | tf_op jit(solution)/shard_map/ppermute | solution.py:319
  39.9 7.2 %collective-permute-start.4 = (f32[16,768]{1,0:T(8,128)S(1)}, f32[16,768]{1,0:T(8,128)S(1)}, u32[]{:S(2)}, u32[]{:S(2)}) collective-permute-start(f32[16,768]{1,0:T(8,128)S(1)} %shard_map.87.c_ref), channel_id=1, source_target_pairs={{0,1},{1,0},{2,3},{3,2},{4,5},{5,4},{6,7},{7,6},{8,9},{9,8},{10,11... | collective-permute-start | bytes 147464 | tf_op jit(solution)/shard_map/ppermute | solution.py:319
  40.0 9.6 %collective-permute-start.5 = (f32[16,768]{1,0:T(8,128)S(1)}, f32[16,768]{1,0:T(8,128)S(1)}, u32[]{:S(2)}, u32[]{:S(2)}) collective-permute-start(f32[16,768]{1,0:T(8,128)S(1)} %shard_map.87.c_ref), channel_id=1, source_target_pairs={{1,2},{2,1},{3,4},{4,3},{5,6},{6,5},{7,8},{8,7},{9,10},{10,9},{11,... | collective-permute-start | bytes 147464 | tf_op jit(solution)/shard_map/ppermute | solution.py:324

commit v4 on v2

--- a/solution.py
+++ b/solution.py
@@ -1,3 +1,5 @@
+import functools
+
 import jax
 import jax.numpy as jnp
 from jax import lax
@@ -9,7 +11,7 @@
 AXES = ("planes", "rows")
 LANES = 128
 CAP = 32
-SLOT = 5
+SLOT = 9
 PREPARE_MB = 50
 PITCH = 9
 WIDE = 256
@@ -21,6 +23,10 @@
 
 def place():
     return lax.axis_index(AXES)
+
+
+def across(block):
+    return block + 2 * (block & 1) - 1
 
 
 def update(coupled, c, projected, diag):
@@ -43,6 +49,7 @@
     slab, left, fan, weight, tile, neuron, row, row_s, neuron_s, sem2,
 ):
     group = 16 * PITCH
+    devices = out_ref.shape[0] // SLOT
     small = [
         pltpu.make_async_copy(source, target, sem2.at[i])
         for i, (source, target) in enumerate(
@@ -100,8 +107,12 @@
             names = swap_blocks(jnp.broadcast_to(names, (16, LANES)))
             for g in range(4):
                 owner = lax.div(neuron_s[2 * b + h, g * CAP], 768)
-                out_ref[pl.ds(owner * SLOT, 4), :] = slots[4 * g : 4 * g + 4]
-                out_ref[pl.ds(owner * SLOT + 4, 1), :] = names[4 * g : 4 * g + 1]
+                other = across(owner)
+                other = jnp.where((other < 0) | (other >= devices), owner, other)
+                for to, half in ((owner, 0), (other, 1)):
+                    out_ref[pl.ds(to * SLOT + 4 * half, 4), :] = slots[4 * g : 4 * g + 4]
+                    at = pl.ds(half * 64, 64)
+                    out_ref[pl.ds(to * SLOT + 8, 1), at] = names[4 * g : 4 * g + 1, half * 64 : half * 64 + 64]
 
 
 def open_kernel(out_ref):
@@ -144,27 +155,27 @@
     )(movie, entry_tile.reshape(table), entry_neuron.reshape(table), entry_weights)
 
 
-def combine_kernel(got_ref, ready_ref, out_ref, first_ref):
+def gathered(half, block, got_ref, out_ref):
     sources = got_ref.shape[0] // SLOT
-    first = (place() * 768).astype(jnp.float32)
-    lane4 = lax.broadcasted_iota(jnp.int32, (1, LANES), 1) // CAP
+    lane = lax.broadcasted_iota(jnp.int32, (1, LANES), 1)
     sub = lax.broadcasted_iota(jnp.int32, (256, LANES), 0).astype(jnp.float32)
     sums = jnp.zeros((96, 256), jnp.float32)
     for b in range(sources // 8):
         lefts, hots = [], []
         for i in range(2):
             row = (2 * b + i) * 4 * SLOT
-            x = jnp.concatenate([got_ref[row + s * SLOT : row + s * SLOT + 4, :] for s in range(4)], axis=0)
+            r0, r1, r2, r3 = (got_ref[row + s * SLOT + 8 : row + s * SLOT + 9, :] for s in range(4))
+            pairs = [jnp.where(lane % 64 < 32, r0, r1), jnp.where(lane % 64 < 32, r2, r3)]
+            pairs[1 - half] = pltpu.roll(pairs[1 - half], 64, 1)
+            name = jnp.where(lane < 64, *pairs) - (block * 768).astype(jnp.float32)
+            x = jnp.concatenate(
+                [got_ref[row + s * SLOT + 4 * half : row + s * SLOT + 4 * half + 4, :] for s in range(4)], axis=0
+            )
             x = swap_blocks(x)
-            name = got_ref[row + 4 : row + 5, :]
-            for s in range(1, 4):
-                name = jnp.where(lane4 == s, got_ref[row + s * SLOT + 4 : row + s * SLOT + 5, :], name)
-            name = name - first
             high = jnp.where(name >= 512.0, 2.0, jnp.where(name >= 256.0, 1.0, 0.0))
             low = name - 256.0 * high
             big = x.astype(jnp.bfloat16).astype(jnp.float32)
-            rest = x - big
-            both = jnp.concatenate([big, rest], axis=0)
+            both = jnp.concatenate([big, x - big], axis=0)
             lefts.append(
                 jnp.concatenate([jnp.where(high == float(h), both, 0.0) for h in range(3)], axis=0).astype(jnp.bfloat16)
             )
@@ -175,19 +186,27 @@
         )
     for h in range(3):
         out_ref[:, h * 256 : h * 256 + 256] = sums[h * 32 : h * 32 + 16] + sums[h * 32 + 16 : h * 32 + 32]
+
+
+def first_kernel(got_ref, ready_ref, out_ref, first_ref):
+    gathered(0, place(), got_ref, out_ref)
     first_ref[...] = update(ready_ref[0:16, :], ready_ref[16:32, :], out_ref[...], ready_ref[32:33, :])
 
 
-def combine(got, ready):
-    out = jax.ShapeDtypeStruct((16, ready.shape[1]), jnp.float32)
-    return pl.pallas_call(
-        combine_kernel,
-        out_shape=(out, out),
+def beyond_kernel(got_ref, own_ref, out_ref):
+    gathered(1, across(place()), got_ref, out_ref)
+
+
+def combine(kernel, got, other, outs):
+    out = jax.ShapeDtypeStruct((16, other.shape[1]), jnp.float32)
+    return pl.pallas_call(
+        kernel,
+        out_shape=(out,) * outs,
         in_specs=[VMEM] * 2,
-        out_specs=(VMEM, VMEM),
+        out_specs=(VMEM,) * outs,
         compiler_params=pltpu.CompilerParams(vmem_limit_bytes=16 << 20),
-        cost_estimate=pl.CostEstimate(flops=10**10, bytes_accessed=10**6, transcendentals=0),
-    )(got, ready)
+        cost_estimate=pl.CostEstimate(flops=10**10 if outs > 1 else 10**8, bytes_accessed=10**6, transcendentals=0),
+    )(got, other)
 
 
 def halves(x):
@@ -246,7 +265,7 @@
         + [pltpu.VMEM((n, n), jnp.float32)] * 3
         + [pltpu.SemaphoreType.DMA((4,))],
         compiler_params=pltpu.CompilerParams(vmem_limit_bytes=PREPARE_MB << 20),
-        cost_estimate=pl.CostEstimate(flops=5 * 10**9, bytes_accessed=10**7, transcendentals=0),
+        cost_estimate=pl.CostEstimate(flops=2 * 10**10, bytes_accessed=10**7, transcendentals=0),
     )(c, a, b, *matrices)
 
 
@@ -277,22 +296,36 @@
     out_ref[...] = update(part_ref[...] + far, c_ref[...], projected_ref[...], ready_ref[32:33, :])
 
 
-def step(part, b, weights, c, projected, ready):
-    return pl.pallas_call(
-        step_kernel,
-        out_shape=jax.ShapeDtypeStruct(c.shape, jnp.float32),
-        in_specs=[VMEM] * 7,
+def second_step_kernel(
+    last, part_ref, other_ref, beyond_ref, high_ref, low_ref, c_ref, projected_ref, ready_ref, out_ref
+):
+    block = across(place())
+    b = update(other_ref[0:16, :], other_ref[16:32, :], beyond_ref[...], other_ref[32:33, :])
+    row = lax.broadcasted_iota(jnp.int32, b.shape, 0)
+    b = jnp.where(row < jnp.where((block < 0) | (block > last), 0, 16), b, 0.0)
+    far = times(b, high_ref[...], low_ref[...])
+    out_ref[...] = update(part_ref[...] + far, c_ref[...], projected_ref[...], ready_ref[32:33, :])
+
+
+def step(kernel, *operands):
+    return pl.pallas_call(
+        kernel,
+        out_shape=jax.ShapeDtypeStruct(operands[0].shape, jnp.float32),
+        in_specs=[VMEM] * len(operands),
         out_specs=VMEM,
         compiler_params=pltpu.CompilerParams(vmem_limit_bytes=16 << 20),
         cost_estimate=pl.CostEstimate(flops=3 * 10**8, bytes_accessed=10**6, transcendentals=0),
-    )(part, b, *weights, c, projected, ready)
-
-
-def exchange(c):
+    )(*operands)
+
+
+def swap_in_chip(c):
     n = lax.axis_size(AXES)
-    a = lax.ppermute(c, AXES, [(i, i ^ 1) for i in range(n)])
-    b = lax.ppermute(c, AXES, [(i, i + 1) for i in range(1, n - 1, 2)] + [(i + 1, i) for i in range(1, n - 1, 2)])
-    return a, b
+    return lax.ppermute(c, AXES, [(i, i ^ 1) for i in range(n)])
+
+
+def swap_across(c):
+    n = lax.axis_size(AXES)
+    return lax.ppermute(c, AXES, [(i, across(i)) for i in range(1, n - 1)])
 
 
 def local(
@@ -308,16 +341,23 @@
     devices = lax.axis_size(AXES)
     matrices = (intersection_self, intersection_prev, intersection_next)
     c, _ = lax.optimization_barrier((prev_traces, opening()))
-    a, b = exchange(c)
+    a, b = swap_in_chip(c), swap_across(c)
     here = pltpu.with_memory_space_constraint(movie, pltpu.VMEM)
     send = contributions(here, entry_tile, entry_neuron, entry_weights, devices)
     got = lax.all_to_all(send.reshape(devices, 1, SLOT * LANES), AXES, 0, 0)
     ready, *split = prepare(c, a, b, matrices)
-    projected, c = combine(got.reshape(devices * SLOT, LANES), ready)
-    for _ in range(SWEEPS - 1):
-        a, b = exchange(c)
+    other = swap_across(ready)
+    got = got.reshape(devices * SLOT, LANES)
+    projected, c = combine(first_kernel, got, ready, 2)
+    a = swap_in_chip(c)
+    beyond, = combine(beyond_kernel, got, projected, 1)
+    part = near(c, a, matrices)
+    second_step = functools.partial(second_step_kernel, devices - 1)
+    c = step(second_step, part, other, beyond, *split, c, projected, ready)
+    for _ in range(SWEEPS - 2):
+        a, b = swap_in_chip(c), swap_across(c)
         part = near(c, a, matrices)
-        c = step(part, b, split, c, projected, ready)
+        c = step(step_kernel, part, b, *split, c, projected, ready)
     return c
 
 

time: 54.2 us -> 50.5 us (0.932)
  waiting for transfers between devices: 17.4 us -> 8.28 us
  starting transfers between devices: 21.7 us -> 25.2 us
  Pallas kernels: 14.4 us -> 15.5 us
  local copies, waits for them, and re-layouts: 0.22 us -> 1.12 us
    ppermute x6, waiting for transfers between devices: 10.1 us -> 5.41 us  [the longest x3 5.05 us: swap_across(): return lax.ppermute(c, AXES, [(i, across(i)) for i in range(1, n - 1)])]
    all_to_all x1, waiting for transfers between devices: 7.28 us -> 2.87 us  [local(): got = lax.all_to_all(send.reshape(devices, 1, SLOT * LANES), AXES, 0, 0)]
    ppermute x6, starting transfers between devices: 15.7 us -> 19.2 us  [the longest x3 19 us: swap_across(): return lax.ppermute(c, AXES, [(i, across(i)) for i in range(1, n - 1)])]
    pallas_call x3 -> x4, Pallas kernels: 2.33 us -> 3.24 us  [the longest x2 1.72 us: combine(): pl.pallas_call(kernel, out_shape=(out,) * outs, in_specs=[VMEM] * 2, out_...]
    unnamed x10, local copies, waits for them, and re-layouts: 0.22 us -> 1.12 us
  transfers between devices with their start and end apart: 7 -> 7, of which waited for: 3 -> 3; matrix products, arithmetic and copies ran while one was open for 0% -> 0% of each run, Pallas kernels for 21% -> 27%
where the time goes in v4:
time: 50.5 us; the launch traced here: 50.3 us
  starting transfers between devices  25.2 us (50%)
  Pallas kernels  15.5 us (31%)
  waiting for transfers between devices  8.28 us (16%)
  local copies, waits for them, and re-layouts  1.12 us (2%)
    ppermute x3, starting transfers between devices, swap_across(): return lax.ppermute(c, AXES, [(i, across(i)) for i in range(1, n - 1)])  19 us
    all_to_all x1, starting transfers between devices, local(): got = lax.all_to_all(send.reshape(devices, 1, SLOT * LANES), AXES, 0, 0)  6.02 us
    pallas_call x1, Pallas kernels, contributions(): pl.pallas_call(contrib_kernel, out_shape=jax.ShapeDtypeStruct((devices *...  6 us
    ppermute x3, waiting for transfers between devices, swap_across(): return lax.ppermute(c, AXES, [(i, across(i)) for i in range(1, n - 1)])  5.05 us
    pallas_call x1, Pallas kernels, prepare(): pl.pallas_call(prepare_kernel, out_shape=(jax.ShapeDtypeStruct((40, n), j...  3.78 us
    all_to_all x1, waiting for transfers between devices, local(): got = lax.all_to_all(send.reshape(devices, 1, SLOT * LANES), AXES, 0, 0)  2.87 us
    pallas_call x2, Pallas kernels, near(): pl.pallas_call(near_kernel, out_shape=jax.ShapeDtypeStruct(c.shape, jnp.f...  1.9 us
    pallas_call x2, Pallas kernels, combine(): pl.pallas_call(kernel, out_shape=(out,) * outs, in_specs=[VMEM] * 2, out_...  1.72 us
  transfers between devices with their start and end apart: 7, of which 3 were waited for; matrix products, arithmetic and copies ran while one was open for 0% of the time, Pallas kernels for 27%

profile of v4, /device:TPU:2, one launch (start us, length us, event | category | flops | bytes accessed | tf_op | source)
XLA Modules:
  0.0 50.3 jit_solution(11316542978629931210)
XLA Ops:
  0.0 0.0 copy-start.4
  0.0 0.0 copy-start.3
  0.0 0.6 %shard_map.83 = f32[8,128]{1,0:T(8,128)} custom-call(), custom_call_target="tpu_custom_call" | custom-call | flops 10000000000 | bytes 10000000 | tf_op jit(solution)/shard_map/pallas_call | solution.py:123
  0.6 0.2 copy-done.4
  0.8 8.1 %collective-permute-start.1 = (f32[16,768]{1,0:T(8,128)S(1)}, f32[16,768]{1,0:T(8,128)S(1)}, u32[]{:S(2)}, u32[]{:S(2)}) collective-permute-start(f32[16,768]{1,0:T(8,128)S(1)} %copy-done.4), channel_id=1, source_target_pairs={{1,2},{2,1},{3,4},{4,3},{5,6},{6,5},{7,8},{8,7},{9,10},{10,9},{11,... | collective-permute-start | bytes 147464 | tf_op jit(solution)/shard_map/ppermute | solution.py:328
  8.9 0.1 collective-permute-start
  9.0 0.0 copy-done.3
  9.0 6.0 %shard_map.82 = f32[1152,128]{1,0:T(8,128)} custom-call(bf16[2048,2048]{1,0:T(8,128)(2,1)S(1)} %copy-done.3, s32[16,128]{1,0:T(8,128)} %bitcast.7, s32[16,128]{1,0:T(8,128)} %bitcast.8, bf16[2048,128]{1,0:T(8,128)(2,1)} %weight_hbm.1), custom_call_target="tpu_custom_call" | custom-call | flops 10000000000 | bytes 10000000 | tf_op jit(solution)/shard_map/pallas_call | solution.py:136
  15.0 6.0 %all-to-all-start = ((f32[128,1,1152]{2,1,0:T(1,128)}), f32[128,1,1152]{2,1,0:T(1,128)S(1)}, u32[]{:S(2)}, u32[]{:S(2)}) async-start(f32[128,1,1152]{2,1,0:T(1,128)} %bitcast.6), calls=%async_computation | async-start | bytes 1179648 | tf_op jit(solution)/shard_map/all_to_all | solution.py:347
  21.0 0.0 collective-permute-done.1.b_ref
  21.0 0.0 collective-permute-done.a_ref
  21.0 3.8 %shard_map.84 = (f32[40,768]{1,0:T(8,128)S(1)}, bf16[768,768]{1,0:T(8,128)(2,1)S(1)}, bf16[768,768]{1,0:T(8,128)(2,1)S(1)}) custom-call(f32[16,768]{1,0:T(8,128)S(1)} %copy-done.4, f32[16,768]{1,0:T(8,128)S(1)} %collective-permute-done.a_ref, f32[16,768]{1,0:T(8,128)S(1)} %collective-permute-done.1.b_ref, f32[768,768]{1,0:T(8,128)} %self_ref.3, ...), custom_call_target="tpu_custom_call" | custom-call | flops 20000000000 | bytes 10000000 | tf_op jit(solution)/shard_map/pallas_call | solution.py:259
  24.8 7.3 %collective-permute-start.3 = (f32[40,768]{1,0:T(8,128)S(1)}, f32[40,768]{1,0:T(8,128)S(1)}, u32[]{:S(2)}, u32[]{:S(2)}) collective-permute-start(f32[40,768]{1,0:T(8,128)S(1)} %get-tuple-element.12.ready_ref), channel_id=1, source_target_pairs={{1,2},{2,1},{3,4},{4,3},{5,6},{6,5},{7,8},{8,7},{9,10},{10,9},{11,... | collective-permute-start | bytes 368648 | tf_op jit(solution)/shard_map/ppermute | solution.py:328
  32.1 2.9 %all-to-all-done = f32[128,1,1152]{2,1,0:T(1,128)S(1)} async-done(((f32[128,1,1152]{2,1,0:T(1,128)}), f32[128,1,1152]{2,1,0:T(1,128)S(1)}, u32[]{:S(2)}, u32[]{:S(2)}) %all-to-all-start) | async-done | bytes 589856 | tf_op jit(solution)/shard_map/all_to_all | solution.py:347
  35.0 0.0 copy-start
  35.0 0.0 copy-start.1
  35.0 0.0 copy-start.2
  35.0 0.9 %shard_map.85 = (f32[16,768]{1,0:T(8,128)S(1)}, f32[16,768]{1,0:T(8,128)S(1)}) custom-call(f32[1152,128]{1,0:T(8,128)S(1)} %bitcast.4, f32[40,768]{1,0:T(8,128)S(1)} %get-tuple-element.12.ready_ref), custom_call_target="tpu_custom_call" | custom-call | flops 10000000000 | bytes 1000000 | tf_op jit(solution)/shard_map/pallas_call | solution.py:202
  35.9 0.1 collective-permute-start.2
  36.0 0.8 %shard_map.87.beyond_ref = f32[16,768]{1,0:T(8,128)S(1)} custom-call(f32[1152,128]{1,0:T(8,128)S(1)} %bitcast.5, f32[16,768]{1,0:T(8,128)S(1)} %get-tuple-element.14.own_ref.projected_ref), custom_call_target="tpu_custom_call" | custom-call | flops 100000000 | bytes 1000000 | tf_op jit(solution)/shard_map/pallas_call | solution.py:202
  36.8 0.4 collective-permute-done.2.a_ref
  37.2 0.0 copy-done
  37.2 0.2 copy-done.1
  37.4 0.7 %copy-done.2 = f32[768,768]{1,0:T(8,128)S(1)} copy-done((f32[768,768]{1,0:T(8,128)S(1)}, f32[768,768]{1,0:T(8,128)}, u32[]{:S(2)}) %copy-start.2) | copy-done | bytes 2359320
  38.1 0.9 %shard_map.86.part_ref = f32[16,768]{1,0:T(8,128)S(1)} custom-call(f32[16,768]{1,0:T(8,128)S(1)} %get-tuple-element.13.c_ref, f32[16,768]{1,0:T(8,128)S(1)} %collective-permute-done.2.a_ref, f32[768,768]{1,0:T(8,128)S(1)} %copy-done, f32[768,768]{1,0:T(8,128)S(1)} %copy-done.1, f32[768,768]{1,0:T(8,128)S(1)} %copy-done.2), custom_call_target="tpu_custom_call" | custom-call | flops 500000000 | bytes 1000000 | tf_op jit(solution)/shard_map/pallas_call | solution.py:284
  39.1 0.0 collective-permute-done.3.other_ref
  39.1 0.5 shard_map.88.c_ref
  39.5 0.0 collective-permute-start.4
  39.6 3.6 %collective-permute-start.5 = (f32[16,768]{1,0:T(8,128)S(1)}, f32[16,768]{1,0:T(8,128)S(1)}, u32[]{:S(2)}, u32[]{:S(2)}) collective-permute-start(f32[16,768]{1,0:T(8,128)S(1)} %shard_map.88.c_ref), channel_id=1, source_target_pairs={{1,2},{2,1},{3,4},{4,3},{5,6},{6,5},{7,8},{8,7},{9,10},{10,9},{11,... | collective-permute-start | bytes 147464 | tf_op jit(solution)/shard_map/ppermute | solution.py:328
  43.2 0.0 collective-permute-done.4.a_ref
  43.2 1.0 %shard_map.89.part_ref = f32[16,768]{1,0:T(8,128)S(1)} custom-call(f32[16,768]{1,0:T(8,128)S(1)} %shard_map.88.c_ref, f32[16,768]{1,0:T(8,128)S(1)} %collective-permute-done.4.a_ref, f32[768,768]{1,0:T(8,128)S(1)} %copy-done, f32[768,768]{1,0:T(8,128)S(1)} %copy-done.1, f32[768,768]{1,0:T(8,128)S(1)} %copy-done.2), custom_call_target="tpu_custom_call" | custom-call | flops 500000000 | bytes 1000000 | tf_op jit(solution)/shard_map/pallas_call | solution.py:284
  44.1 5.0 %collective-permute-done.5.b_ref = f32[16,768]{1,0:T(8,128)S(1)} collective-permute-done((f32[16,768]{1,0:T(8,128)S(1)}, f32[16,768]{1,0:T(8,128)S(1)}, u32[]{:S(2)}, u32[]{:S(2)}) %collective-permute-start.5) | collective-permute-done | bytes 49184 | tf_op jit(solution)/shard_map/ppermute | solution.py:328
  49.2 1.1 %shard_map.90 = f32[16,768]{1,0:T(8,128)} custom-call(f32[16,768]{1,0:T(8,128)S(1)} %shard_map.89.part_ref, f32[16,768]{1,0:T(8,128)S(1)} %collective-permute-done.5.b_ref, bf16[768,768]{1,0:T(8,128)(2,1)S(1)} %get-tuple-element.15.high_ref, bf16[768,768]{1,0:T(8,128)(2,1)S(1)} %get-tuple-element.16.low_ref, f32[16,768]{1,0:T(8,128)S(1)} %shard_map.88.c_ref, ...), custom_call_target="tpu_custom_call" | custom-call | flops 300000000 | bytes 1000000 | tf_op jit(solution)/shard_map/pallas_call | solution.py:311
Async XLA Ops:
  0.0 0.8 %copy-start.4 = (f32[16,768]{1,0:T(8,128)S(1)}, f32[16,768]{1,0:T(8,128)}, u32[]{:S(2)}) copy-start(f32[16,768]{1,0:T(8,128)} %c_hbm) | copy-start | bytes 147460
  0.0 9.0 %copy-start.3 = (bf16[2048,2048]{1,0:T(8,128)(2,1)S(1)}, bf16[2048,2048]{1,0:T(8,128)(2,1)}, u32[]{:S(2)}) copy-start(bf16[2048,2048]{1,0:T(8,128)(2,1)} %movie_ref.1) | copy-start | bytes 25165828
  0.8 20.2 %collective-permute-start.1 = (f32[16,768]{1,0:T(8,128)S(1)}, f32[16,768]{1,0:T(8,128)S(1)}, u32[]{:S(2)}, u32[]{:S(2)}) collective-permute-start(f32[16,768]{1,0:T(8,128)S(1)} %copy-done.4), channel_id=1, source_target_pairs={{1,2},{2,1},{3,4},{4,3},{5,6},{6,5},{7,8},{8,7},{9,10},{10,9},{11,... | collective-permute-start | bytes 147464 | tf_op jit(solution)/shard_map/ppermute | solution.py:328
  8.9 12.2 %collective-permute-start = (f32[16,768]{1,0:T(8,128)S(1)}, f32[16,768]{1,0:T(8,128)S(1)}, u32[]{:S(2)}, u32[]{:S(2)}) collective-permute-start(f32[16,768]{1,0:T(8,128)S(1)} %copy-done.4), channel_id=1, source_target_pairs={{0,1},{1,0},{2,3},{3,2},{4,5},{5,4},{6,7},{7,6},{8,9},{9,8},{10,11... | collective-permute-start | bytes 147464 | tf_op jit(solution)/shard_map/ppermute | solution.py:323
  15.0 20.0 %all-to-all-start = ((f32[128,1,1152]{2,1,0:T(1,128)}), f32[128,1,1152]{2,1,0:T(1,128)S(1)}, u32[]{:S(2)}, u32[]{:S(2)}) async-start(f32[128,1,1152]{2,1,0:T(1,128)} %bitcast.6), calls=%async_computation | async-start | bytes 1179648 | tf_op jit(solution)/shard_map/all_to_all | solution.py:347
  24.8 14.2 %collective-permute-start.3 = (f32[40,768]{1,0:T(8,128)S(1)}, f32[40,768]{1,0:T(8,128)S(1)}, u32[]{:S(2)}, u32[]{:S(2)}) collective-permute-start(f32[40,768]{1,0:T(8,128)S(1)} %get-tuple-element.12.ready_ref), channel_id=1, source_target_pairs={{1,2},{2,1},{3,4},{4,3},{5,6},{6,5},{7,8},{8,7},{9,10},{10,9},{11,... | collective-permute-start | bytes 368648 | tf_op jit(solution)/shard_map/ppermute | solution.py:328
  35.0 2.2 %copy-start = (f32[768,768]{1,0:T(8,128)S(1)}, f32[768,768]{1,0:T(8,128)}, u32[]{:S(2)}) copy-start(f32[768,768]{1,0:T(8,128)} %self_ref.3) | copy-start | bytes 7077892
  35.0 2.4 %copy-start.1 = (f32[768,768]{1,0:T(8,128)S(1)}, f32[768,768]{1,0:T(8,128)}, u32[]{:S(2)}) copy-start(f32[768,768]{1,0:T(8,128)} %prev_ref.3) | copy-start | bytes 7077892
  35.0 3.1 %copy-start.2 = (f32[768,768]{1,0:T(8,128)S(1)}, f32[768,768]{1,0:T(8,128)}, u32[]{:S(2)}) copy-start(f32[768,768]{1,0:T(8,128)} %next_ref.3) | copy-start | bytes 7077892
  35.9 1.3 %collective-permute-start.2 = (f32[16,768]{1,0:T(8,128)S(1)}, f32[16,768]{1,0:T(8,128)S(1)}, u32[]{:S(2)}, u32[]{:S(2)}) collective-permute-start(f32[16,768]{1,0:T(8,128)S(1)} %get-tuple-element.13.c_ref), channel_id=1, source_target_pairs={{0,1},{1,0},{2,3},{3,2},{4,5},{5,4},{6,7},{7,6},{8,9},{9,8},{10,11... | collective-permute-start | bytes 147464 | tf_op jit(solution)/shard_map/ppermute | solution.py:323
  39.5 3.7 %collective-permute-start.4 = (f32[16,768]{1,0:T(8,128)S(1)}, f32[16,768]{1,0:T(8,128)S(1)}, u32[]{:S(2)}, u32[]{:S(2)}) collective-permute-start(f32[16,768]{1,0:T(8,128)S(1)} %shard_map.88.c_ref), channel_id=1, source_target_pairs={{0,1},{1,0},{2,3},{3,2},{4,5},{5,4},{6,7},{7,6},{8,9},{9,8},{10,11... | collective-permute-start | bytes 147464 | tf_op jit(solution)/shard_map/ppermute | solution.py:323
  39.6 9.6 %collective-permute-start.5 = (f32[16,768]{1,0:T(8,128)S(1)}, f32[16,768]{1,0:T(8,128)S(1)}, u32[]{:S(2)}, u32[]{:S(2)}) collective-permute-start(f32[16,768]{1,0:T(8,128)S(1)} %shard_map.88.c_ref), channel_id=1, source_target_pairs={{1,2},{2,1},{3,4},{4,3},{5,6},{6,5},{7,8},{8,7},{9,10},{10,9},{11,... | collective-permute-start | bytes 147464 | tf_op jit(solution)/shard_map/ppermute | solution.py:328

commit v5 on v4

--- a/solution.py
+++ b/solution.py
@@ -222,7 +222,7 @@
 
 
 def prepare_kernel(
-    c_hbm, a_ref, b_ref, self_hbm, prev_hbm, next_hbm, out_ref, high_ref, low_ref, c, own, close, far, sem
+    c_hbm, a_ref, b_ref, self_hbm, prev_hbm, next_hbm, out_ref, high_ref, low_ref, near_hbm, c, own, close, far, sem
 ):
     even = place() % 2 == 0
 
@@ -247,10 +247,13 @@
     out_ref[16:32, :] = c[...]
     total = times(c[...], *halves(own[...]))
     fetch(next_hbm, close, 2).wait()
+    keep = fetch(close, near_hbm, 4)
+    keep.start()
     total = total + times(a_ref[...], *halves(close[...]))
     fetch(prev_hbm, far, 3).wait()
     high_ref[...], low_ref[...] = halves(far[...])
     out_ref[0:16, :] = total + times(b_ref[...], high_ref[...], low_ref[...])
+    keep.wait()
 
 
 def prepare(c, a, b, matrices):
@@ -258,37 +261,30 @@
     half = jax.ShapeDtypeStruct((n, n), jnp.bfloat16)
     return pl.pallas_call(
         prepare_kernel,
-        out_shape=(jax.ShapeDtypeStruct((40, n), jnp.float32), half, half),
+        out_shape=(jax.ShapeDtypeStruct((40, n), jnp.float32), half, half, jax.ShapeDtypeStruct((n, n), jnp.float32)),
         in_specs=[HBM, VMEM, VMEM, HBM, HBM, HBM],
-        out_specs=(VMEM,) * 3,
+        out_specs=(VMEM,) * 3 + (HBM,),
         scratch_shapes=[pltpu.VMEM(c.shape, jnp.float32)]
         + [pltpu.VMEM((n, n), jnp.float32)] * 3
-        + [pltpu.SemaphoreType.DMA((4,))],
+        + [pltpu.SemaphoreType.DMA((5,))],
         compiler_params=pltpu.CompilerParams(vmem_limit_bytes=PREPARE_MB << 20),
         cost_estimate=pl.CostEstimate(flops=2 * 10**10, bytes_accessed=10**7, transcendentals=0),
     )(c, a, b, *matrices)
 
 
-def near_kernel(c_ref, a_ref, self_ref, prev_ref, next_ref, out_ref):
-    own = times(c_ref[...], *halves(self_ref[...]))
-
-    def rest(near_ref):
-        out_ref[...] = own + times(a_ref[...], *halves(near_ref[...]))
-
-    even = place() % 2 == 0
-    pl.when(even)(lambda: rest(next_ref))
-    pl.when(jnp.logical_not(even))(lambda: rest(prev_ref))
-
-
-def near(c, a, matrices):
+def near_kernel(c_ref, a_ref, self_ref, close_ref, out_ref):
+    out_ref[...] = times(c_ref[...], *halves(self_ref[...])) + times(a_ref[...], *halves(close_ref[...]))
+
+
+def near(c, a, own, close):
     return pl.pallas_call(
         near_kernel,
         out_shape=jax.ShapeDtypeStruct(c.shape, jnp.float32),
-        in_specs=[VMEM] * 5,
+        in_specs=[VMEM] * 4,
         out_specs=VMEM,
         compiler_params=pltpu.CompilerParams(vmem_limit_bytes=16 << 20),
         cost_estimate=pl.CostEstimate(flops=5 * 10**8, bytes_accessed=10**6, transcendentals=0),
-    )(c, a, *matrices)
+    )(c, a, own, close)
 
 
 def step_kernel(part_ref, b_ref, high_ref, low_ref, c_ref, projected_ref, ready_ref, out_ref):
@@ -345,18 +341,18 @@
     here = pltpu.with_memory_space_constraint(movie, pltpu.VMEM)
     send = contributions(here, entry_tile, entry_neuron, entry_weights, devices)
     got = lax.all_to_all(send.reshape(devices, 1, SLOT * LANES), AXES, 0, 0)
-    ready, *split = prepare(c, a, b, matrices)
+    ready, *split, close = prepare(c, a, b, matrices)
     other = swap_across(ready)
     got = got.reshape(devices * SLOT, LANES)
     projected, c = combine(first_kernel, got, ready, 2)
     a = swap_in_chip(c)
     beyond, = combine(beyond_kernel, got, projected, 1)
-    part = near(c, a, matrices)
+    part = near(c, a, intersection_self, close)
     second_step = functools.partial(second_step_kernel, devices - 1)
     c = step(second_step, part, other, beyond, *split, c, projected, ready)
     for _ in range(SWEEPS - 2):
         a, b = swap_in_chip(c), swap_across(c)
-        part = near(c, a, matrices)
+        part = near(c, a, intersection_self, close)
         c = step(step_kernel, part, b, *split, c, projected, ready)
     return c
 

time: 50.5 us -> 49.7 us (0.984)
  starting transfers between devices: 25.2 us -> 26.1 us
  waiting for transfers between devices: 8.28 us -> 7.43 us
  local copies, waits for them, and re-layouts: 1.12 us -> 0.4 us
    ppermute x3, starting transfers between devices: 19 us -> 19.8 us  [swap_across(): return lax.ppermute(c, AXES, [(i, across(i)) for i in range(1, n - 1)])]
    ppermute x3, waiting for transfers between devices: 5.05 us -> 4.33 us  [swap_across(): return lax.ppermute(c, AXES, [(i, across(i)) for i in range(1, n - 1)])]
    unnamed x10 -> x8, local copies, waits for them, and re-layouts: 1.12 us -> 0.4 us
where the time goes in v5:
time: 49.7 us; the launch traced here: 49.4 us
  starting transfers between devices  26.1 us (53%)
  Pallas kernels  15.4 us (31%)
  waiting for transfers between devices  7.43 us (15%)
    ppermute x3, starting transfers between devices, swap_across(): return lax.ppermute(c, AXES, [(i, across(i)) for i in range(1, n - 1)])  19.8 us
    pallas_call x1, Pallas kernels, contributions(): pl.pallas_call(contrib_kernel, out_shape=jax.ShapeDtypeStruct((devices *...  6.01 us
    all_to_all x1, starting transfers between devices, local(): got = lax.all_to_all(send.reshape(devices, 1, SLOT * LANES), AXES, 0, 0)  6.01 us
    ppermute x3, waiting for transfers between devices, swap_across(): return lax.ppermute(c, AXES, [(i, across(i)) for i in range(1, n - 1)])  4.33 us
    pallas_call x1, Pallas kernels, prepare(): pl.pallas_call(prepare_kernel, out_shape=(jax.ShapeDtypeStruct((40, n), j...  3.91 us
    all_to_all x1, waiting for transfers between devices, local(): got = lax.all_to_all(send.reshape(devices, 1, SLOT * LANES), AXES, 0, 0)  2.74 us
    pallas_call x2, Pallas kernels, combine(): pl.pallas_call(kernel, out_shape=(out,) * outs, in_specs=[VMEM] * 2, out_...  1.71 us
    pallas_call x2, Pallas kernels, near(): pl.pallas_call(near_kernel, out_shape=jax.ShapeDtypeStruct(c.shape, jnp.f...  1.6 us
  transfers between devices with their start and end apart: 7, of which 3 were waited for; matrix products, arithmetic and copies ran while one was open for 0% of the time, Pallas kernels for 27%

profile of v5, /device:TPU:2, one launch (start us, length us, event | category | flops | bytes accessed | tf_op | source)
XLA Modules:
  0.0 49.4 jit_solution(15179539511957275442)
XLA Ops:
  0.0 0.0 copy-start.3
  0.0 0.0 copy-start.2
  0.0 0.6 %shard_map.83 = f32[8,128]{1,0:T(8,128)} custom-call(), custom_call_target="tpu_custom_call" | custom-call | flops 10000000000 | bytes 10000000 | tf_op jit(solution)/shard_map/pallas_call | solution.py:123
  0.6 0.2 copy-done.3
  0.8 8.1 %collective-permute-start.1 = (f32[16,768]{1,0:T(8,128)S(1)}, f32[16,768]{1,0:T(8,128)S(1)}, u32[]{:S(2)}, u32[]{:S(2)}) collective-permute-start(f32[16,768]{1,0:T(8,128)S(1)} %copy-done.3), channel_id=1, source_target_pairs={{1,2},{2,1},{3,4},{4,3},{5,6},{6,5},{7,8},{8,7},{9,10},{10,9},{11,... | collective-permute-start | bytes 147464 | tf_op jit(solution)/shard_map/ppermute | solution.py:324
  8.9 0.1 collective-permute-start
  9.0 0.0 copy-done.2
  9.0 6.0 %shard_map.82 = f32[1152,128]{1,0:T(8,128)} custom-call(bf16[2048,2048]{1,0:T(8,128)(2,1)S(1)} %copy-done.2, s32[16,128]{1,0:T(8,128)} %bitcast.7, s32[16,128]{1,0:T(8,128)} %bitcast.8, bf16[2048,128]{1,0:T(8,128)(2,1)} %weight_hbm.1), custom_call_target="tpu_custom_call" | custom-call | flops 10000000000 | bytes 10000000 | tf_op jit(solution)/shard_map/pallas_call | solution.py:136
  15.0 6.0 %all-to-all-start = ((f32[128,1,1152]{2,1,0:T(1,128)}), f32[128,1,1152]{2,1,0:T(1,128)S(1)}, u32[]{:S(2)}, u32[]{:S(2)}) async-start(f32[128,1,1152]{2,1,0:T(1,128)} %bitcast.6), calls=%async_computation | async-start | bytes 1179648 | tf_op jit(solution)/shard_map/all_to_all | solution.py:343
  21.0 0.0 collective-permute-done.1.b_ref
  21.0 0.0 collective-permute-done.a_ref
  21.0 3.9 %shard_map.84 = (f32[40,768]{1,0:T(8,128)S(1)}, bf16[768,768]{1,0:T(8,128)(2,1)S(1)}, bf16[768,768]{1,0:T(8,128)(2,1)S(1)}, f32[768,768]{1,0:T(8,128)}) custom-call(f32[16,768]{1,0:T(8,128)S(1)} %copy-done.3, f32[16,768]{1,0:T(8,128)S(1)} %collective-permute-done.a_ref, f32[16,768]{1,0:T(8,128)S(1)} %collective-permute-done.1.b_ref, f32[768,768]{1,0:T(8,128)} %self_ref.3, ...), custom_call_target="tpu_custom_call" | custom-call | flops 20000000000 | bytes 10000000 | tf_op jit(solution)/shard_map/pallas_call | solution.py:262
  25.0 7.3 %collective-permute-start.3 = (f32[40,768]{1,0:T(8,128)S(1)}, f32[40,768]{1,0:T(8,128)S(1)}, u32[]{:S(2)}, u32[]{:S(2)}) collective-permute-start(f32[40,768]{1,0:T(8,128)S(1)} %get-tuple-element.13.ready_ref), channel_id=1, source_target_pairs={{1,2},{2,1},{3,4},{4,3},{5,6},{6,5},{7,8},{8,7},{9,10},{10,9},{11,... | collective-permute-start | bytes 368648 | tf_op jit(solution)/shard_map/ppermute | solution.py:324
  32.3 2.7 %all-to-all-done = f32[128,1,1152]{2,1,0:T(1,128)S(1)} async-done(((f32[128,1,1152]{2,1,0:T(1,128)}), f32[128,1,1152]{2,1,0:T(1,128)S(1)}, u32[]{:S(2)}, u32[]{:S(2)}) %all-to-all-start) | async-done | bytes 589856 | tf_op jit(solution)/shard_map/all_to_all | solution.py:343
  35.0 0.0 copy-start
  35.0 0.0 copy-start.1
  35.0 0.9 %shard_map.85 = (f32[16,768]{1,0:T(8,128)S(1)}, f32[16,768]{1,0:T(8,128)S(1)}) custom-call(f32[1152,128]{1,0:T(8,128)S(1)} %bitcast.4, f32[40,768]{1,0:T(8,128)S(1)} %get-tuple-element.13.ready_ref), custom_call_target="tpu_custom_call" | custom-call | flops 10000000000 | bytes 1000000 | tf_op jit(solution)/shard_map/pallas_call | solution.py:202
  35.9 0.1 collective-permute-start.2
  36.0 0.8 %shard_map.87.beyond_ref = f32[16,768]{1,0:T(8,128)S(1)} custom-call(f32[1152,128]{1,0:T(8,128)S(1)} %bitcast.5, f32[16,768]{1,0:T(8,128)S(1)} %get-tuple-element.16.own_ref.projected_ref), custom_call_target="tpu_custom_call" | custom-call | flops 100000000 | bytes 1000000 | tf_op jit(solution)/shard_map/pallas_call | solution.py:202
  36.8 0.4 collective-permute-done.2.a_ref
  37.2 0.0 copy-done
  37.2 0.2 copy-done.1
  37.4 0.8 %shard_map.86.part_ref = f32[16,768]{1,0:T(8,128)S(1)} custom-call(f32[16,768]{1,0:T(8,128)S(1)} %get-tuple-element.14.c_ref, f32[16,768]{1,0:T(8,128)S(1)} %collective-permute-done.2.a_ref, f32[768,768]{1,0:T(8,128)S(1)} %copy-done, f32[768,768]{1,0:T(8,128)S(1)} %copy-done.1), custom_call_target="tpu_custom_call" | custom-call | flops 500000000 | bytes 1000000 | tf_op jit(solution)/shard_map/pallas_call | solution.py:280
  38.2 0.0 collective-permute-done.3.other_ref
  38.2 0.5 shard_map.88.c_ref
  38.6 0.0 collective-permute-start.4
  38.7 4.5 %collective-permute-start.5 = (f32[16,768]{1,0:T(8,128)S(1)}, f32[16,768]{1,0:T(8,128)S(1)}, u32[]{:S(2)}, u32[]{:S(2)}) collective-permute-start(f32[16,768]{1,0:T(8,128)S(1)} %shard_map.88.c_ref), channel_id=1, source_target_pairs={{1,2},{2,1},{3,4},{4,3},{5,6},{6,5},{7,8},{8,7},{9,10},{10,9},{11,... | collective-permute-start | bytes 147464 | tf_op jit(solution)/shard_map/ppermute | solution.py:324
  43.2 0.0 collective-permute-done.4.a_ref
  43.2 0.8 %shard_map.89.part_ref = f32[16,768]{1,0:T(8,128)S(1)} custom-call(f32[16,768]{1,0:T(8,128)S(1)} %shard_map.88.c_ref, f32[16,768]{1,0:T(8,128)S(1)} %collective-permute-done.4.a_ref, f32[768,768]{1,0:T(8,128)S(1)} %copy-done, f32[768,768]{1,0:T(8,128)S(1)} %copy-done.1), custom_call_target="tpu_custom_call" | custom-call | flops 500000000 | bytes 1000000 | tf_op jit(solution)/shard_map/pallas_call | solution.py:280
  44.0 4.3 %collective-permute-done.5.b_ref = f32[16,768]{1,0:T(8,128)S(1)} collective-permute-done((f32[16,768]{1,0:T(8,128)S(1)}, f32[16,768]{1,0:T(8,128)S(1)}, u32[]{:S(2)}, u32[]{:S(2)}) %collective-permute-start.5) | collective-permute-done | bytes 49184 | tf_op jit(solution)/shard_map/ppermute | solution.py:324
  48.3 1.1 %shard_map.90 = f32[16,768]{1,0:T(8,128)} custom-call(f32[16,768]{1,0:T(8,128)S(1)} %shard_map.89.part_ref, f32[16,768]{1,0:T(8,128)S(1)} %collective-permute-done.5.b_ref, bf16[768,768]{1,0:T(8,128)(2,1)S(1)} %get-tuple-element.17.high_ref, bf16[768,768]{1,0:T(8,128)(2,1)S(1)} %get-tuple-element.18.low_ref, f32[16,768]{1,0:T(8,128)S(1)} %shard_map.88.c_ref, ...), custom_call_target="tpu_custom_call" | custom-call | flops 300000000 | bytes 1000000 | tf_op jit(solution)/shard_map/pallas_call | solution.py:307
Async XLA Ops:
  0.0 0.8 %copy-start.3 = (f32[16,768]{1,0:T(8,128)S(1)}, f32[16,768]{1,0:T(8,128)}, u32[]{:S(2)}) copy-start(f32[16,768]{1,0:T(8,128)} %c_hbm) | copy-start | bytes 147460
  0.0 9.0 %copy-start.2 = (bf16[2048,2048]{1,0:T(8,128)(2,1)S(1)}, bf16[2048,2048]{1,0:T(8,128)(2,1)}, u32[]{:S(2)}) copy-start(bf16[2048,2048]{1,0:T(8,128)(2,1)} %movie_ref.1) | copy-start | bytes 25165828
  0.8 20.2 %collective-permute-start.1 = (f32[16,768]{1,0:T(8,128)S(1)}, f32[16,768]{1,0:T(8,128)S(1)}, u32[]{:S(2)}, u32[]{:S(2)}) collective-permute-start(f32[16,768]{1,0:T(8,128)S(1)} %copy-done.3), channel_id=1, source_target_pairs={{1,2},{2,1},{3,4},{4,3},{5,6},{6,5},{7,8},{8,7},{9,10},{10,9},{11,... | collective-permute-start | bytes 147464 | tf_op jit(solution)/shard_map/ppermute | solution.py:324
  8.9 12.2 %collective-permute-start = (f32[16,768]{1,0:T(8,128)S(1)}, f32[16,768]{1,0:T(8,128)S(1)}, u32[]{:S(2)}, u32[]{:S(2)}) collective-permute-start(f32[16,768]{1,0:T(8,128)S(1)} %copy-done.3), channel_id=1, source_target_pairs={{0,1},{1,0},{2,3},{3,2},{4,5},{5,4},{6,7},{7,6},{8,9},{9,8},{10,11... | collective-permute-start | bytes 147464 | tf_op jit(solution)/shard_map/ppermute | solution.py:319
  15.0 20.0 %all-to-all-start = ((f32[128,1,1152]{2,1,0:T(1,128)}), f32[128,1,1152]{2,1,0:T(1,128)S(1)}, u32[]{:S(2)}, u32[]{:S(2)}) async-start(f32[128,1,1152]{2,1,0:T(1,128)} %bitcast.6), calls=%async_computation | async-start | bytes 1179648 | tf_op jit(solution)/shard_map/all_to_all | solution.py:343
  25.0 13.2 %collective-permute-start.3 = (f32[40,768]{1,0:T(8,128)S(1)}, f32[40,768]{1,0:T(8,128)S(1)}, u32[]{:S(2)}, u32[]{:S(2)}) collective-permute-start(f32[40,768]{1,0:T(8,128)S(1)} %get-tuple-element.13.ready_ref), channel_id=1, source_target_pairs={{1,2},{2,1},{3,4},{4,3},{5,6},{6,5},{7,8},{8,7},{9,10},{10,9},{11,... | collective-permute-start | bytes 368648 | tf_op jit(solution)/shard_map/ppermute | solution.py:324
  35.0 2.2 %copy-start = (f32[768,768]{1,0:T(8,128)S(1)}, f32[768,768]{1,0:T(8,128)}, u32[]{:S(2)}) copy-start(f32[768,768]{1,0:T(8,128)} %self_ref.3) | copy-start | bytes 7077892
  35.0 2.4 %copy-start.1 = (f32[768,768]{1,0:T(8,128)S(1)}, f32[768,768]{1,0:T(8,128)}, u32[]{:S(2)}) copy-start(f32[768,768]{1,0:T(8,128)} %get-tuple-element.15.close_ref) | copy-start | bytes 7077892
  35.9 1.3 %collective-permute-start.2 = (f32[16,768]{1,0:T(8,128)S(1)}, f32[16,768]{1,0:T(8,128)S(1)}, u32[]{:S(2)}, u32[]{:S(2)}) collective-permute-start(f32[16,768]{1,0:T(8,128)S(1)} %get-tuple-element.14.c_ref), channel_id=1, source_target_pairs={{0,1},{1,0},{2,3},{3,2},{4,5},{5,4},{6,7},{7,6},{8,9},{9,8},{10,11... | collective-permute-start | bytes 147464 | tf_op jit(solution)/shard_map/ppermute | solution.py:319
  38.6 4.5 %collective-permute-start.4 = (f32[16,768]{1,0:T(8,128)S(1)}, f32[16,768]{1,0:T(8,128)S(1)}, u32[]{:S(2)}, u32[]{:S(2)}) collective-permute-start(f32[16,768]{1,0:T(8,128)S(1)} %shard_map.88.c_ref), channel_id=1, source_target_pairs={{0,1},{1,0},{2,3},{3,2},{4,5},{5,4},{6,7},{7,6},{8,9},{9,8},{10,11... | collective-permute-start | bytes 147464 | tf_op jit(solution)/shard_map/ppermute | solution.py:319
  38.7 9.6 %collective-permute-start.5 = (f32[16,768]{1,0:T(8,128)S(1)}, f32[16,768]{1,0:T(8,128)S(1)}, u32[]{:S(2)}, u32[]{:S(2)}) collective-permute-start(f32[16,768]{1,0:T(8,128)S(1)} %shard_map.88.c_ref), channel_id=1, source_target_pairs={{1,2},{2,1},{3,4},{4,3},{5,6},{6,5},{7,8},{8,7},{9,10},{10,9},{11,... | collective-permute-start | bytes 147464 | tf_op jit(solution)/shard_map/ppermute | solution.py:324

commit v6 on v5

--- a/solution.py
+++ b/solution.py
@@ -64,20 +64,25 @@
     for copy in small:
         copy.start()
     out_ref[...] = jnp.zeros_like(out_ref)
-    for copy in small:
-        copy.wait()
+
+    def spread(first, last):
+        @pl.loop(first, last, unroll=2)
+        def _(r):
+            base = r * 2 * group
+            for f in range(16):
+                x = movie_ref[pl.ds(pl.multiple_of(r * 16, 16), 16), pl.ds(f * LANES, LANES)].astype(jnp.float32)
+                slab[pl.ds(base + f * PITCH, 8), :] = x[:8]
+                slab[pl.ds(base + group + f * PITCH, 8), :] = x[8:]
+
+    steps = movie_ref.shape[0] // 16
+    spread(0, steps // 2)
+    small[0].wait()
     row[...] = (tile[...] >> 3) * group + (tile[...] & 7)
     to_scalar = pltpu.make_async_copy(row, row_s, sem2.at[5])
     to_scalar.start()
-
-    @pl.loop(0, movie_ref.shape[0] // 16, unroll=2)
-    def _(r):
-        base = r * 2 * group
-        for f in range(16):
-            x = movie_ref[pl.ds(pl.multiple_of(r * 16, 16), 16), pl.ds(f * LANES, LANES)].astype(jnp.float32)
-            slab[pl.ds(base + f * PITCH, 8), :] = x[:8]
-            slab[pl.ds(base + group + f * PITCH, 8), :] = x[8:]
-
+    spread(steps // 2, steps)
+    for copy in small[1:]:
+        copy.wait()
     to_scalar.wait()
     fan[...] = jnp.zeros_like(fan)
     eighth = lax.broadcasted_iota(jnp.int32, (16, WIDE), 1) % PIECE

time: 49.7 us -> 48.7 us (0.980)
  Pallas kernels: 15.4 us -> 14.4 us
    pallas_call x1, Pallas kernels: 6.01 us -> 5.01 us  [contributions(): pl.pallas_call(contrib_kernel, out_shape=jax.ShapeDtypeStruct((devices *...]
  transfers between devices with their start and end apart: 7 -> 7, of which waited for: 3 -> 3; matrix products, arithmetic and copies ran while one was open for 0% -> 0% of each run, Pallas kernels for 27% -> 25%
where the time goes in v6:
time: 48.7 us; the launch traced here: 48.4 us
  starting transfers between devices  26.1 us (54%)
  Pallas kernels  14.4 us (30%)
  waiting for transfers between devices  7.43 us (15%)
    ppermute x3, starting transfers between devices, swap_across(): return lax.ppermute(c, AXES, [(i, across(i)) for i in range(1, n - 1)])  19.8 us
    all_to_all x1, starting transfers between devices, local(): got = lax.all_to_all(send.reshape(devices, 1, SLOT * LANES), AXES, 0, 0)  6.01 us
    pallas_call x1, Pallas kernels, contributions(): pl.pallas_call(contrib_kernel, out_shape=jax.ShapeDtypeStruct((devices *...  5.01 us
    ppermute x3, waiting for transfers between devices, swap_across(): return lax.ppermute(c, AXES, [(i, across(i)) for i in range(1, n - 1)])  4.33 us
    pallas_call x1, Pallas kernels, prepare(): pl.pallas_call(prepare_kernel, out_shape=(jax.ShapeDtypeStruct((40, n), j...  3.91 us
    all_to_all x1, waiting for transfers between devices, local(): got = lax.all_to_all(send.reshape(devices, 1, SLOT * LANES), AXES, 0, 0)  2.74 us
    pallas_call x2, Pallas kernels, combine(): pl.pallas_call(kernel, out_shape=(out,) * outs, in_specs=[VMEM] * 2, out_...  1.72 us
    pallas_call x2, Pallas kernels, near(): pl.pallas_call(near_kernel, out_shape=jax.ShapeDtypeStruct(c.shape, jnp.f...  1.6 us
  transfers between devices with their start and end apart: 7, of which 3 were waited for; matrix products, arithmetic and copies ran while one was open for 0% of the time, Pallas kernels for 25%

profile of v6, /device:TPU:2, one launch (start us, length us, event | category | flops | bytes accessed | tf_op | source)
XLA Modules:
  0.0 48.4 jit_solution(17638211451545598594)
XLA Ops:
  0.0 0.0 copy-start.3
  0.0 0.0 copy-start.2
  0.0 0.6 %shard_map.83 = f32[8,128]{1,0:T(8,128)} custom-call(), custom_call_target="tpu_custom_call" | custom-call | flops 10000000000 | bytes 10000000 | tf_op jit(solution)/shard_map/pallas_call | solution.py:128
  0.6 0.2 copy-done.3
  0.8 8.1 %collective-permute-start.1 = (f32[16,768]{1,0:T(8,128)S(1)}, f32[16,768]{1,0:T(8,128)S(1)}, u32[]{:S(2)}, u32[]{:S(2)}) collective-permute-start(f32[16,768]{1,0:T(8,128)S(1)} %copy-done.3), channel_id=1, source_target_pairs={{1,2},{2,1},{3,4},{4,3},{5,6},{6,5},{7,8},{8,7},{9,10},{10,9},{11,... | collective-permute-start | bytes 147464 | tf_op jit(solution)/shard_map/ppermute | solution.py:329
  8.9 0.1 collective-permute-start
  9.0 0.0 copy-done.2
  9.0 5.0 %shard_map.82 = f32[1152,128]{1,0:T(8,128)} custom-call(bf16[2048,2048]{1,0:T(8,128)(2,1)S(1)} %copy-done.2, s32[16,128]{1,0:T(8,128)} %bitcast.7, s32[16,128]{1,0:T(8,128)} %bitcast.8, bf16[2048,128]{1,0:T(8,128)(2,1)} %weight_hbm.1), custom_call_target="tpu_custom_call" | custom-call | flops 10000000000 | bytes 10000000 | tf_op jit(solution)/shard_map/pallas_call | solution.py:141
  14.0 6.0 %all-to-all-start = ((f32[128,1,1152]{2,1,0:T(1,128)}), f32[128,1,1152]{2,1,0:T(1,128)S(1)}, u32[]{:S(2)}, u32[]{:S(2)}) async-start(f32[128,1,1152]{2,1,0:T(1,128)} %bitcast.6), calls=%async_computation | async-start | bytes 1179648 | tf_op jit(solution)/shard_map/all_to_all | solution.py:348
  20.0 0.0 collective-permute-done.1.b_ref
  20.0 0.0 collective-permute-done.a_ref
  20.0 3.9 %shard_map.84 = (f32[40,768]{1,0:T(8,128)S(1)}, bf16[768,768]{1,0:T(8,128)(2,1)S(1)}, bf16[768,768]{1,0:T(8,128)(2,1)S(1)}, f32[768,768]{1,0:T(8,128)}) custom-call(f32[16,768]{1,0:T(8,128)S(1)} %copy-done.3, f32[16,768]{1,0:T(8,128)S(1)} %collective-permute-done.a_ref, f32[16,768]{1,0:T(8,128)S(1)} %collective-permute-done.1.b_ref, f32[768,768]{1,0:T(8,128)} %self_ref.3, ...), custom_call_target="tpu_custom_call" | custom-call | flops 20000000000 | bytes 10000000 | tf_op jit(solution)/shard_map/pallas_call | solution.py:267
  24.0 7.3 %collective-permute-start.3 = (f32[40,768]{1,0:T(8,128)S(1)}, f32[40,768]{1,0:T(8,128)S(1)}, u32[]{:S(2)}, u32[]{:S(2)}) collective-permute-start(f32[40,768]{1,0:T(8,128)S(1)} %get-tuple-element.13.ready_ref), channel_id=1, source_target_pairs={{1,2},{2,1},{3,4},{4,3},{5,6},{6,5},{7,8},{8,7},{9,10},{10,9},{11,... | collective-permute-start | bytes 368648 | tf_op jit(solution)/shard_map/ppermute | solution.py:329
  31.3 2.7 %all-to-all-done = f32[128,1,1152]{2,1,0:T(1,128)S(1)} async-done(((f32[128,1,1152]{2,1,0:T(1,128)}), f32[128,1,1152]{2,1,0:T(1,128)S(1)}, u32[]{:S(2)}, u32[]{:S(2)}) %all-to-all-start) | async-done | bytes 589856 | tf_op jit(solution)/shard_map/all_to_all | solution.py:348
  34.0 0.0 copy-start
  34.0 0.0 copy-start.1
  34.0 0.9 %shard_map.85 = (f32[16,768]{1,0:T(8,128)S(1)}, f32[16,768]{1,0:T(8,128)S(1)}) custom-call(f32[1152,128]{1,0:T(8,128)S(1)} %bitcast.4, f32[40,768]{1,0:T(8,128)S(1)} %get-tuple-element.13.ready_ref), custom_call_target="tpu_custom_call" | custom-call | flops 10000000000 | bytes 1000000 | tf_op jit(solution)/shard_map/pallas_call | solution.py:207
  34.9 0.1 collective-permute-start.2
  35.0 0.8 %shard_map.87.beyond_ref = f32[16,768]{1,0:T(8,128)S(1)} custom-call(f32[1152,128]{1,0:T(8,128)S(1)} %bitcast.5, f32[16,768]{1,0:T(8,128)S(1)} %get-tuple-element.16.own_ref.projected_ref), custom_call_target="tpu_custom_call" | custom-call | flops 100000000 | bytes 1000000 | tf_op jit(solution)/shard_map/pallas_call | solution.py:207
  35.8 0.4 collective-permute-done.2.a_ref
  36.2 0.0 copy-done
  36.2 0.2 copy-done.1
  36.4 0.8 %shard_map.86.part_ref = f32[16,768]{1,0:T(8,128)S(1)} custom-call(f32[16,768]{1,0:T(8,128)S(1)} %get-tuple-element.14.c_ref, f32[16,768]{1,0:T(8,128)S(1)} %collective-permute-done.2.a_ref, f32[768,768]{1,0:T(8,128)S(1)} %copy-done, f32[768,768]{1,0:T(8,128)S(1)} %copy-done.1), custom_call_target="tpu_custom_call" | custom-call | flops 500000000 | bytes 1000000 | tf_op jit(solution)/shard_map/pallas_call | solution.py:285
  37.2 0.0 collective-permute-done.3.other_ref
  37.2 0.5 shard_map.88.c_ref
  37.6 0.0 collective-permute-start.4
  37.7 4.5 %collective-permute-start.5 = (f32[16,768]{1,0:T(8,128)S(1)}, f32[16,768]{1,0:T(8,128)S(1)}, u32[]{:S(2)}, u32[]{:S(2)}) collective-permute-start(f32[16,768]{1,0:T(8,128)S(1)} %shard_map.88.c_ref), channel_id=1, source_target_pairs={{1,2},{2,1},{3,4},{4,3},{5,6},{6,5},{7,8},{8,7},{9,10},{10,9},{11,... | collective-permute-start | bytes 147464 | tf_op jit(solution)/shard_map/ppermute | solution.py:329
  42.2 0.0 collective-permute-done.4.a_ref
  42.2 0.8 %shard_map.89.part_ref = f32[16,768]{1,0:T(8,128)S(1)} custom-call(f32[16,768]{1,0:T(8,128)S(1)} %shard_map.88.c_ref, f32[16,768]{1,0:T(8,128)S(1)} %collective-permute-done.4.a_ref, f32[768,768]{1,0:T(8,128)S(1)} %copy-done, f32[768,768]{1,0:T(8,128)S(1)} %copy-done.1), custom_call_target="tpu_custom_call" | custom-call | flops 500000000 | bytes 1000000 | tf_op jit(solution)/shard_map/pallas_call | solution.py:285
  43.0 4.3 %collective-permute-done.5.b_ref = f32[16,768]{1,0:T(8,128)S(1)} collective-permute-done((f32[16,768]{1,0:T(8,128)S(1)}, f32[16,768]{1,0:T(8,128)S(1)}, u32[]{:S(2)}, u32[]{:S(2)}) %collective-permute-start.5) | collective-permute-done | bytes 49184 | tf_op jit(solution)/shard_map/ppermute | solution.py:329
  47.3 1.1 %shard_map.90 = f32[16,768]{1,0:T(8,128)} custom-call(f32[16,768]{1,0:T(8,128)S(1)} %shard_map.89.part_ref, f32[16,768]{1,0:T(8,128)S(1)} %collective-permute-done.5.b_ref, bf16[768,768]{1,0:T(8,128)(2,1)S(1)} %get-tuple-element.17.high_ref, bf16[768,768]{1,0:T(8,128)(2,1)S(1)} %get-tuple-element.18.low_ref, f32[16,768]{1,0:T(8,128)S(1)} %shard_map.88.c_ref, ...), custom_call_target="tpu_custom_call" | custom-call | flops 300000000 | bytes 1000000 | tf_op jit(solution)/shard_map/pallas_call | solution.py:312
Async XLA Ops:
  0.0 0.8 %copy-start.3 = (f32[16,768]{1,0:T(8,128)S(1)}, f32[16,768]{1,0:T(8,128)}, u32[]{:S(2)}) copy-start(f32[16,768]{1,0:T(8,128)} %c_hbm) | copy-start | bytes 147460
  0.0 9.0 %copy-start.2 = (bf16[2048,2048]{1,0:T(8,128)(2,1)S(1)}, bf16[2048,2048]{1,0:T(8,128)(2,1)}, u32[]{:S(2)}) copy-start(bf16[2048,2048]{1,0:T(8,128)(2,1)} %movie_ref.1) | copy-start | bytes 25165828
  0.8 19.2 %collective-permute-start.1 = (f32[16,768]{1,0:T(8,128)S(1)}, f32[16,768]{1,0:T(8,128)S(1)}, u32[]{:S(2)}, u32[]{:S(2)}) collective-permute-start(f32[16,768]{1,0:T(8,128)S(1)} %copy-done.3), channel_id=1, source_target_pairs={{1,2},{2,1},{3,4},{4,3},{5,6},{6,5},{7,8},{8,7},{9,10},{10,9},{11,... | collective-permute-start | bytes 147464 | tf_op jit(solution)/shard_map/ppermute | solution.py:329
  8.9 11.2 %collective-permute-start = (f32[16,768]{1,0:T(8,128)S(1)}, f32[16,768]{1,0:T(8,128)S(1)}, u32[]{:S(2)}, u32[]{:S(2)}) collective-permute-start(f32[16,768]{1,0:T(8,128)S(1)} %copy-done.3), channel_id=1, source_target_pairs={{0,1},{1,0},{2,3},{3,2},{4,5},{5,4},{6,7},{7,6},{8,9},{9,8},{10,11... | collective-permute-start | bytes 147464 | tf_op jit(solution)/shard_map/ppermute | solution.py:324
  14.0 20.0 %all-to-all-start = ((f32[128,1,1152]{2,1,0:T(1,128)}), f32[128,1,1152]{2,1,0:T(1,128)S(1)}, u32[]{:S(2)}, u32[]{:S(2)}) async-start(f32[128,1,1152]{2,1,0:T(1,128)} %bitcast.6), calls=%async_computation | async-start | bytes 1179648 | tf_op jit(solution)/shard_map/all_to_all | solution.py:348
  24.0 13.2 %collective-permute-start.3 = (f32[40,768]{1,0:T(8,128)S(1)}, f32[40,768]{1,0:T(8,128)S(1)}, u32[]{:S(2)}, u32[]{:S(2)}) collective-permute-start(f32[40,768]{1,0:T(8,128)S(1)} %get-tuple-element.13.ready_ref), channel_id=1, source_target_pairs={{1,2},{2,1},{3,4},{4,3},{5,6},{6,5},{7,8},{8,7},{9,10},{10,9},{11,... | collective-permute-start | bytes 368648 | tf_op jit(solution)/shard_map/ppermute | solution.py:329
  34.0 2.2 %copy-start = (f32[768,768]{1,0:T(8,128)S(1)}, f32[768,768]{1,0:T(8,128)}, u32[]{:S(2)}) copy-start(f32[768,768]{1,0:T(8,128)} %self_ref.3) | copy-start | bytes 7077892
  34.0 2.4 %copy-start.1 = (f32[768,768]{1,0:T(8,128)S(1)}, f32[768,768]{1,0:T(8,128)}, u32[]{:S(2)}) copy-start(f32[768,768]{1,0:T(8,128)} %get-tuple-element.15.close_ref) | copy-start | bytes 7077892
  34.9 1.3 %collective-permute-start.2 = (f32[16,768]{1,0:T(8,128)S(1)}, f32[16,768]{1,0:T(8,128)S(1)}, u32[]{:S(2)}, u32[]{:S(2)}) collective-permute-start(f32[16,768]{1,0:T(8,128)S(1)} %get-tuple-element.14.c_ref), channel_id=1, source_target_pairs={{0,1},{1,0},{2,3},{3,2},{4,5},{5,4},{6,7},{7,6},{8,9},{9,8},{10,11... | collective-permute-start | bytes 147464 | tf_op jit(solution)/shard_map/ppermute | solution.py:324
  37.6 4.5 %collective-permute-start.4 = (f32[16,768]{1,0:T(8,128)S(1)}, f32[16,768]{1,0:T(8,128)S(1)}, u32[]{:S(2)}, u32[]{:S(2)}) collective-permute-start(f32[16,768]{1,0:T(8,128)S(1)} %shard_map.88.c_ref), channel_id=1, source_target_pairs={{0,1},{1,0},{2,3},{3,2},{4,5},{5,4},{6,7},{7,6},{8,9},{9,8},{10,11... | collective-permute-start | bytes 147464 | tf_op jit(solution)/shard_map/ppermute | solution.py:324
  37.7 9.6 %collective-permute-start.5 = (f32[16,768]{1,0:T(8,128)S(1)}, f32[16,768]{1,0:T(8,128)S(1)}, u32[]{:S(2)}, u32[]{:S(2)}) collective-permute-start(f32[16,768]{1,0:T(8,128)S(1)} %shard_map.88.c_ref), channel_id=1, source_target_pairs={{1,2},{2,1},{3,4},{4,3},{5,6},{6,5},{7,8},{8,7},{9,10},{10,9},{11,... | collective-permute-start | bytes 147464 | tf_op jit(solution)/shard_map/ppermute | solution.py:329

commit v7 on v6

--- a/solution.py
+++ b/solution.py
@@ -66,7 +66,7 @@
     out_ref[...] = jnp.zeros_like(out_ref)
 
     def spread(first, last):
-        @pl.loop(first, last, unroll=2)
+        @pl.loop(first, last, unroll=4)
         def _(r):
             base = r * 2 * group
             for f in range(16):

time: 48.7 us -> 48.7 us (level)
  no operation moved by 1% of the time
where the time goes in v7:
time: 48.7 us; the launch traced here: 48.4 us
  starting transfers between devices  26.1 us (54%)
  Pallas kernels  14.3 us (29%)
  waiting for transfers between devices  7.43 us (15%)
    ppermute x3, starting transfers between devices, swap_across(): return lax.ppermute(c, AXES, [(i, across(i)) for i in range(1, n - 1)])  19.8 us
    all_to_all x1, starting transfers between devices, local(): got = lax.all_to_all(send.reshape(devices, 1, SLOT * LANES), AXES, 0, 0)  6.01 us
    pallas_call x1, Pallas kernels, contributions(): pl.pallas_call(contrib_kernel, out_shape=jax.ShapeDtypeStruct((devices *...  4.98 us
    ppermute x3, waiting for transfers between devices, swap_across(): return lax.ppermute(c, AXES, [(i, across(i)) for i in range(1, n - 1)])  4.33 us
    pallas_call x1, Pallas kernels, prepare(): pl.pallas_call(prepare_kernel, out_shape=(jax.ShapeDtypeStruct((40, n), j...  3.91 us
    all_to_all x1, waiting for transfers between devices, local(): got = lax.all_to_all(send.reshape(devices, 1, SLOT * LANES), AXES, 0, 0)  2.74 us
    pallas_call x2, Pallas kernels, combine(): pl.pallas_call(kernel, out_shape=(out,) * outs, in_specs=[VMEM] * 2, out_...  1.72 us
    pallas_call x2, Pallas kernels, near(): pl.pallas_call(near_kernel, out_shape=jax.ShapeDtypeStruct(c.shape, jnp.f...  1.6 us
  transfers between devices with their start and end apart: 7, of which 3 were waited for; matrix products, arithmetic and copies ran while one was open for 0% of the time, Pallas kernels for 25%

profile of v7, /device:TPU:2, one launch (start us, length us, event | category | flops | bytes accessed | tf_op | source)
XLA Modules:
  0.0 48.4 jit_solution(1438225130551442372)
XLA Ops:
  0.0 0.0 copy-start.3
  0.0 0.0 copy-start.2
  0.0 0.6 %shard_map.83 = f32[8,128]{1,0:T(8,128)} custom-call(), custom_call_target="tpu_custom_call" | custom-call | flops 10000000000 | bytes 10000000 | tf_op jit(solution)/shard_map/pallas_call | solution.py:128
  0.6 0.2 copy-done.3
  0.8 8.1 %collective-permute-start.1 = (f32[16,768]{1,0:T(8,128)S(1)}, f32[16,768]{1,0:T(8,128)S(1)}, u32[]{:S(2)}, u32[]{:S(2)}) collective-permute-start(f32[16,768]{1,0:T(8,128)S(1)} %copy-done.3), channel_id=1, source_target_pairs={{1,2},{2,1},{3,4},{4,3},{5,6},{6,5},{7,8},{8,7},{9,10},{10,9},{11,... | collective-permute-start | bytes 147464 | tf_op jit(solution)/shard_map/ppermute | solution.py:329
  8.9 0.1 collective-permute-start
  9.0 0.0 copy-done.2
  9.0 5.0 %shard_map.82 = f32[1152,128]{1,0:T(8,128)} custom-call(bf16[2048,2048]{1,0:T(8,128)(2,1)S(1)} %copy-done.2, s32[16,128]{1,0:T(8,128)} %bitcast.7, s32[16,128]{1,0:T(8,128)} %bitcast.8, bf16[2048,128]{1,0:T(8,128)(2,1)} %weight_hbm.1), custom_call_target="tpu_custom_call" | custom-call | flops 10000000000 | bytes 10000000 | tf_op jit(solution)/shard_map/pallas_call | solution.py:141
  14.0 6.0 %all-to-all-start = ((f32[128,1,1152]{2,1,0:T(1,128)}), f32[128,1,1152]{2,1,0:T(1,128)S(1)}, u32[]{:S(2)}, u32[]{:S(2)}) async-start(f32[128,1,1152]{2,1,0:T(1,128)} %bitcast.6), calls=%async_computation | async-start | bytes 1179648 | tf_op jit(solution)/shard_map/all_to_all | solution.py:348
  20.0 0.0 collective-permute-done.1.b_ref
  20.0 0.0 collective-permute-done.a_ref
  20.0 3.9 %shard_map.84 = (f32[40,768]{1,0:T(8,128)S(1)}, bf16[768,768]{1,0:T(8,128)(2,1)S(1)}, bf16[768,768]{1,0:T(8,128)(2,1)S(1)}, f32[768,768]{1,0:T(8,128)}) custom-call(f32[16,768]{1,0:T(8,128)S(1)} %copy-done.3, f32[16,768]{1,0:T(8,128)S(1)} %collective-permute-done.a_ref, f32[16,768]{1,0:T(8,128)S(1)} %collective-permute-done.1.b_ref, f32[768,768]{1,0:T(8,128)} %self_ref.3, ...), custom_call_target="tpu_custom_call" | custom-call | flops 20000000000 | bytes 10000000 | tf_op jit(solution)/shard_map/pallas_call | solution.py:267
  23.9 7.3 %collective-permute-start.3 = (f32[40,768]{1,0:T(8,128)S(1)}, f32[40,768]{1,0:T(8,128)S(1)}, u32[]{:S(2)}, u32[]{:S(2)}) collective-permute-start(f32[40,768]{1,0:T(8,128)S(1)} %get-tuple-element.13.ready_ref), channel_id=1, source_target_pairs={{1,2},{2,1},{3,4},{4,3},{5,6},{6,5},{7,8},{8,7},{9,10},{10,9},{11,... | collective-permute-start | bytes 368648 | tf_op jit(solution)/shard_map/ppermute | solution.py:329
  31.2 2.7 %all-to-all-done = f32[128,1,1152]{2,1,0:T(1,128)S(1)} async-done(((f32[128,1,1152]{2,1,0:T(1,128)}), f32[128,1,1152]{2,1,0:T(1,128)S(1)}, u32[]{:S(2)}, u32[]{:S(2)}) %all-to-all-start) | async-done | bytes 589856 | tf_op jit(solution)/shard_map/all_to_all | solution.py:348
  34.0 0.0 copy-start
  34.0 0.0 copy-start.1
  34.0 0.9 %shard_map.85 = (f32[16,768]{1,0:T(8,128)S(1)}, f32[16,768]{1,0:T(8,128)S(1)}) custom-call(f32[1152,128]{1,0:T(8,128)S(1)} %bitcast.4, f32[40,768]{1,0:T(8,128)S(1)} %get-tuple-element.13.ready_ref), custom_call_target="tpu_custom_call" | custom-call | flops 10000000000 | bytes 1000000 | tf_op jit(solution)/shard_map/pallas_call | solution.py:207
  34.9 0.1 collective-permute-start.2
  34.9 0.9 %shard_map.87.beyond_ref = f32[16,768]{1,0:T(8,128)S(1)} custom-call(f32[1152,128]{1,0:T(8,128)S(1)} %bitcast.5, f32[16,768]{1,0:T(8,128)S(1)} %get-tuple-element.16.own_ref.projected_ref), custom_call_target="tpu_custom_call" | custom-call | flops 100000000 | bytes 1000000 | tf_op jit(solution)/shard_map/pallas_call | solution.py:207
  35.8 0.4 collective-permute-done.2.a_ref
  36.2 0.0 copy-done
  36.2 0.2 copy-done.1
  36.4 0.8 %shard_map.86.part_ref = f32[16,768]{1,0:T(8,128)S(1)} custom-call(f32[16,768]{1,0:T(8,128)S(1)} %get-tuple-element.14.c_ref, f32[16,768]{1,0:T(8,128)S(1)} %collective-permute-done.2.a_ref, f32[768,768]{1,0:T(8,128)S(1)} %copy-done, f32[768,768]{1,0:T(8,128)S(1)} %copy-done.1), custom_call_target="tpu_custom_call" | custom-call | flops 500000000 | bytes 1000000 | tf_op jit(solution)/shard_map/pallas_call | solution.py:285
  37.2 0.0 collective-permute-done.3.other_ref
  37.2 0.5 shard_map.88.c_ref
  37.6 0.0 collective-permute-start.4
  37.7 4.5 %collective-permute-start.5 = (f32[16,768]{1,0:T(8,128)S(1)}, f32[16,768]{1,0:T(8,128)S(1)}, u32[]{:S(2)}, u32[]{:S(2)}) collective-permute-start(f32[16,768]{1,0:T(8,128)S(1)} %shard_map.88.c_ref), channel_id=1, source_target_pairs={{1,2},{2,1},{3,4},{4,3},{5,6},{6,5},{7,8},{8,7},{9,10},{10,9},{11,... | collective-permute-start | bytes 147464 | tf_op jit(solution)/shard_map/ppermute | solution.py:329
  42.2 0.0 collective-permute-done.4.a_ref
  42.2 0.8 %shard_map.89.part_ref = f32[16,768]{1,0:T(8,128)S(1)} custom-call(f32[16,768]{1,0:T(8,128)S(1)} %shard_map.88.c_ref, f32[16,768]{1,0:T(8,128)S(1)} %collective-permute-done.4.a_ref, f32[768,768]{1,0:T(8,128)S(1)} %copy-done, f32[768,768]{1,0:T(8,128)S(1)} %copy-done.1), custom_call_target="tpu_custom_call" | custom-call | flops 500000000 | bytes 1000000 | tf_op jit(solution)/shard_map/pallas_call | solution.py:285
  43.0 4.3 %collective-permute-done.5.b_ref = f32[16,768]{1,0:T(8,128)S(1)} collective-permute-done((f32[16,768]{1,0:T(8,128)S(1)}, f32[16,768]{1,0:T(8,128)S(1)}, u32[]{:S(2)}, u32[]{:S(2)}) %collective-permute-start.5) | collective-permute-done | bytes 49184 | tf_op jit(solution)/shard_map/ppermute | solution.py:329
  47.3 1.1 %shard_map.90 = f32[16,768]{1,0:T(8,128)} custom-call(f32[16,768]{1,0:T(8,128)S(1)} %shard_map.89.part_ref, f32[16,768]{1,0:T(8,128)S(1)} %collective-permute-done.5.b_ref, bf16[768,768]{1,0:T(8,128)(2,1)S(1)} %get-tuple-element.17.high_ref, bf16[768,768]{1,0:T(8,128)(2,1)S(1)} %get-tuple-element.18.low_ref, f32[16,768]{1,0:T(8,128)S(1)} %shard_map.88.c_ref, ...), custom_call_target="tpu_custom_call" | custom-call | flops 300000000 | bytes 1000000 | tf_op jit(solution)/shard_map/pallas_call | solution.py:312
Async XLA Ops:
  0.0 0.8 %copy-start.3 = (f32[16,768]{1,0:T(8,128)S(1)}, f32[16,768]{1,0:T(8,128)}, u32[]{:S(2)}) copy-start(f32[16,768]{1,0:T(8,128)} %c_hbm) | copy-start | bytes 147460
  0.0 9.0 %copy-start.2 = (bf16[2048,2048]{1,0:T(8,128)(2,1)S(1)}, bf16[2048,2048]{1,0:T(8,128)(2,1)}, u32[]{:S(2)}) copy-start(bf16[2048,2048]{1,0:T(8,128)(2,1)} %movie_ref.1) | copy-start | bytes 25165828
  0.8 19.2 %collective-permute-start.1 = (f32[16,768]{1,0:T(8,128)S(1)}, f32[16,768]{1,0:T(8,128)S(1)}, u32[]{:S(2)}, u32[]{:S(2)}) collective-permute-start(f32[16,768]{1,0:T(8,128)S(1)} %copy-done.3), channel_id=1, source_target_pairs={{1,2},{2,1},{3,4},{4,3},{5,6},{6,5},{7,8},{8,7},{9,10},{10,9},{11,... | collective-permute-start | bytes 147464 | tf_op jit(solution)/shard_map/ppermute | solution.py:329
  8.9 11.1 %collective-permute-start = (f32[16,768]{1,0:T(8,128)S(1)}, f32[16,768]{1,0:T(8,128)S(1)}, u32[]{:S(2)}, u32[]{:S(2)}) collective-permute-start(f32[16,768]{1,0:T(8,128)S(1)} %copy-done.3), channel_id=1, source_target_pairs={{0,1},{1,0},{2,3},{3,2},{4,5},{5,4},{6,7},{7,6},{8,9},{9,8},{10,11... | collective-permute-start | bytes 147464 | tf_op jit(solution)/shard_map/ppermute | solution.py:324
  14.0 20.0 %all-to-all-start = ((f32[128,1,1152]{2,1,0:T(1,128)}), f32[128,1,1152]{2,1,0:T(1,128)S(1)}, u32[]{:S(2)}, u32[]{:S(2)}) async-start(f32[128,1,1152]{2,1,0:T(1,128)} %bitcast.6), calls=%async_computation | async-start | bytes 1179648 | tf_op jit(solution)/shard_map/all_to_all | solution.py:348
  23.9 13.2 %collective-permute-start.3 = (f32[40,768]{1,0:T(8,128)S(1)}, f32[40,768]{1,0:T(8,128)S(1)}, u32[]{:S(2)}, u32[]{:S(2)}) collective-permute-start(f32[40,768]{1,0:T(8,128)S(1)} %get-tuple-element.13.ready_ref), channel_id=1, source_target_pairs={{1,2},{2,1},{3,4},{4,3},{5,6},{6,5},{7,8},{8,7},{9,10},{10,9},{11,... | collective-permute-start | bytes 368648 | tf_op jit(solution)/shard_map/ppermute | solution.py:329
  34.0 2.2 %copy-start = (f32[768,768]{1,0:T(8,128)S(1)}, f32[768,768]{1,0:T(8,128)}, u32[]{:S(2)}) copy-start(f32[768,768]{1,0:T(8,128)} %self_ref.3) | copy-start | bytes 7077892
  34.0 2.4 %copy-start.1 = (f32[768,768]{1,0:T(8,128)S(1)}, f32[768,768]{1,0:T(8,128)}, u32[]{:S(2)}) copy-start(f32[768,768]{1,0:T(8,128)} %get-tuple-element.15.close_ref) | copy-start | bytes 7077892
  34.9 1.3 %collective-permute-start.2 = (f32[16,768]{1,0:T(8,128)S(1)}, f32[16,768]{1,0:T(8,128)S(1)}, u32[]{:S(2)}, u32[]{:S(2)}) collective-permute-start(f32[16,768]{1,0:T(8,128)S(1)} %get-tuple-element.14.c_ref), channel_id=1, source_target_pairs={{0,1},{1,0},{2,3},{3,2},{4,5},{5,4},{6,7},{7,6},{8,9},{9,8},{10,11... | collective-permute-start | bytes 147464 | tf_op jit(solution)/shard_map/ppermute | solution.py:324
  37.6 4.5 %collective-permute-start.4 = (f32[16,768]{1,0:T(8,128)S(1)}, f32[16,768]{1,0:T(8,128)S(1)}, u32[]{:S(2)}, u32[]{:S(2)}) collective-permute-start(f32[16,768]{1,0:T(8,128)S(1)} %shard_map.88.c_ref), channel_id=1, source_target_pairs={{0,1},{1,0},{2,3},{3,2},{4,5},{5,4},{6,7},{7,6},{8,9},{9,8},{10,11... | collective-permute-start | bytes 147464 | tf_op jit(solution)/shard_map/ppermute | solution.py:324
  37.7 9.6 %collective-permute-start.5 = (f32[16,768]{1,0:T(8,128)S(1)}, f32[16,768]{1,0:T(8,128)S(1)}, u32[]{:S(2)}, u32[]{:S(2)}) collective-permute-start(f32[16,768]{1,0:T(8,128)S(1)} %shard_map.88.c_ref), channel_id=1, source_target_pairs={{1,2},{2,1},{3,4},{4,3},{5,6},{6,5},{7,8},{8,7},{9,10},{10,9},{11,... | collective-permute-start | bytes 147464 | tf_op jit(solution)/shard_map/ppermute | solution.py:329

commit v8 on v6

--- a/solution.py
+++ b/solution.py
@@ -121,14 +121,14 @@
 
 
 def open_kernel(out_ref):
-    out_ref[...] = jnp.zeros_like(out_ref)
+    del out_ref
 
 
 def opening():
     return pl.pallas_call(
         open_kernel,
         out_shape=jax.ShapeDtypeStruct((8, LANES), jnp.float32),
-        out_specs=VMEM,
+        out_specs=HBM,
         compiler_params=pltpu.CompilerParams(vmem_limit_bytes=1 << 20, has_side_effects=True),
         cost_estimate=pl.CostEstimate(flops=10**10, bytes_accessed=10**7, transcendentals=0),
     )()

time: 48.7 us -> 48.7 us (level)
  Pallas kernels: 14.4 us -> 13.8 us
  local copies, waits for them, and re-layouts: 0.4 us -> 0.99 us
    pallas_call x1, Pallas kernels: 0.59 us -> 0.01 us  [opening(): pl.pallas_call(open_kernel, out_shape=jax.ShapeDtypeStruct((8, LANES), jn...]
    unnamed x8, local copies, waits for them, and re-layouts: 0.4 us -> 0.99 us
where the time goes in v8:
time: 48.7 us; the launch traced here: 48.4 us
  starting transfers between devices  26.1 us (54%)
  Pallas kernels  13.8 us (28%)
  waiting for transfers between devices  7.43 us (15%)
  local copies, waits for them, and re-layouts  0.99 us (2%)
    ppermute x3, starting transfers between devices, swap_across(): return lax.ppermute(c, AXES, [(i, across(i)) for i in range(1, n - 1)])  19.8 us
    all_to_all x1, starting transfers between devices, local(): got = lax.all_to_all(send.reshape(devices, 1, SLOT * LANES), AXES, 0, 0)  5.99 us
    pallas_call x1, Pallas kernels, contributions(): pl.pallas_call(contrib_kernel, out_shape=jax.ShapeDtypeStruct((devices *...  5.02 us
    ppermute x3, waiting for transfers between devices, swap_across(): return lax.ppermute(c, AXES, [(i, across(i)) for i in range(1, n - 1)])  4.33 us
    pallas_call x1, Pallas kernels, prepare(): pl.pallas_call(prepare_kernel, out_shape=(jax.ShapeDtypeStruct((40, n), j...  3.91 us
    all_to_all x1, waiting for transfers between devices, local(): got = lax.all_to_all(send.reshape(devices, 1, SLOT * LANES), AXES, 0, 0)  2.74 us
    pallas_call x2, Pallas kernels, combine(): pl.pallas_call(kernel, out_shape=(out,) * outs, in_specs=[VMEM] * 2, out_...  1.71 us
    pallas_call x2, Pallas kernels, near(): pl.pallas_call(near_kernel, out_shape=jax.ShapeDtypeStruct(c.shape, jnp.f...  1.6 us
  transfers between devices with their start and end apart: 7, of which 3 were waited for; matrix products, arithmetic and copies ran while one was open for 0% of the time, Pallas kernels for 25%

profile of v8, /device:TPU:2, one launch (start us, length us, event | category | flops | bytes accessed | tf_op | source)
XLA Modules:
  0.0 48.4 jit_solution(1309211583506693494)
XLA Ops:
  0.0 0.0 copy-start.3
  0.0 0.0 copy-start.2
  0.0 0.8 %copy-done.3 = f32[16,768]{1,0:T(8,128)S(1)} copy-done((f32[16,768]{1,0:T(8,128)S(1)}, f32[16,768]{1,0:T(8,128)}, u32[]{:S(2)}) %copy-start.3) | copy-done | bytes 49176
  0.8 8.1 %collective-permute-start.1 = (f32[16,768]{1,0:T(8,128)S(1)}, f32[16,768]{1,0:T(8,128)S(1)}, u32[]{:S(2)}, u32[]{:S(2)}) collective-permute-start(f32[16,768]{1,0:T(8,128)S(1)} %copy-done.3), channel_id=1, source_target_pairs={{1,2},{2,1},{3,4},{4,3},{5,6},{6,5},{7,8},{8,7},{9,10},{10,9},{11,... | collective-permute-start | bytes 147464 | tf_op jit(solution)/shard_map/ppermute | solution.py:329
  8.9 0.1 collective-permute-start
  9.0 0.0 copy-done.2
  9.0 5.0 %shard_map.82 = f32[1152,128]{1,0:T(8,128)} custom-call(bf16[2048,2048]{1,0:T(8,128)(2,1)S(1)} %copy-done.2, s32[16,128]{1,0:T(8,128)} %bitcast.7, s32[16,128]{1,0:T(8,128)} %bitcast.8, bf16[2048,128]{1,0:T(8,128)(2,1)} %weight_hbm.1), custom_call_target="tpu_custom_call" | custom-call | flops 10000000000 | bytes 10000000 | tf_op jit(solution)/shard_map/pallas_call | solution.py:141
  14.0 6.0 %all-to-all-start = ((f32[128,1,1152]{2,1,0:T(1,128)}), f32[128,1,1152]{2,1,0:T(1,128)S(1)}, u32[]{:S(2)}, u32[]{:S(2)}) async-start(f32[128,1,1152]{2,1,0:T(1,128)} %bitcast.6), calls=%async_computation | async-start | bytes 1179648 | tf_op jit(solution)/shard_map/all_to_all | solution.py:348
  20.0 0.0 collective-permute-done.1.b_ref
  20.0 0.0 collective-permute-done.a_ref
  20.0 3.9 %shard_map.84 = (f32[40,768]{1,0:T(8,128)S(1)}, bf16[768,768]{1,0:T(8,128)(2,1)S(1)}, bf16[768,768]{1,0:T(8,128)(2,1)S(1)}, f32[768,768]{1,0:T(8,128)}) custom-call(f32[16,768]{1,0:T(8,128)S(1)} %copy-done.3, f32[16,768]{1,0:T(8,128)S(1)} %collective-permute-done.a_ref, f32[16,768]{1,0:T(8,128)S(1)} %collective-permute-done.1.b_ref, f32[768,768]{1,0:T(8,128)} %self_ref.3, ...), custom_call_target="tpu_custom_call" | custom-call | flops 20000000000 | bytes 10000000 | tf_op jit(solution)/shard_map/pallas_call | solution.py:267
  23.9 7.3 %collective-permute-start.3 = (f32[40,768]{1,0:T(8,128)S(1)}, f32[40,768]{1,0:T(8,128)S(1)}, u32[]{:S(2)}, u32[]{:S(2)}) collective-permute-start(f32[40,768]{1,0:T(8,128)S(1)} %get-tuple-element.13.ready_ref), channel_id=1, source_target_pairs={{1,2},{2,1},{3,4},{4,3},{5,6},{6,5},{7,8},{8,7},{9,10},{10,9},{11,... | collective-permute-start | bytes 368648 | tf_op jit(solution)/shard_map/ppermute | solution.py:329
  31.3 2.7 %all-to-all-done = f32[128,1,1152]{2,1,0:T(1,128)S(1)} async-done(((f32[128,1,1152]{2,1,0:T(1,128)}), f32[128,1,1152]{2,1,0:T(1,128)S(1)}, u32[]{:S(2)}, u32[]{:S(2)}) %all-to-all-start) | async-done | bytes 589856 | tf_op jit(solution)/shard_map/all_to_all | solution.py:348
  34.0 0.0 copy-start
  34.0 0.0 copy-start.1
  34.0 0.9 %shard_map.85 = (f32[16,768]{1,0:T(8,128)S(1)}, f32[16,768]{1,0:T(8,128)S(1)}) custom-call(f32[1152,128]{1,0:T(8,128)S(1)} %bitcast.4, f32[40,768]{1,0:T(8,128)S(1)} %get-tuple-element.13.ready_ref), custom_call_target="tpu_custom_call" | custom-call | flops 10000000000 | bytes 1000000 | tf_op jit(solution)/shard_map/pallas_call | solution.py:207
  34.9 0.1 collective-permute-start.2
  35.0 0.8 %shard_map.87.beyond_ref = f32[16,768]{1,0:T(8,128)S(1)} custom-call(f32[1152,128]{1,0:T(8,128)S(1)} %bitcast.5, f32[16,768]{1,0:T(8,128)S(1)} %get-tuple-element.16.own_ref.projected_ref), custom_call_target="tpu_custom_call" | custom-call | flops 100000000 | bytes 1000000 | tf_op jit(solution)/shard_map/pallas_call | solution.py:207
  35.8 0.4 collective-permute-done.2.a_ref
  36.2 0.0 copy-done
  36.2 0.2 copy-done.1
  36.4 0.8 %shard_map.86.part_ref = f32[16,768]{1,0:T(8,128)S(1)} custom-call(f32[16,768]{1,0:T(8,128)S(1)} %get-tuple-element.14.c_ref, f32[16,768]{1,0:T(8,128)S(1)} %collective-permute-done.2.a_ref, f32[768,768]{1,0:T(8,128)S(1)} %copy-done, f32[768,768]{1,0:T(8,128)S(1)} %copy-done.1), custom_call_target="tpu_custom_call" | custom-call | flops 500000000 | bytes 1000000 | tf_op jit(solution)/shard_map/pallas_call | solution.py:285
  37.2 0.0 collective-permute-done.3.other_ref
  37.2 0.5 shard_map.88.c_ref
  37.6 0.0 collective-permute-start.4
  37.7 4.5 %collective-permute-start.5 = (f32[16,768]{1,0:T(8,128)S(1)}, f32[16,768]{1,0:T(8,128)S(1)}, u32[]{:S(2)}, u32[]{:S(2)}) collective-permute-start(f32[16,768]{1,0:T(8,128)S(1)} %shard_map.88.c_ref), channel_id=1, source_target_pairs={{1,2},{2,1},{3,4},{4,3},{5,6},{6,5},{7,8},{8,7},{9,10},{10,9},{11,... | collective-permute-start | bytes 147464 | tf_op jit(solution)/shard_map/ppermute | solution.py:329
  42.2 0.0 collective-permute-done.4.a_ref
  42.2 0.8 %shard_map.89.part_ref = f32[16,768]{1,0:T(8,128)S(1)} custom-call(f32[16,768]{1,0:T(8,128)S(1)} %shard_map.88.c_ref, f32[16,768]{1,0:T(8,128)S(1)} %collective-permute-done.4.a_ref, f32[768,768]{1,0:T(8,128)S(1)} %copy-done, f32[768,768]{1,0:T(8,128)S(1)} %copy-done.1), custom_call_target="tpu_custom_call" | custom-call | flops 500000000 | bytes 1000000 | tf_op jit(solution)/shard_map/pallas_call | solution.py:285
  43.0 4.3 %collective-permute-done.5.b_ref = f32[16,768]{1,0:T(8,128)S(1)} collective-permute-done((f32[16,768]{1,0:T(8,128)S(1)}, f32[16,768]{1,0:T(8,128)S(1)}, u32[]{:S(2)}, u32[]{:S(2)}) %collective-permute-start.5) | collective-permute-done | bytes 49184 | tf_op jit(solution)/shard_map/ppermute | solution.py:329
  47.3 1.1 %shard_map.90 = f32[16,768]{1,0:T(8,128)} custom-call(f32[16,768]{1,0:T(8,128)S(1)} %shard_map.89.part_ref, f32[16,768]{1,0:T(8,128)S(1)} %collective-permute-done.5.b_ref, bf16[768,768]{1,0:T(8,128)(2,1)S(1)} %get-tuple-element.17.high_ref, bf16[768,768]{1,0:T(8,128)(2,1)S(1)} %get-tuple-element.18.low_ref, f32[16,768]{1,0:T(8,128)S(1)} %shard_map.88.c_ref, ...), custom_call_target="tpu_custom_call" | custom-call | flops 300000000 | bytes 1000000 | tf_op jit(solution)/shard_map/pallas_call | solution.py:312
  (1 shorter events, 0.0 us)
Async XLA Ops:
  0.0 0.8 %copy-start.3 = (f32[16,768]{1,0:T(8,128)S(1)}, f32[16,768]{1,0:T(8,128)}, u32[]{:S(2)}) copy-start(f32[16,768]{1,0:T(8,128)} %c_hbm) | copy-start | bytes 147460
  0.0 9.0 %copy-start.2 = (bf16[2048,2048]{1,0:T(8,128)(2,1)S(1)}, bf16[2048,2048]{1,0:T(8,128)(2,1)}, u32[]{:S(2)}) copy-start(bf16[2048,2048]{1,0:T(8,128)(2,1)} %movie_ref.1) | copy-start | bytes 25165828
  0.8 19.2 %collective-permute-start.1 = (f32[16,768]{1,0:T(8,128)S(1)}, f32[16,768]{1,0:T(8,128)S(1)}, u32[]{:S(2)}, u32[]{:S(2)}) collective-permute-start(f32[16,768]{1,0:T(8,128)S(1)} %copy-done.3), channel_id=1, source_target_pairs={{1,2},{2,1},{3,4},{4,3},{5,6},{6,5},{7,8},{8,7},{9,10},{10,9},{11,... | collective-permute-start | bytes 147464 | tf_op jit(solution)/shard_map/ppermute | solution.py:329
  8.9 11.1 %collective-permute-start = (f32[16,768]{1,0:T(8,128)S(1)}, f32[16,768]{1,0:T(8,128)S(1)}, u32[]{:S(2)}, u32[]{:S(2)}) collective-permute-start(f32[16,768]{1,0:T(8,128)S(1)} %copy-done.3), channel_id=1, source_target_pairs={{0,1},{1,0},{2,3},{3,2},{4,5},{5,4},{6,7},{7,6},{8,9},{9,8},{10,11... | collective-permute-start | bytes 147464 | tf_op jit(solution)/shard_map/ppermute | solution.py:324
  14.0 20.0 %all-to-all-start = ((f32[128,1,1152]{2,1,0:T(1,128)}), f32[128,1,1152]{2,1,0:T(1,128)S(1)}, u32[]{:S(2)}, u32[]{:S(2)}) async-start(f32[128,1,1152]{2,1,0:T(1,128)} %bitcast.6), calls=%async_computation | async-start | bytes 1179648 | tf_op jit(solution)/shard_map/all_to_all | solution.py:348
  23.9 13.2 %collective-permute-start.3 = (f32[40,768]{1,0:T(8,128)S(1)}, f32[40,768]{1,0:T(8,128)S(1)}, u32[]{:S(2)}, u32[]{:S(2)}) collective-permute-start(f32[40,768]{1,0:T(8,128)S(1)} %get-tuple-element.13.ready_ref), channel_id=1, source_target_pairs={{1,2},{2,1},{3,4},{4,3},{5,6},{6,5},{7,8},{8,7},{9,10},{10,9},{11,... | collective-permute-start | bytes 368648 | tf_op jit(solution)/shard_map/ppermute | solution.py:329
  34.0 2.2 %copy-start = (f32[768,768]{1,0:T(8,128)S(1)}, f32[768,768]{1,0:T(8,128)}, u32[]{:S(2)}) copy-start(f32[768,768]{1,0:T(8,128)} %self_ref.3) | copy-start | bytes 7077892
  34.0 2.4 %copy-start.1 = (f32[768,768]{1,0:T(8,128)S(1)}, f32[768,768]{1,0:T(8,128)}, u32[]{:S(2)}) copy-start(f32[768,768]{1,0:T(8,128)} %get-tuple-element.15.close_ref) | copy-start | bytes 7077892
  34.9 1.3 %collective-permute-start.2 = (f32[16,768]{1,0:T(8,128)S(1)}, f32[16,768]{1,0:T(8,128)S(1)}, u32[]{:S(2)}, u32[]{:S(2)}) collective-permute-start(f32[16,768]{1,0:T(8,128)S(1)} %get-tuple-element.14.c_ref), channel_id=1, source_target_pairs={{0,1},{1,0},{2,3},{3,2},{4,5},{5,4},{6,7},{7,6},{8,9},{9,8},{10,11... | collective-permute-start | bytes 147464 | tf_op jit(solution)/shard_map/ppermute | solution.py:324
  37.6 4.5 %collective-permute-start.4 = (f32[16,768]{1,0:T(8,128)S(1)}, f32[16,768]{1,0:T(8,128)S(1)}, u32[]{:S(2)}, u32[]{:S(2)}) collective-permute-start(f32[16,768]{1,0:T(8,128)S(1)} %shard_map.88.c_ref), channel_id=1, source_target_pairs={{0,1},{1,0},{2,3},{3,2},{4,5},{5,4},{6,7},{7,6},{8,9},{9,8},{10,11... | collective-permute-start | bytes 147464 | tf_op jit(solution)/shard_map/ppermute | solution.py:324
  37.7 9.6 %collective-permute-start.5 = (f32[16,768]{1,0:T(8,128)S(1)}, f32[16,768]{1,0:T(8,128)S(1)}, u32[]{:S(2)}, u32[]{:S(2)}) collective-permute-start(f32[16,768]{1,0:T(8,128)S(1)} %shard_map.88.c_ref), channel_id=1, source_target_pairs={{1,2},{2,1},{3,4},{4,3},{5,6},{6,5},{7,8},{8,7},{9,10},{10,9},{11,... | collective-permute-start | bytes 147464 | tf_op jit(solution)/shard_map/ppermute | solution.py:329
